TPU v7x, 32 devices: a whole 2x2x4 slice. The times are simulated.
32 devices in a mesh: fsdp: 4 (over y, core), ctx: 8 (over z, x).
Axes of the slice: x: 2, y: 2, z: 4, core: 2. Of those that a mesh axis runs over, the one named last changes fastest.
Arguments:
- tokens_in: bfloat16 [4, 2048, 1024], P('fsdp', 'ctx'), may hold values from -6 to 6
- block_ids: int32 [4, 2048], P('fsdp', 'ctx'), may hold values from 0 to 9, never falling along the last dimension, each value on 1 to 256 neighbouring positions
- w_query: bfloat16 [1024, 1024], P(('fsdp', 'ctx')), may hold values from -0.1875 to 0.1875
- w_key: bfloat16 [1024, 1024], P(('fsdp', 'ctx')), may hold values from -0.1875 to 0.1875
- w_value: bfloat16 [1024, 1024], P(('fsdp', 'ctx')), may hold values from -0.1875 to 0.1875
- w_out: bfloat16 [1024, 1024], P(('fsdp', 'ctx')), may hold values from -1.5 to 1.5
- w_up: bfloat16 [1024, 4096], P(('fsdp', 'ctx')), may hold values from -0.1875 to 0.1875
- w_down: bfloat16 [4096, 1024], P(('fsdp', 'ctx')), may hold values from -0.09375 to 0.09375
- norm_gain: bfloat16 [4, 1024], P(None, ('fsdp', 'ctx')), may hold values from 0.5 to 1.5
- cotangent: bfloat16 [4, 2048, 1024], P('fsdp', 'ctx'), may hold values from -6 to 6
Outputs:
- layer_out: bfloat16 [4, 2048, 1024], P('fsdp', 'ctx')
- grad_tokens: bfloat16 [4, 2048, 1024], P('fsdp', 'ctx')
- grad_query: float32 [1024, 1024], P(('fsdp', 'ctx'))
- grad_key: float32 [1024, 1024], P(('fsdp', 'ctx'))
- grad_value: float32 [1024, 1024], P(('fsdp', 'ctx'))
- grad_out: float32 [1024, 1024], P(('fsdp', 'ctx'))
- grad_up: float32 [1024, 4096], P(('fsdp', 'ctx'))
- grad_down: float32 [4096, 1024], P(('fsdp', 'ctx'))
- grad_gain: float32 [4, 1024], P(None, ('fsdp', 'ctx'))
Inputs may be any that keep to these rules, and one draw needn't show every extreme that they name: `block_ids`: along each sequence block numbers never fall; every block has 1 to 256 positions and one has exactly 256.
All inputs are finite; a program needn't handle non-finite values.
Results may differ from a plain program's by a relative error of at most 0.018.
Values may be sent and summed in bfloat16 or wider, within the bound.
A program may use at most 256 MiB of HBM per device.

v0:
```python
import math

import jax
import jax.numpy as jnp
from jax import lax
from jax.sharding import PartitionSpec as P

HEADS = 16
HD = 64


EPS = 1e-05
MASKED = -1e30


def from_behind(block, axis, distance):
    devices = range(lax.axis_size(axis))
    route = [((i - distance) % len(devices), i) for i in devices]
    return lax.ppermute(block, axis, route)


def layer_norm(values, gain):
    centre = values - jnp.mean(values, axis=-1, keepdims=True)
    spread = jnp.mean(centre * centre, axis=-1, keepdims=True)
    return centre * lax.rsqrt(spread + EPS) * gain


def gelu_exact(values):
    return jax.nn.gelu(values, approximate=False)


def project(left, right):
    return jnp.dot(left, right, preferred_element_type=jnp.float32)


def outer_sum(left, right):
    return lax.dot_general(
        left, right, (((0,), (0,)), ((), ())), preferred_element_type=jnp.float32
    )


def back_project(grad, weight):
    return lax.dot_general(
        grad, weight, (((1,), (1,)), ((), ())), preferred_element_type=jnp.float32
    )


def split_heads(values):
    return values.reshape(values.shape[0], HEADS, HD)


def attend(carry, head_queries, query_blocks, key_rows, key_blocks, scale):
    best, total, accum = carry
    width = key_rows.shape[1] // 2
    keys = split_heads(key_rows[:, :width])
    values = split_heads(key_rows[:, width:])
    scores = (
        jnp.einsum("qhd,khd->hqk", head_queries, keys, preferred_element_type=jnp.float32) * scale
    )
    allowed = key_blocks[None, None, :] <= query_blocks[None, :, None]
    scores = jnp.where(allowed, scores, MASKED)
    newest = jnp.maximum(best, jnp.max(scores, axis=2))
    weights = jnp.where(allowed, jnp.exp(scores - newest[:, :, None]), 0.0)
    factor = jnp.exp(best - newest)
    total = total * factor + jnp.sum(weights, axis=2)
    update = jnp.einsum(
        "hqk,khd->qhd", weights.astype(jnp.bfloat16), values, preferred_element_type=jnp.float32
    )
    accum = accum * jnp.transpose(factor)[:, :, None] + update
    return (newest, total, accum)


def score_grads(
    head_queries, head_grads, log_total, delta, query_blocks, key_rows, key_blocks, scale
):
    width = key_rows.shape[1] // 2
    rows = key_rows.shape[0]
    query_rows = head_queries.shape[0]
    keys = split_heads(key_rows[:, :width])
    values = split_heads(key_rows[:, width:])
    scores = (
        jnp.einsum("qhd,khd->hqk", head_queries, keys, preferred_element_type=jnp.float32) * scale
    )
    allowed = key_blocks[None, None, :] <= query_blocks[None, :, None]
    probs = jnp.where(
        allowed, jnp.exp(jnp.where(allowed, scores, MASKED) - log_total[:, :, None]), 0.0
    )
    grad_values = jnp.einsum(
        "hqk,qhd->khd", probs.astype(jnp.bfloat16), head_grads, preferred_element_type=jnp.float32
    )
    grad_probs = jnp.einsum("qhd,khd->hqk", head_grads, values, preferred_element_type=jnp.float32)
    grad_scores = (probs * (grad_probs - delta[:, :, None])).astype(jnp.bfloat16)
    grad_queries = (
        jnp.einsum("hqk,khd->qhd", grad_scores, keys, preferred_element_type=jnp.float32) * scale
    )
    grad_keys = (
        jnp.einsum("hqk,qhd->khd", grad_scores, head_queries, preferred_element_type=jnp.float32)
        * scale
    )
    joined = jnp.concatenate(
        [grad_keys.reshape(rows, width), grad_values.reshape(rows, width)], axis=1
    )
    return (grad_queries.reshape(query_rows, width), joined)


def guarded(head_queries, head_grads, log_total, delta, query_blocks, key_rows, key_blocks, scale):
    live = jnp.min(key_blocks) <= jnp.max(query_blocks)
    rows, columns = key_rows.shape

    def run(unused):
        return score_grads(
            head_queries, head_grads, log_total, delta, query_blocks, key_rows, key_blocks, scale
        )

    def skip(unused):
        return (
            jnp.zeros((head_queries.shape[0], columns // 2), jnp.float32),
            jnp.zeros((rows, columns), jnp.float32),
        )

    return lax.cond(live, run, skip, 0)


def body(tokens_in, block_ids, w_query, w_key, w_value, w_out, w_up, w_down, norm_gain, cotangent):
    scale = 1.0 / math.sqrt(HD)
    stride = tokens_in.shape[1]
    width = tokens_in.shape[2]
    cycle_size = lax.axis_size("ctx")
    place = lax.axis_index("ctx")
    shards = (w_query, w_key, w_value, w_out, w_up, w_down, norm_gain)
    gathered = (
        lax.all_gather(w_query, ("fsdp", "ctx"), axis=0, tiled=True),
        lax.all_gather(w_key, ("fsdp", "ctx"), axis=0, tiled=True),
        lax.all_gather(w_value, ("fsdp", "ctx"), axis=0, tiled=True),
        lax.all_gather(w_out, ("fsdp", "ctx"), axis=0, tiled=True),
        lax.all_gather(w_up, ("fsdp", "ctx"), axis=0, tiled=True),
        lax.all_gather(w_down, ("fsdp", "ctx"), axis=0, tiled=True),
        lax.all_gather(norm_gain, ("fsdp", "ctx"), axis=1, tiled=True),
    )
    full_query, full_key, full_value, full_out, full_up, full_down, full_gain = gathered
    gains = full_gain.astype(jnp.float32)
    sequence_blocks = lax.all_gather(block_ids, "ctx", axis=1, tiled=True)[0]
    own_blocks = block_ids[0]
    top_block = jnp.max(own_blocks)
    tokens = tokens_in[0].astype(jnp.float32)
    normed = layer_norm(tokens, gains[0]).astype(jnp.bfloat16)
    queries = project(normed, full_query).astype(jnp.bfloat16)
    key_value = jnp.concatenate(
        [project(normed, full_key), project(normed, full_value)], axis=1
    ).astype(jnp.bfloat16)
    head_queries = split_heads(queries)
    start_state = (
        jnp.full((HEADS, stride), MASKED, jnp.float32),
        jnp.zeros((HEADS, stride), jnp.float32),
        jnp.zeros((stride, HEADS, HD), jnp.float32),
    )
    piece = lax.all_gather(key_value, "ctx", axis=0, tiled=True)
    rows = piece.shape[0]
    size = math.gcd(rows, stride)

    def visit(index, state):
        key_rows = lax.dynamic_slice_in_dim(piece, index * size, size, 0)
        key_blocks = lax.dynamic_slice_in_dim(sequence_blocks, index * size, size, 0)
        return lax.cond(
            jnp.min(key_blocks) <= top_block,
            lambda inner: attend(inner, head_queries, own_blocks, key_rows, key_blocks, scale),
            lambda inner: inner,
            state,
        )

    best, total, accum = lax.fori_loop(0, rows // size, visit, start_state)
    mixed = accum / jnp.transpose(total)[:, :, None]
    log_total = best + jnp.log(total)
    mixed_low = mixed.reshape(stride, width).astype(jnp.bfloat16)
    branch = project(mixed_low, full_out)
    hidden = tokens + layer_norm(branch, gains[1])
    inner = layer_norm(hidden, gains[2]).astype(jnp.bfloat16)
    lifted = project(inner, full_up)
    active = gelu_exact(lifted).astype(jnp.bfloat16)
    lowered = project(active, full_down)
    layer_out = (hidden + layer_norm(lowered, gains[3])).astype(jnp.bfloat16)[None]
    regathered = (
        lax.all_gather(shards[0], ("fsdp", "ctx"), axis=0, tiled=True),
        lax.all_gather(shards[1], ("fsdp", "ctx"), axis=0, tiled=True),
        lax.all_gather(shards[2], ("fsdp", "ctx"), axis=0, tiled=True),
        lax.all_gather(shards[3], ("fsdp", "ctx"), axis=0, tiled=True),
        lax.all_gather(shards[4], ("fsdp", "ctx"), axis=0, tiled=True),
        lax.all_gather(shards[5], ("fsdp", "ctx"), axis=0, tiled=True),
        lax.all_gather(shards[6], ("fsdp", "ctx"), axis=1, tiled=True),
    )
    back_query, back_key, back_value, back_out, back_up, back_down, back_gain = regathered
    back_gains = back_gain.astype(jnp.float32)
    upstream = cotangent[0].astype(jnp.float32)
    unused_four, pull_four = jax.vjp(layer_norm, lowered, back_gains[3])
    grad_lowered, gain_four = pull_four(upstream)
    grad_lowered = grad_lowered.astype(jnp.bfloat16)
    grad_down = outer_sum(active, grad_lowered)
    grad_active = back_project(grad_lowered, back_down)
    unused_gelu, pull_gelu = jax.vjp(gelu_exact, lifted)
    grad_lifted = pull_gelu(grad_active)[0].astype(jnp.bfloat16)
    grad_up = outer_sum(inner, grad_lifted)
    grad_inner = back_project(grad_lifted, back_up)
    unused_three, pull_three = jax.vjp(layer_norm, hidden, back_gains[2])
    grad_hidden_branch, gain_three = pull_three(grad_inner)
    grad_hidden = upstream + grad_hidden_branch
    unused_two, pull_two = jax.vjp(layer_norm, branch, back_gains[1])
    grad_branch, gain_two = pull_two(grad_hidden)
    grad_branch = grad_branch.astype(jnp.bfloat16)
    grad_out = outer_sum(mixed_low, grad_branch)
    grad_mixed = back_project(grad_branch, back_out).astype(jnp.bfloat16)
    head_grads = split_heads(grad_mixed)
    delta = jnp.transpose(jnp.sum(head_grads.astype(jnp.float32) * mixed, axis=2))
    query_grad, kv_grad = guarded(
        head_queries, head_grads, log_total, delta, own_blocks, key_value, own_blocks, scale
    )

    def pass_grads(values):
        return from_behind(values.astype(jnp.bfloat16), "ctx", 1).astype(values.dtype)

    def cycle_keys(step, state):
        travel, kv_accum, query_accum = state
        travel = from_behind(travel, "ctx", 1)
        kv_accum = pass_grads(kv_accum)
        source = (place - step) % cycle_size
        key_blocks = lax.dynamic_slice_in_dim(sequence_blocks, source * stride, stride, 0)
        part_query, part_kv = guarded(
            head_queries, head_grads, log_total, delta, own_blocks, travel, key_blocks, scale
        )
        return (travel, kv_accum + part_kv, query_accum + part_query)

    unused_travel, kv_accum, query_grad = lax.fori_loop(
        1, cycle_size, cycle_keys, (key_value, kv_grad, query_grad)
    )
    kv_grad = pass_grads(kv_accum)
    query_low = query_grad.astype(jnp.bfloat16)
    kv_low = kv_grad.astype(jnp.bfloat16)
    key_low = kv_low[:, :width]
    value_low = kv_low[:, width:]
    grad_query = outer_sum(normed, query_low)
    grad_key = outer_sum(normed, key_low)
    grad_value = outer_sum(normed, value_low)
    grad_normed = (
        back_project(query_low, back_query)
        + back_project(key_low, back_key)
        + back_project(value_low, back_value)
    )
    unused_one, pull_one = jax.vjp(layer_norm, tokens, back_gains[0])
    grad_norm_in, gain_one = pull_one(grad_normed)
    grad_tokens = (grad_hidden + grad_norm_in).astype(jnp.bfloat16)[None]
    gain_grads = jnp.stack([gain_one, gain_two, gain_three, gain_four])
    summed = (
        lax.psum_scatter(grad_query, ("fsdp", "ctx"), scatter_dimension=0, tiled=True),
        lax.psum_scatter(grad_key, ("fsdp", "ctx"), scatter_dimension=0, tiled=True),
        lax.psum_scatter(grad_value, ("fsdp", "ctx"), scatter_dimension=0, tiled=True),
        lax.psum_scatter(grad_out, ("fsdp", "ctx"), scatter_dimension=0, tiled=True),
        lax.psum_scatter(grad_up, ("fsdp", "ctx"), scatter_dimension=0, tiled=True),
        lax.psum_scatter(grad_down, ("fsdp", "ctx"), scatter_dimension=0, tiled=True),
        lax.psum_scatter(gain_grads, ("fsdp", "ctx"), scatter_dimension=1, tiled=True),
    )
    return (
        layer_out,
        grad_tokens,
        summed[0],
        summed[1],
        summed[2],
        summed[3],
        summed[4],
        summed[5],
        summed[6],
    )


def solution(mesh):
    placed = (
        P("fsdp", "ctx", None),
        P("fsdp", "ctx"),
        P(("fsdp", "ctx"), None),
        P(("fsdp", "ctx"), None),
        P(("fsdp", "ctx"), None),
        P(("fsdp", "ctx"), None),
        P(("fsdp", "ctx"), None),
        P(("fsdp", "ctx"), None),
        P(None, ("fsdp", "ctx")),
        P("fsdp", "ctx", None),
    )
    return jax.shard_map(
        body,
        mesh=mesh,
        in_specs=placed,
        out_specs=(
            P("fsdp", "ctx", None),
            P("fsdp", "ctx", None),
            P(("fsdp", "ctx"), None),
            P(("fsdp", "ctx"), None),
            P(("fsdp", "ctx"), None),
            P(("fsdp", "ctx"), None),
            P(("fsdp", "ctx"), None),
            P(("fsdp", "ctx"), None),
            P(None, ("fsdp", "ctx")),
        ),
        check_vma=False,
    )
```

profile of v0, /device:TPU:0, one launch (start us, length us, event | category | flops | bytes accessed | tf_op | source)
XLA Modules:
  0.0 2387.5 jit_solution(1215820751819294761)
XLA Ops:
  9.5 70.1 %all-gather = bf16[32,32,4]{1,2,0:T(4,128)(2,1)S(1)} all-gather(bf16[1,32,4]{1,2,0:T(4,128)(2,1)} %bitcast.220), channel_id=1, replica_groups=mesh['fsdp'=4,'ctx'=8] {'fsdp','ctx'}, dimensions={0}, use_global_device_ids=true | all-gather | bytes 8448 | tf_op jit(solution)/shard_map/all_gather | solution.py:138
  85.4 43.1 %all-gather.9.cloned.1.call-done = bf16[1024,1024]{1,0:T(8,128)(2,1)} async-done(((bf16[32,1024]{1,0:T(8,128)(2,1)}), bf16[1024,1024]{1,0:T(8,128)(2,1)}) %all-gather.9.cloned.1.call-update) | async-done | bytes 2097168 | tf_op jit(solution)/shard_map/all_gather | solution.py:133
  135.9 19.5 all_gather.34
  157.7 29.1 %all-gather.15.cloned.1.call-done = bf16[1024,1024]{1,0:T(8,128)(2,1)} async-done(((bf16[32,1024]{1,0:T(8,128)(2,1)}), bf16[1024,1024]{1,0:T(8,128)(2,1)}) %all-gather.15.cloned.1.call-update) | async-done | bytes 2097168 | tf_op jit(solution)/shard_map/all_gather | solution.py:132
  189.3 122.8 %all-gather.13.cloned.1.call-done = bf16[2048,2048]{1,0:T(8,128)(2,1)} async-done(((bf16[256,2048]{1,0:T(8,128)(2,1)}), bf16[2048,2048]{1,0:T(8,128)(2,1)}) %all-gather.13.cloned.1.call-update) | async-done | bytes 8388624 | tf_op jit(solution)/shard_map/all_gather | solution.py:157
  324.6 20.8 while.36
  345.5 24.0 %all-gather.17.cloned.1.call-done = bf16[1024,1024]{1,0:T(8,128)(2,1)} async-done(((bf16[32,1024]{1,0:T(8,128)(2,1)}), bf16[1024,1024]{1,0:T(8,128)(2,1)}) %all-gather.17.cloned.1.call-update) | async-done | bytes 2097168 | tf_op jit(solution)/shard_map/all_gather | solution.py:135
  372.9 75.5 %all-gather.19.cloned.1.call-done = bf16[1024,4096]{1,0:T(8,128)(2,1)} async-done(((bf16[32,4096]{1,0:T(8,128)(2,1)}), bf16[1024,4096]{1,0:T(8,128)(2,1)}) %all-gather.19.cloned.1.call-update) | async-done | bytes 8388624 | tf_op jit(solution)/shard_map/all_gather | solution.py:136
  448.3 15.9 multiply_convert_fusion.2
  464.3 62.8 %all-gather.21.cloned.1.call-done = bf16[4096,1024]{1,0:T(8,128)(2,1)} async-done(((bf16[128,1024]{1,0:T(8,128)(2,1)}), bf16[4096,1024]{1,0:T(8,128)(2,1)}) %all-gather.21.cloned.1.call-update) | async-done | bytes 8388624 | tf_op jit(solution)/shard_map/all_gather | solution.py:137
  569.6 354.8 %while.37 = (s32[]{:T(128)}, bf16[256,2048]{0,1:T(8,128)(2,1)}, bf16[256,2048]{0,1:T(8,128)(2,1)}, f32[256,1024]{0,1:T(8,128)}, s32[]{:T(128)}, /*index=5*/s32[2...) while((s32[]{:T(128)}, bf16[256,2048]{0,1:T(8,128)(2,1)}, ...), condition=%wide.region_30.31_spmd, body=%wide.region_26.30_spmd.sunk | while | flops 686620928 | bytes 52154900 | solution.py:231
  574.6 24.1 %collective-permute-done = bf16[256,2048]{0,1:T(8,128)(2,1)} collective-permute-done((bf16[256,2048]{0,1:T(8,128)(2,1)}, bf16[256,2048]{0,1:T(8,128)(2,1)}, u32[]{:S(2)}, u32[]{:S(2)}) %collective-permute-start) | collective-permute-done | bytes 1048608 | tf_op jit(solution)/shard_map/while/body/eval_jaxpr/ppermute | solution.py:19
  603.6 16.9 collective-permute-done.1
  626.1 25.9 %collective-permute-done = bf16[256,2048]{0,1:T(8,128)(2,1)} collective-permute-done((bf16[256,2048]{0,1:T(8,128)(2,1)}, bf16[256,2048]{0,1:T(8,128)(2,1)}, u32[]{:S(2)}, u32[]{:S(2)}) %collective-permute-start) | collective-permute-done | bytes 1048608 | tf_op jit(solution)/shard_map/while/body/eval_jaxpr/ppermute | solution.py:19
  656.8 16.1 collective-permute-done.1
  677.3 27.1 %collective-permute-done = bf16[256,2048]{0,1:T(8,128)(2,1)} collective-permute-done((bf16[256,2048]{0,1:T(8,128)(2,1)}, bf16[256,2048]{0,1:T(8,128)(2,1)}, u32[]{:S(2)}, u32[]{:S(2)}) %collective-permute-start) | collective-permute-done | bytes 1048608 | tf_op jit(solution)/shard_map/while/body/eval_jaxpr/ppermute | solution.py:19
  709.2 15.2 collective-permute-done.1
  728.8 27.1 %collective-permute-done = bf16[256,2048]{0,1:T(8,128)(2,1)} collective-permute-done((bf16[256,2048]{0,1:T(8,128)(2,1)}, bf16[256,2048]{0,1:T(8,128)(2,1)}, u32[]{:S(2)}, u32[]{:S(2)}) %collective-permute-start) | collective-permute-done | bytes 1048608 | tf_op jit(solution)/shard_map/while/body/eval_jaxpr/ppermute | solution.py:19
  760.7 14.4 collective-permute-done.1
  779.5 27.1 %collective-permute-done = bf16[256,2048]{0,1:T(8,128)(2,1)} collective-permute-done((bf16[256,2048]{0,1:T(8,128)(2,1)}, bf16[256,2048]{0,1:T(8,128)(2,1)}, u32[]{:S(2)}, u32[]{:S(2)}) %collective-permute-start) | collective-permute-done | bytes 1048608 | tf_op jit(solution)/shard_map/while/body/eval_jaxpr/ppermute | solution.py:19
  811.4 13.5 collective-permute-done.1
  829.3 27.1 %collective-permute-done = bf16[256,2048]{0,1:T(8,128)(2,1)} collective-permute-done((bf16[256,2048]{0,1:T(8,128)(2,1)}, bf16[256,2048]{0,1:T(8,128)(2,1)}, u32[]{:S(2)}, u32[]{:S(2)}) %collective-permute-start) | collective-permute-done | bytes 1048608 | tf_op jit(solution)/shard_map/while/body/eval_jaxpr/ppermute | solution.py:19
  861.2 12.6 collective-permute-done.1
  878.3 27.1 %collective-permute-done = bf16[256,2048]{0,1:T(8,128)(2,1)} collective-permute-done((bf16[256,2048]{0,1:T(8,128)(2,1)}, bf16[256,2048]{0,1:T(8,128)(2,1)}, u32[]{:S(2)}, u32[]{:S(2)}) %collective-permute-start) | collective-permute-done | bytes 1048608 | tf_op jit(solution)/shard_map/while/body/eval_jaxpr/ppermute | solution.py:19
  927.3 19.4 collective-permute-done.2
  987.7 95.6 %reduce-scatter.22.cloned.1.call-done = f32[32,4]{1,0:T(8,128)} async-done(((f32[1024,4]{1,0:T(8,128)}), f32[32,4]{1,0:T(8,128)}) %reduce-scatter.22.cloned.1.call-update) | async-done | bytes 528
  1084.7 142.6 %reduce-scatter.16.cloned.1.call-done = f32[32,1024]{1,0:T(8,128)} async-done(((f32[1024,1024]{1,0:T(8,128)}), f32[32,1024]{1,0:T(8,128)}) %reduce-scatter.16.cloned.1.call-update) | async-done | bytes 131088 | tf_op jit(solution)/shard_map/reduce_scatter | solution.py:255
  1227.3 144.8 %reduce-scatter.10.cloned.1.call-done = f32[32,1024]{1,0:T(8,128)} async-done(((f32[1024,1024]{1,0:T(8,128)}), f32[32,1024]{1,0:T(8,128)}) %reduce-scatter.10.cloned.1.call-update) | async-done | bytes 131088 | tf_op jit(solution)/shard_map/reduce_scatter | solution.py:252
  1372.1 145.6 %reduce-scatter.12.cloned.1.call-done = f32[32,1024]{1,0:T(8,128)} async-done(((f32[1024,1024]{1,0:T(8,128)}), f32[32,1024]{1,0:T(8,128)}) %reduce-scatter.12.cloned.1.call-update) | async-done | bytes 131088 | tf_op jit(solution)/shard_map/reduce_scatter | solution.py:253
  1517.7 144.5 %reduce-scatter.14.cloned.1.call-done = f32[32,1024]{1,0:T(8,128)} async-done(((f32[1024,1024]{1,0:T(8,128)}), f32[32,1024]{1,0:T(8,128)}) %reduce-scatter.14.cloned.1.call-update) | async-done | bytes 131088 | tf_op jit(solution)/shard_map/reduce_scatter | solution.py:254
  1662.3 358.4 %reduce-scatter.20.cloned.1.call-done = f32[128,1024]{1,0:T(8,128)} async-done(((f32[4096,1024]{1,0:T(8,128)}), f32[128,1024]{1,0:T(8,128)}) %reduce-scatter.20.cloned.1.call-update) | async-done | bytes 524304 | tf_op jit(solution)/shard_map/reduce_scatter | solution.py:257
  2020.7 360.1 %reduce-scatter.18.cloned.1.call-done = f32[32,4096]{1,0:T(8,128)} async-done(((f32[1024,4096]{1,0:T(8,128)}), f32[32,4096]{1,0:T(8,128)}) %reduce-scatter.18.cloned.1.call-update) | async-done | bytes 524304 | tf_op jit(solution)/shard_map/reduce_scatter | solution.py:256
  (258 shorter events, 218.7 us)
Async XLA Ops:
  7.2 121.3 %copy-start = (bf16[1,256,1024]{2,1,0:T(8,128)(2,1)S(1)}, bf16[1,256,1024]{2,1,0:T(8,128)(2,1)}, u32[]{:S(2)}) copy-start(bf16[1,256,1024]{2,1,0:T(8,128)(2,1)} %param.20) | copy-start | bytes 1572868
  7.2 75.6 %all-gather.11.cloned.1.call-start = ((), (), s32[]{:S(2)}) async-start(), calls=%async_computation.8 | async-start | bytes 2162688 | tf_op jit(solution)/shard_map/all_gather | solution.py:134
  7.9 120.5 %all-gather.9.cloned.1.call-start = ((), (), s32[]{:S(2)}) async-start(), calls=%async_computation.7 | async-start | bytes 2162688 | tf_op jit(solution)/shard_map/all_gather | solution.py:133
  8.7 178.1 %all-gather.15.cloned.1.call-start = ((), (), s32[]{:S(2)}) async-start(), calls=%async_computation.10 | async-start | bytes 2162688 | tf_op jit(solution)/shard_map/all_gather | solution.py:132
  9.4 302.7 %all-gather.13.cloned.1.call-start = ((), (), s32[]{:S(2)}) async-start(), calls=%async_computation.9 | async-start | bytes 9437184 | tf_op jit(solution)/shard_map/all_gather | solution.py:157
  80.9 105.9 %copy-start.27 = (f32[256]{0:T(256)}, f32[256]{0:T(256)S(1)}, u32[]{:S(2)}) copy-start(f32[256]{0:T(256)S(1)} %broadcast_multiply_fusion.3) | copy-start | bytes 3076
  131.9 237.6 %all-gather.17.cloned.1.call-start = ((), (), s32[]{:S(2)}) async-start(), calls=%async_computation.11 | async-start | bytes 2162688 | tf_op jit(solution)/shard_map/all_gather | solution.py:135
  132.5 315.8 %all-gather.19.cloned.1.call-start = ((), (), s32[]{:S(2)}) async-start(), calls=%async_computation.12 | async-start | bytes 8650752 | tf_op jit(solution)/shard_map/all_gather | solution.py:136
  133.1 394.0 %all-gather.21.cloned.1.call-start = ((), (), s32[]{:S(2)}) async-start(), calls=%async_computation.13 | async-start | bytes 8650752 | tf_op jit(solution)/shard_map/all_gather | solution.py:137
  133.9 949.4 %reduce-scatter.22.cloned.1.call-start = ((), (), s32[]{:S(2)}) async-start(), calls=%async_computation.20 | async-start | bytes 540672
  372.6 180.7 %copy-start.1 = (f32[256,1024]{1,0:T(8,128)}, f32[256,1024]{1,0:T(8,128)S(1)}, u32[]{:S(2)}) copy-start(f32[256,1024]{1,0:T(8,128)S(1)} %get-tuple-element.737) | copy-start | bytes 3145732
  569.6 29.1 %collective-permute-start = (bf16[256,2048]{0,1:T(8,128)(2,1)}, bf16[256,2048]{0,1:T(8,128)(2,1)}, u32[]{:S(2)}, u32[]{:S(2)}) collective-permute-start(bf16[256,2048]{0,1:T(8,128)(2,1)} %get-tuple-element.977), channel_id=1, source_target_pairs={{7,0},{0,1},{1,2},{2,3},{3,4},{4,5},{5,6},{6,7},{15,8},{8,9},{9,10... | collective-permute-start | bytes 3145736 | tf_op jit(solution)/shard_map/while/body/eval_jaxpr/ppermute | solution.py:19
  571.1 49.4 %collective-permute-start.1 = (bf16[256,2048]{0,1:T(8,128)(2,1)}, bf16[256,2048]{0,1:T(8,128)(2,1)}, u32[]{:S(2)}, u32[]{:S(2)}) collective-permute-start(bf16[256,2048]{0,1:T(8,128)(2,1)} %get-tuple-element.978), channel_id=1, source_target_pairs={{7,0},{0,1},{1,2},{2,3},{3,4},{4,5},{5,6},{6,7},{15,8},{8,9},{9,10... | collective-permute-start | bytes 3145736 | tf_op jit(solution)/shard_map/while/body/eval_jaxpr/ppermute | solution.py:19
  622.9 29.0 %collective-permute-start = (bf16[256,2048]{0,1:T(8,128)(2,1)}, bf16[256,2048]{0,1:T(8,128)(2,1)}, u32[]{:S(2)}, u32[]{:S(2)}) collective-permute-start(bf16[256,2048]{0,1:T(8,128)(2,1)} %get-tuple-element.977), channel_id=1, source_target_pairs={{7,0},{0,1},{1,2},{2,3},{3,4},{4,5},{5,6},{6,7},{15,8},{8,9},{9,10... | collective-permute-start | bytes 3145736 | tf_op jit(solution)/shard_map/while/body/eval_jaxpr/ppermute | solution.py:19
  622.9 49.9 %collective-permute-start.1 = (bf16[256,2048]{0,1:T(8,128)(2,1)}, bf16[256,2048]{0,1:T(8,128)(2,1)}, u32[]{:S(2)}, u32[]{:S(2)}) collective-permute-start(bf16[256,2048]{0,1:T(8,128)(2,1)} %get-tuple-element.978), channel_id=1, source_target_pairs={{7,0},{0,1},{1,2},{2,3},{3,4},{4,5},{5,6},{6,7},{15,8},{8,9},{9,10... | collective-permute-start | bytes 3145736 | tf_op jit(solution)/shard_map/while/body/eval_jaxpr/ppermute | solution.py:19
  675.3 29.0 %collective-permute-start = (bf16[256,2048]{0,1:T(8,128)(2,1)}, bf16[256,2048]{0,1:T(8,128)(2,1)}, u32[]{:S(2)}, u32[]{:S(2)}) collective-permute-start(bf16[256,2048]{0,1:T(8,128)(2,1)} %get-tuple-element.977), channel_id=1, source_target_pairs={{7,0},{0,1},{1,2},{2,3},{3,4},{4,5},{5,6},{6,7},{15,8},{8,9},{9,10... | collective-permute-start | bytes 3145736 | tf_op jit(solution)/shard_map/while/body/eval_jaxpr/ppermute | solution.py:19
  675.3 49.1 %collective-permute-start.1 = (bf16[256,2048]{0,1:T(8,128)(2,1)}, bf16[256,2048]{0,1:T(8,128)(2,1)}, u32[]{:S(2)}, u32[]{:S(2)}) collective-permute-start(bf16[256,2048]{0,1:T(8,128)(2,1)} %get-tuple-element.978), channel_id=1, source_target_pairs={{7,0},{0,1},{1,2},{2,3},{3,4},{4,5},{5,6},{6,7},{15,8},{8,9},{9,10... | collective-permute-start | bytes 3145736 | tf_op jit(solution)/shard_map/while/body/eval_jaxpr/ppermute | solution.py:19
  726.9 29.0 %collective-permute-start = (bf16[256,2048]{0,1:T(8,128)(2,1)}, bf16[256,2048]{0,1:T(8,128)(2,1)}, u32[]{:S(2)}, u32[]{:S(2)}) collective-permute-start(bf16[256,2048]{0,1:T(8,128)(2,1)} %get-tuple-element.977), channel_id=1, source_target_pairs={{7,0},{0,1},{1,2},{2,3},{3,4},{4,5},{5,6},{6,7},{15,8},{8,9},{9,10... | collective-permute-start | bytes 3145736 | tf_op jit(solution)/shard_map/while/body/eval_jaxpr/ppermute | solution.py:19
  726.9 48.2 %collective-permute-start.1 = (bf16[256,2048]{0,1:T(8,128)(2,1)}, bf16[256,2048]{0,1:T(8,128)(2,1)}, u32[]{:S(2)}, u32[]{:S(2)}) collective-permute-start(bf16[256,2048]{0,1:T(8,128)(2,1)} %get-tuple-element.978), channel_id=1, source_target_pairs={{7,0},{0,1},{1,2},{2,3},{3,4},{4,5},{5,6},{6,7},{15,8},{8,9},{9,10... | collective-permute-start | bytes 3145736 | tf_op jit(solution)/shard_map/while/body/eval_jaxpr/ppermute | solution.py:19
  777.5 29.0 %collective-permute-start = (bf16[256,2048]{0,1:T(8,128)(2,1)}, bf16[256,2048]{0,1:T(8,128)(2,1)}, u32[]{:S(2)}, u32[]{:S(2)}) collective-permute-start(bf16[256,2048]{0,1:T(8,128)(2,1)} %get-tuple-element.977), channel_id=1, source_target_pairs={{7,0},{0,1},{1,2},{2,3},{3,4},{4,5},{5,6},{6,7},{15,8},{8,9},{9,10... | collective-permute-start | bytes 3145736 | tf_op jit(solution)/shard_map/while/body/eval_jaxpr/ppermute | solution.py:19
  777.5 47.4 %collective-permute-start.1 = (bf16[256,2048]{0,1:T(8,128)(2,1)}, bf16[256,2048]{0,1:T(8,128)(2,1)}, u32[]{:S(2)}, u32[]{:S(2)}) collective-permute-start(bf16[256,2048]{0,1:T(8,128)(2,1)} %get-tuple-element.978), channel_id=1, source_target_pairs={{7,0},{0,1},{1,2},{2,3},{3,4},{4,5},{5,6},{6,7},{15,8},{8,9},{9,10... | collective-permute-start | bytes 3145736 | tf_op jit(solution)/shard_map/while/body/eval_jaxpr/ppermute | solution.py:19
  827.3 29.0 %collective-permute-start = (bf16[256,2048]{0,1:T(8,128)(2,1)}, bf16[256,2048]{0,1:T(8,128)(2,1)}, u32[]{:S(2)}, u32[]{:S(2)}) collective-permute-start(bf16[256,2048]{0,1:T(8,128)(2,1)} %get-tuple-element.977), channel_id=1, source_target_pairs={{7,0},{0,1},{1,2},{2,3},{3,4},{4,5},{5,6},{6,7},{15,8},{8,9},{9,10... | collective-permute-start | bytes 3145736 | tf_op jit(solution)/shard_map/while/body/eval_jaxpr/ppermute | solution.py:19
  827.3 46.5 %collective-permute-start.1 = (bf16[256,2048]{0,1:T(8,128)(2,1)}, bf16[256,2048]{0,1:T(8,128)(2,1)}, u32[]{:S(2)}, u32[]{:S(2)}) collective-permute-start(bf16[256,2048]{0,1:T(8,128)(2,1)} %get-tuple-element.978), channel_id=1, source_target_pairs={{7,0},{0,1},{1,2},{2,3},{3,4},{4,5},{5,6},{6,7},{15,8},{8,9},{9,10... | collective-permute-start | bytes 3145736 | tf_op jit(solution)/shard_map/while/body/eval_jaxpr/ppermute | solution.py:19
  876.3 29.0 %collective-permute-start = (bf16[256,2048]{0,1:T(8,128)(2,1)}, bf16[256,2048]{0,1:T(8,128)(2,1)}, u32[]{:S(2)}, u32[]{:S(2)}) collective-permute-start(bf16[256,2048]{0,1:T(8,128)(2,1)} %get-tuple-element.977), channel_id=1, source_target_pairs={{7,0},{0,1},{1,2},{2,3},{3,4},{4,5},{5,6},{6,7},{15,8},{8,9},{9,10... | collective-permute-start | bytes 3145736 | tf_op jit(solution)/shard_map/while/body/eval_jaxpr/ppermute | solution.py:19
  876.3 45.7 %collective-permute-start.1 = (bf16[256,2048]{0,1:T(8,128)(2,1)}, bf16[256,2048]{0,1:T(8,128)(2,1)}, u32[]{:S(2)}, u32[]{:S(2)}) collective-permute-start(bf16[256,2048]{0,1:T(8,128)(2,1)} %get-tuple-element.978), channel_id=1, source_target_pairs={{7,0},{0,1},{1,2},{2,3},{3,4},{4,5},{5,6},{6,7},{15,8},{8,9},{9,10... | collective-permute-start | bytes 3145736 | tf_op jit(solution)/shard_map/while/body/eval_jaxpr/ppermute | solution.py:19
  924.4 22.2 collective-permute-start.2
  950.0 277.3 %reduce-scatter.16.cloned.1.call-start = ((), (), s32[]{:S(2)}) async-start(), calls=%async_computation.17 | async-start | bytes 4325376 | tf_op jit(solution)/shard_map/reduce_scatter | solution.py:255
  952.9 419.2 %reduce-scatter.10.cloned.1.call-start = ((), (), s32[]{:S(2)}) async-start(), calls=%async_computation.14 | async-start | bytes 4325376 | tf_op jit(solution)/shard_map/reduce_scatter | solution.py:252
  957.2 560.5 %reduce-scatter.12.cloned.1.call-start = ((), (), s32[]{:S(2)}) async-start(), calls=%async_computation.15 | async-start | bytes 4325376 | tf_op jit(solution)/shard_map/reduce_scatter | solution.py:253
  960.1 702.1 %reduce-scatter.14.cloned.1.call-start = ((), (), s32[]{:S(2)}) async-start(), calls=%async_computation.16 | async-start | bytes 4325376 | tf_op jit(solution)/shard_map/reduce_scatter | solution.py:254
  963.0 1057.6 %reduce-scatter.20.cloned.1.call-start = ((), (), s32[]{:S(2)}) async-start(), calls=%async_computation.19 | async-start | bytes 17301504 | tf_op jit(solution)/shard_map/reduce_scatter | solution.py:257
  974.0 1406.8 %reduce-scatter.18.cloned.1.call-start = ((), (), s32[]{:S(2)}) async-start(), calls=%async_computation.18 | async-start | bytes 17301504 | tf_op jit(solution)/shard_map/reduce_scatter | solution.py:256
  (30 other events, 501.1 us)
Sparse Core Ops, SparseCore 0:
  11.0 59.1 all-gather.10
  73.2 55.2 all-gather.8
  131.4 55.2 all-gather.14
  188.7 123.3 all-gather.12
  314.9 54.6 all-gather.16
  372.4 75.9 all-gather.18
  451.3 75.7 all-gather.20
  950.2 133.0 reduce-scatter.21
  1086.2 141.1 reduce-scatter.15
  1230.0 142.0 reduce-scatter.9
  1375.0 142.7 reduce-scatter.11
  1520.4 141.7 reduce-scatter.13
  1665.1 355.4 reduce-scatter.19
  2023.4 357.3 reduce-scatter.17
where the time goes:
time: 2390 us
  waiting for transfers between devices  2060 us (86%)
  matrix products  96.3 us (4%)
  blocking collectives  89.6 us (4%)
  other arithmetic  58.4 us (2%)
  local copies, waits for them, and re-layouts  44.2 us (2%)
    reduce_scatter x1, waiting for transfers between devices, body(): lax.psum_scatter(grad_up, ('fsdp', 'ctx'), scatter_dimension=0, tiled=True)  360 us
    reduce_scatter x1, waiting for transfers between devices, body(): lax.psum_scatter(grad_down, ('fsdp', 'ctx'), scatter_dimension=0, tiled=T...  358 us
    ppermute x15, waiting for transfers between devices, from_behind(): return lax.ppermute(block, axis, route)  305 us
    reduce_scatter x1, waiting for transfers between devices, body(): lax.psum_scatter(grad_key, ('fsdp', 'ctx'), scatter_dimension=0, tiled=True)  146 us
    reduce_scatter x1, waiting for transfers between devices, body(): lax.psum_scatter(grad_query, ('fsdp', 'ctx'), scatter_dimension=0, tiled=...  145 us
    reduce_scatter x1, waiting for transfers between devices, body(): lax.psum_scatter(grad_value, ('fsdp', 'ctx'), scatter_dimension=0, tiled=...  145 us
    reduce_scatter x1, waiting for transfers between devices, body(): lax.psum_scatter(grad_out, ('fsdp', 'ctx'), scatter_dimension=0, tiled=True)  143 us
    all_gather x1, waiting for transfers between devices, body(): piece = lax.all_gather(key_value, 'ctx', axis=0, tiled=True)  123 us
  transfers between devices with their start and end apart: 29, of which 28 were waited for; matrix products, arithmetic and copies ran while one was open for 6% of the time, Pallas kernels for 0%

commit v1 on v0

--- a/solution.py
+++ b/solution.py
@@ -3,6 +3,8 @@
 import jax
 import jax.numpy as jnp
 from jax import lax
+from jax.experimental import pallas as pl
+from jax.experimental.pallas import tpu as pltpu
 from jax.sharding import PartitionSpec as P
 
 HEADS = 16
@@ -270,6 +272,293 @@
     )
 
 
+TILE = 256
+
+
+def nt(left, right):
+    return lax.dot_general(
+        left, right, (((1,), (1,)), ((), ())), preferred_element_type=jnp.float32
+    )
+
+
+def nn(left, right):
+    return lax.dot_general(
+        left, right, (((1,), (0,)), ((), ())), preferred_element_type=jnp.float32
+    )
+
+
+def tn(left, right):
+    return lax.dot_general(
+        left, right, (((0,), (0,)), ((), ())), preferred_element_type=jnp.float32
+    )
+
+
+def both_heads(rows):
+    lane = lax.broadcasted_iota(jnp.int32, rows.shape, 1)
+    zero = jnp.zeros_like(rows)
+    return jnp.concatenate(
+        [jnp.where(lane < HD, rows, zero), jnp.where(lane < HD, zero, rows)], axis=0
+    )
+
+
+def own_lanes(pair):
+    half = pair.shape[0] // 2
+    lane = lax.broadcasted_iota(jnp.int32, (half, pair.shape[1]), 1)
+    return jnp.where(lane < HD, pair[:half], pair[half:])
+
+
+def attend_kernel(query_ref, key_ref, value_ref, row_ref, col_ref, mixed_ref, log_ref, score_ref):
+    tile = pl.program_id(0)
+    tiles = pl.num_programs(0)
+    wide = 2 * HD
+    scaled = both_heads((query_ref[...].astype(jnp.float32) * HD**-0.5).astype(jnp.bfloat16))
+    own = row_ref[...]
+    own = jnp.concatenate([own, own], axis=0)
+
+    def score(index, best, masked):
+        at = pl.multiple_of(index * TILE, TILE)
+        part = nt(scaled, key_ref[pl.ds(at, TILE), :])
+        if masked:
+            part = jnp.where(col_ref[:, pl.ds(at, TILE)] <= own, part, MASKED)
+        score_ref[:, pl.ds(at, TILE)] = part
+        for lane in range(0, TILE, wide):
+            best = jnp.maximum(best, part[:, lane : lane + wide])
+        return best
+
+    best = jnp.full((2 * TILE, wide), MASKED, jnp.float32)
+    best = lax.fori_loop(0, tile, lambda i, b: score(i, b, False), best)
+    stop = jnp.minimum(tile + 2, tiles)
+    best = lax.fori_loop(tile, stop, lambda i, b: score(i, b, True), best)
+    best = jnp.max(best, axis=1, keepdims=True)
+
+    def weigh(index, carry):
+        total, accum = carry
+        at = pl.multiple_of(index * TILE, TILE)
+        weights = jnp.exp(score_ref[:, pl.ds(at, TILE)] - best)
+        for lane in range(0, TILE, wide):
+            total = total + weights[:, lane : lane + wide]
+        return (total, accum + nn(weights.astype(jnp.bfloat16), value_ref[pl.ds(at, TILE), :]))
+
+    zero = jnp.zeros((2 * TILE, wide), jnp.float32)
+    total, accum = lax.fori_loop(0, stop, weigh, (zero, zero))
+    total = jnp.sum(total, axis=1, keepdims=True)
+    mixed_ref[...] = own_lanes(accum / total)
+    log_total = jnp.broadcast_to(best + jnp.log(total), (2 * TILE, wide))
+    log_ref[0] = jnp.transpose(log_total)[:8]
+
+
+def attention_forward(joined, blocks):
+    rows = joined.shape[0]
+    wide = 2 * HD
+    tiles = rows // TILE
+    return pl.pallas_call(
+        attend_kernel,
+        grid=(tiles,),
+        out_shape=(
+            jax.ShapeDtypeStruct((rows, wide), jnp.float32),
+            jax.ShapeDtypeStruct((tiles, 8, 2 * TILE), jnp.float32),
+        ),
+        in_specs=[
+            pl.BlockSpec((TILE, wide), lambda t: (t, 0)),
+            pl.BlockSpec((rows, wide), lambda t: (0, 1)),
+            pl.BlockSpec((rows, wide), lambda t: (0, 2)),
+            pl.BlockSpec((TILE, 1), lambda t: (t, 0)),
+            pl.BlockSpec((1, rows), lambda t: (0, 0)),
+        ],
+        out_specs=(
+            pl.BlockSpec((TILE, wide), lambda t: (t, 0)),
+            pl.BlockSpec((1, 8, 2 * TILE), lambda t: (t, 0, 0)),
+        ),
+        scratch_shapes=[pltpu.VMEM((2 * TILE, rows), jnp.float32)],
+        name="attention_forward",
+    )(joined, joined, joined, blocks.reshape(rows, 1), blocks.reshape(1, rows))
+
+
+def grads_kernel(
+    query_ref, key_ref, value_ref, grad_ref, mixed_ref, log_ref, row_ref, col_ref, out_ref, key_sum, value_sum
+):
+    tile = pl.program_id(0)
+    tiles = pl.num_programs(0)
+    wide = 2 * HD
+
+    @pl.when(tile == 0)
+    def _():
+        key_sum[...] = jnp.zeros_like(key_sum)
+        value_sum[...] = jnp.zeros_like(value_sum)
+
+    scaled = both_heads((query_ref[...].astype(jnp.float32) * HD**-0.5).astype(jnp.bfloat16))
+    grads = both_heads(grad_ref[...])
+    products = grad_ref[...].astype(jnp.float32) * mixed_ref[...]
+    products = jnp.transpose(products)
+    delta = jnp.concatenate(
+        [
+            jnp.sum(products[:HD], axis=0, keepdims=True),
+            jnp.sum(products[HD:], axis=0, keepdims=True),
+        ],
+        axis=1,
+    )
+    log_total = log_ref[0, :1]
+    own = col_ref[...]
+    own = jnp.concatenate([own, own], axis=1)
+
+    def step(index, accum, masked):
+        at = pl.multiple_of(index * TILE, TILE)
+        here = pl.ds(at, TILE)
+        keys = key_ref[here, :]
+        scores = nt(keys, scaled)
+        if masked:
+            scores = jnp.where(row_ref[here, :] <= own, scores, MASKED)
+        probs = jnp.exp(scores - log_total)
+        value_sum[here, :] += nn(probs.astype(jnp.bfloat16), grads)
+        grad_scores = (probs * (nt(value_ref[here, :], grads) - delta)).astype(jnp.bfloat16)
+        key_sum[here, :] += nn(grad_scores, scaled)
+        return accum + tn(grad_scores, keys)
+
+    accum = jnp.zeros((2 * TILE, wide), jnp.float32)
+    accum = lax.fori_loop(0, tile, lambda i, a: step(i, a, False), accum)
+    stop = jnp.minimum(tile + 2, tiles)
+    accum = lax.fori_loop(tile, stop, lambda i, a: step(i, a, True), accum)
+    at = pl.multiple_of(tile * TILE, TILE)
+    out_ref[pl.ds(at, TILE), :wide] = (own_lanes(accum) * HD**-0.5).astype(jnp.bfloat16)
+
+    @pl.when(tile == tiles - 1)
+    def _():
+        out_ref[:, wide : 2 * wide] = key_sum[...].astype(jnp.bfloat16)
+        out_ref[:, 2 * wide :] = value_sum[...].astype(jnp.bfloat16)
+
+
+def attention_backward(joined, grad_mixed, mixed, log_total, blocks):
+    rows = joined.shape[0]
+    wide = 2 * HD
+    tiles = rows // TILE
+    return pl.pallas_call(
+        grads_kernel,
+        grid=(tiles,),
+        out_shape=jax.ShapeDtypeStruct((rows, 3 * wide), jnp.bfloat16),
+        in_specs=[
+            pl.BlockSpec((TILE, wide), lambda t: (t, 0)),
+            pl.BlockSpec((rows, wide), lambda t: (0, 1)),
+            pl.BlockSpec((rows, wide), lambda t: (0, 2)),
+            pl.BlockSpec((TILE, wide), lambda t: (t, 0)),
+            pl.BlockSpec((TILE, wide), lambda t: (t, 0)),
+            pl.BlockSpec((1, 8, 2 * TILE), lambda t: (t, 0, 0)),
+            pl.BlockSpec((rows, 1), lambda t: (0, 0)),
+            pl.BlockSpec((1, TILE), lambda t: (0, t)),
+        ],
+        out_specs=pl.BlockSpec((rows, 3 * wide), lambda t: (0, 0)),
+        scratch_shapes=[
+            pltpu.VMEM((rows, wide), jnp.float32),
+            pltpu.VMEM((rows, wide), jnp.float32),
+        ],
+        name="attention_backward",
+    )(
+        joined,
+        joined,
+        joined,
+        grad_mixed,
+        mixed,
+        log_total,
+        blocks.reshape(rows, 1),
+        blocks.reshape(1, rows),
+    )
+
+
+def to_heads(rows, groups, count):
+    tokens = rows.shape[0]
+    wide = rows.shape[1] // (groups * count)
+    split = rows.reshape(tokens, count, groups, wide).transpose(2, 0, 1, 3)
+    split = split.reshape(groups, tokens, count * wide)
+    whole = lax.all_to_all(split, "ctx", 0, 0, tiled=True)
+    return whole.reshape(groups * tokens, count * wide)
+
+
+def to_tokens(rows, groups, count):
+    tokens = rows.shape[0] // groups
+    wide = rows.shape[1] // count
+    split = lax.all_to_all(rows.reshape(groups, tokens, count * wide), "ctx", 0, 0, tiled=True)
+    split = split.reshape(groups, tokens, count, wide).transpose(1, 2, 0, 3)
+    return split.reshape(tokens, count * groups * wide)
+
+
+def scatter_sum(grad):
+    return lax.psum_scatter(
+        grad.astype(jnp.bfloat16), ("fsdp", "ctx"), scatter_dimension=0, tiled=True
+    ).astype(jnp.float32)
+
+
+def fast_body(
+    tokens_in, block_ids, w_query, w_key, w_value, w_out, w_up, w_down, norm_gain, cotangent
+):
+    axes = ("fsdp", "ctx")
+    width = tokens_in.shape[2]
+    groups = lax.axis_size("ctx")
+    full_gain = lax.all_gather(norm_gain, axes, axis=1, tiled=True)
+    full_qkv = lax.all_gather(
+        jnp.concatenate([w_query, w_key, w_value], axis=1), axes, axis=0, tiled=True
+    )
+    blocks = lax.all_gather(block_ids, "ctx", axis=1, tiled=True)[0]
+    full_out = lax.all_gather(w_out, axes, axis=0, tiled=True)
+    full_up = lax.all_gather(w_up, axes, axis=0, tiled=True)
+    full_down = lax.all_gather(w_down, axes, axis=0, tiled=True)
+    gains = full_gain.astype(jnp.float32)
+    tokens = tokens_in[0].astype(jnp.float32)
+    normed = layer_norm(tokens, gains[0]).astype(jnp.bfloat16)
+    joined = to_heads(project(normed, full_qkv).astype(jnp.bfloat16), groups, 3)
+    mixed, log_total = attention_forward(joined, blocks)
+    mixed_low = to_tokens(mixed.astype(jnp.bfloat16), groups, 1)
+    branch = project(mixed_low, full_out)
+    hidden = tokens + layer_norm(branch, gains[1])
+    inner = layer_norm(hidden, gains[2]).astype(jnp.bfloat16)
+    lifted = project(inner, full_up)
+    active = gelu_exact(lifted).astype(jnp.bfloat16)
+    lowered = project(active, full_down)
+    layer_out = (hidden + layer_norm(lowered, gains[3])).astype(jnp.bfloat16)[None]
+    upstream = cotangent[0].astype(jnp.float32)
+    unused_four, pull_four = jax.vjp(layer_norm, lowered, gains[3])
+    grad_lowered, gain_four = pull_four(upstream)
+    grad_lowered = grad_lowered.astype(jnp.bfloat16)
+    grad_down = scatter_sum(outer_sum(active, grad_lowered))
+    grad_active = back_project(grad_lowered, full_down)
+    unused_gelu, pull_gelu = jax.vjp(gelu_exact, lifted)
+    grad_lifted = pull_gelu(grad_active)[0].astype(jnp.bfloat16)
+    grad_up = scatter_sum(outer_sum(inner, grad_lifted))
+    grad_inner = back_project(grad_lifted, full_up)
+    unused_three, pull_three = jax.vjp(layer_norm, hidden, gains[2])
+    grad_hidden_branch, gain_three = pull_three(grad_inner)
+    grad_hidden = upstream + grad_hidden_branch
+    unused_two, pull_two = jax.vjp(layer_norm, branch, gains[1])
+    grad_branch, gain_two = pull_two(grad_hidden)
+    grad_branch = grad_branch.astype(jnp.bfloat16)
+    grad_out = scatter_sum(outer_sum(mixed_low, grad_branch))
+    grad_mixed = back_project(grad_branch, full_out).astype(jnp.bfloat16)
+    grad_joined = attention_backward(
+        joined, to_heads(grad_mixed, groups, 1), mixed, log_total, blocks
+    )
+    grad_qkv = to_tokens(grad_joined, groups, 3)
+    grad_three = scatter_sum(outer_sum(normed, grad_qkv))
+    grad_normed = back_project(grad_qkv, full_qkv)
+    unused_one, pull_one = jax.vjp(layer_norm, tokens, gains[0])
+    grad_norm_in, gain_one = pull_one(grad_normed)
+    grad_tokens = (grad_hidden + grad_norm_in).astype(jnp.bfloat16)[None]
+    gain_grads = jnp.stack([gain_one, gain_two, gain_three, gain_four])
+    gain_sum = lax.psum_scatter(gain_grads, axes, scatter_dimension=1, tiled=True)
+    return (
+        layer_out,
+        grad_tokens,
+        grad_three[:, :width],
+        grad_three[:, width : 2 * width],
+        grad_three[:, 2 * width :],
+        grad_out,
+        grad_up,
+        grad_down,
+        gain_sum,
+    )
+
+
+def pick(mesh):
+    return fast_body if mesh.shape["ctx"] * 2 == HEADS else body
+
+
 def solution(mesh):
     placed = (
         P("fsdp", "ctx", None),
@@ -284,7 +573,7 @@
         P("fsdp", "ctx", None),
     )
     return jax.shard_map(
-        body,
+        pick(mesh),
         mesh=mesh,
         in_specs=placed,
         out_specs=(

time: 2390 us -> 1230 us (0.51)
  waiting for transfers between devices: 2060 us -> 845 us
  blocking collectives: 89.6 us -> 173 us
  Pallas kernels: 0 us -> 64.1 us
  other arithmetic: 58.4 us -> 16.8 us
  local copies, waits for them, and re-layouts: 44.2 us -> 18 us
    reduce_scatter x6 -> x4, waiting for transfers between devices: 1300 us -> 621 us  [scatter_sum(): lax.psum_scatter(grad.astype(jnp.bfloat16), ('fsdp', 'ctx'), scatter_dime...]
    ppermute x15 -> x0, waiting for transfers between devices: 305 us -> none  [from_behind(): return lax.ppermute(block, axis, route)]
    all_gather x7 -> x4, waiting for transfers between devices: 357 us -> 93.7 us  [the longest x1 62.8 us: fast_body(): full_down = lax.all_gather(w_down, axes, axis=0, tiled=True)]
    pallas_call x0 -> x2, Pallas kernels: none -> 64.1 us  [the longest x1 35.5 us: attention_backward(): pl.pallas_call(grads_kernel, grid=(tiles,), out_shape=jax.ShapeDtypeStruc...]
    all_to_all x0 -> x2, blocking collectives: none -> 59.5 us  [the longest x1 40.6 us: to_tokens(): lax.all_to_all(rows.reshape(groups, tokens, count * wide), 'ctx', 0, 0, t...]
    add x16 -> x0, other arithmetic: 33.6 us -> none  [the longest x14 33.6 us: cycle_keys(): return (travel, kv_accum + part_kv, query_accum + part_query)]
    while x9 -> x0, local copies, waits for them, and re-layouts: 30.4 us -> none
    unnamed x15 -> x10, waiting for transfers between devices: 99.6 us -> 108 us
  transfers between devices with their start and end apart: 29 -> 11, of which waited for: 28 -> 8; matrix products, arithmetic and copies ran while one was open for 6% -> 5% of each run, Pallas kernels for 0% -> 2%
where the time goes in v1:
time: 1230 us; the launch traced here: 1220 us
  waiting for transfers between devices  845 us (69%)
  blocking collectives  173 us (14%)
  matrix products  77.7 us (6%)
  Pallas kernels  64.1 us (5%)
  local copies, waits for them, and re-layouts  18 us (1%)
  other arithmetic  16.8 us (1%)
  starting transfers between devices  14.6 us (1%)
  between operations  14.6 us (1%)
    reduce_scatter x4, waiting for transfers between devices, scatter_sum(): lax.psum_scatter(grad.astype(jnp.bfloat16), ('fsdp', 'ctx'), scatter_dime...  621 us
    unnamed x10, waiting for transfers between devices  108 us
    all_gather x1, blocking collectives, fast_body(): full_gain = lax.all_gather(norm_gain, axes, axis=1, tiled=True)  70.7 us
    all_gather x1, waiting for transfers between devices, fast_body(): full_down = lax.all_gather(w_down, axes, axis=0, tiled=True)  62.8 us
    all_gather x1, blocking collectives, fast_body(): blocks = lax.all_gather(block_ids, 'ctx', axis=1, tiled=True)[0]  42.5 us
    all_to_all x1, blocking collectives, to_tokens(): lax.all_to_all(rows.reshape(groups, tokens, count * wide), 'ctx', 0, 0, t...  40.6 us
    pallas_call x1, Pallas kernels, attention_backward(): pl.pallas_call(grads_kernel, grid=(tiles,), out_shape=jax.ShapeDtypeStruc...  35.5 us
    all_gather x1, waiting for transfers between devices, fast_body(): full_up = lax.all_gather(w_up, axes, axis=0, tiled=True)  30.9 us
  transfers between devices with their start and end apart: 11, of which 8 were waited for; matrix products, arithmetic and copies ran while one was open for 5% of the time, Pallas kernels for 2%

profile of v1, /device:TPU:0, one launch (start us, length us, event | category | flops | bytes accessed | tf_op | source)
XLA Modules:
  0.0 1224.0 jit_solution(6525068134724620223)
XLA Ops:
  10.9 70.7 %all-gather = bf16[32,32,4]{1,2,0:T(4,128)(2,1)S(1)} all-gather(bf16[1,32,4]{1,2,0:T(4,128)(2,1)} %bitcast.159), channel_id=1, replica_groups=mesh['fsdp'=4,'ctx'=8] {'fsdp','ctx'}, dimensions={0}, use_global_device_ids=true | all-gather | bytes 8448 | tf_op jit(solution)/shard_map/all_gather | solution.py:495
  84.3 4.9 fusion.6
  89.5 1.9 copy.40
  91.4 3.6 all-to-all-start
  95.0 42.5 %all_gather.20.col_ref = s32[1,2048]{1,0:T(1,128)S(1)} all-gather(s32[1,256]{1,0:T(1,128)S(1)} %copy-done.15), channel_id=1, replica_groups=mesh['fsdp'=4,'ctx'=8] {'ctx'}, dimensions={1}, use_global_device_ids=true | all-gather | bytes 9216 | tf_op jit(solution)/shard_map/all_gather | solution.py:499
  140.5 28.6 %attention_forward.1 = (f32[2048,128]{1,0:T(8,128)}, f32[8,8,512]{2,1,0:T(8,128)}) custom-call(bf16[2048,384]{1,0:T(8,128)(2,1)} %bitcast.120, bf16[2048,384]{1,0:T(8,128)(2,1)} %bitcast.121, bf16[2048,384]{1,0:T(8,128)(2,1)} %bitcast.122, s32[2048,1]{1,0:T(8,128)} %copy.42.row_ref, s32[1,2048]{1,0:T(1,128)} %copy-done.14), custom_call_target="tpu_custom_call" | custom-call | tf_op jit(solution)/shard_map/attention_forward/pallas_call | solution.py:354
  171.4 10.4 all-to-all-start.1
  181.9 22.9 %all-to-all-done.1 = bf16[8,256,128]{1,2,0:T(8,128)(2,1)S(1)} async-done(((bf16[8,256,128]{1,2,0:T(8,128)(2,1)}), bf16[8,256,128]{1,2,0:T(8,128)(2,1)S(1)}, u32[]{:S(2)}, u32[]{:S(2)}) %all-to-all-start.1) | async-done | bytes 524320 | tf_op jit(solution)/shard_map/all_to_all | solution.py:478
  204.7 2.6 fusion.53
  208.3 30.9 %all-gather.10.cloned.1.call-done = bf16[1024,4096]{1,0:T(8,128)(2,1)} async-done(((bf16[32,4096]{1,0:T(8,128)(2,1)}), bf16[1024,4096]{1,0:T(8,128)(2,1)}) %all-gather.10.cloned.1.call-update) | async-done | bytes 8388624 | tf_op jit(solution)/shard_map/all_gather | solution.py:501
  239.1 15.8 %multiply_convert_fusion = (bf16[256,4096]{1,0:T(8,128)(2,1)}, f32[256,4096]{1,0:T(8,128)}, f32[256,4096]{1,0:T(8,128)}) fusion(bf16[1024,4096]{1,0:T(8,128)(2,1)} %all-gather.10.cloned.1.call-done, f32[256,1024]{1,0:T(8,128)S(1)} %get-tuple-element.30, f32[1024]{0:T(1024)S(1)} %bitcast.143, f32[256]{0:T(256)S(1)} %fusion.40, ...), kind=kOutput, calls=%fused_computation.6 | convolution fusion | flops 2216689664 | bytes 19929088 | tf_op jit(solution)/shard_map/dot_general | solution.py:35
  254.9 62.8 %all-gather.12.cloned.1.call-done = bf16[4096,1024]{1,0:T(8,128)(2,1)} async-done(((bf16[128,1024]{1,0:T(8,128)(2,1)}), bf16[4096,1024]{1,0:T(8,128)(2,1)}) %all-gather.12.cloned.1.call-update) | async-done | bytes 8388624 | tf_op jit(solution)/shard_map/all_gather | solution.py:502
  317.7 6.5 fusion.54
  326.5 11.0 add_convert_fusion
  337.4 6.7 multiply_reduce_fusion
  347.7 18.9 %all_to_all.20 = bf16[8,256,128]{2,1,0:T(8,128)(2,1)} all-to-all(bf16[8,256,128]{2,1,0:T(8,128)(2,1)S(1)} %bitcast.137), channel_id=1, replica_groups=mesh['fsdp'=4,'ctx'=8] {'ctx'}, dimensions={0} | all-to-all | bytes 1048576 | tf_op jit(solution)/shard_map/all_to_all | solution.py:471
  366.6 35.5 %attention_backward.1 = bf16[2048,384]{1,0:T(8,128)(2,1)} custom-call(bf16[2048,384]{1,0:T(8,128)(2,1)} %bitcast.123, bf16[2048,384]{1,0:T(8,128)(2,1)} %bitcast.124, bf16[2048,384]{1,0:T(8,128)(2,1)} %bitcast.125, bf16[2048,128]{1,0:T(8,128)(2,1)} %bitcast.133, f32[2048,128]{1,0:T(8,128)} %get-tuple-element.11.mixed_ref, ...), custom_call_target="tpu_custom_call" | custom-call | tf_op jit(solution)/shard_map/attention_backward/pallas_call | solution.py:434
  402.1 2.6 copy.46
  404.7 40.6 %all_to_all.21 = bf16[8,256,384]{1,2,0:T(8,128)(2,1)S(1)} all-to-all(bf16[8,256,384]{1,2,0:T(8,128)(2,1)} %copy.46), channel_id=1, replica_groups=mesh['fsdp'=4,'ctx'=8] {'ctx'}, dimensions={0} | all-to-all | bytes 3145728 | tf_op jit(solution)/shard_map/all_to_all | solution.py:478
  445.5 5.4 fusion.22
  453.6 3.4 convolution_convert_fusion.4
  457.3 6.1 convolution_convert_fusion.2
  463.5 7.3 convolution_convert_fusion.1
  472.0 7.2 convolution_convert_fusion
  482.1 105.9 %reduce-scatter.16.cloned.1.call-done = f32[32,4]{1,0:T(8,128)} async-done(((f32[1024,4]{1,0:T(8,128)}), f32[32,4]{1,0:T(8,128)}) %reduce-scatter.16.cloned.1.call-update) | async-done | bytes 528
  589.4 136.3 %reduce-scatter.10.cloned.1.call-done = bf16[32,1024]{1,0:T(8,128)(2,1)} async-done(((bf16[1024,1024]{1,0:T(8,128)(2,1)}), bf16[32,1024]{1,0:T(8,128)(2,1)}) %reduce-scatter.10.cloned.1.call-update) | async-done | bytes 65552 | tf_op jit(solution)/shard_map/reduce_scatter | solution.py:484
  727.2 115.6 %reduce-scatter.8.cloned.1.call-done = bf16[32,3072]{1,0:T(8,128)(2,1)} async-done(((bf16[1024,3072]{1,0:T(8,128)(2,1)}), bf16[32,3072]{1,0:T(8,128)(2,1)}) %reduce-scatter.8.cloned.1.call-update) | async-done | bytes 196624 | tf_op jit(solution)/shard_map/reduce_scatter | solution.py:484
  842.8 1.7 fusion.51
  844.4 183.9 %reduce-scatter.12.cloned.1.call-done = bf16[32,4096]{1,0:T(8,128)(2,1)} async-done(((bf16[1024,4096]{1,0:T(8,128)(2,1)}), bf16[32,4096]{1,0:T(8,128)(2,1)}) %reduce-scatter.12.cloned.1.call-update) | async-done | bytes 262160 | tf_op jit(solution)/shard_map/reduce_scatter | solution.py:484
  1028.4 1.8 convert_element_type.101
  1030.1 185.1 %reduce-scatter.14.cloned.1.call-done = bf16[128,1024]{1,0:T(8,128)(2,1)} async-done(((bf16[4096,1024]{1,0:T(8,128)(2,1)}), bf16[128,1024]{1,0:T(8,128)(2,1)}) %reduce-scatter.14.cloned.1.call-update) | async-done | bytes 262160 | tf_op jit(solution)/shard_map/reduce_scatter | solution.py:484
  1215.3 1.8 convert_element_type.103
  (101 shorter events, 28.6 us)
Async XLA Ops:
  7.2 77.1 %all-gather.6.cloned.1.call-start = ((), (), s32[]{:S(2)}) async-start(), calls=%async_computation.9 | async-start | bytes 6488064 | tf_op jit(solution)/shard_map/all_gather | solution.py:496
  8.8 173.0 %all-gather.8.cloned.1.call-start = ((), (), s32[]{:S(2)}) async-start(), calls=%async_computation.10 | async-start | bytes 2162688 | tf_op jit(solution)/shard_map/all_gather | solution.py:500
  9.6 229.5 %all-gather.10.cloned.1.call-start = ((), (), s32[]{:S(2)}) async-start(), calls=%async_computation.11 | async-start | bytes 8650752 | tf_op jit(solution)/shard_map/all_gather | solution.py:501
  10.3 307.4 %all-gather.12.cloned.1.call-start = ((), (), s32[]{:S(2)}) async-start(), calls=%async_computation.12 | async-start | bytes 8650752 | tf_op jit(solution)/shard_map/all_gather | solution.py:502
  89.2 5.8 copy-start.15
  91.4 47.5 %all-to-all-start = ((bf16[8,256,384]{1,2,0:T(8,128)(2,1)}), bf16[8,256,384]{1,2,0:T(8,128)(2,1)S(1)}, u32[]{:S(2)}, u32[]{:S(2)}) async-start(bf16[8,256,384]{1,2,0:T(8,128)(2,1)} %bitcast.6), calls=%async_computation | async-start | bytes 3145728 | tf_op jit(solution)/shard_map/all_to_all | solution.py:471
  137.5 2.9 copy-start.14
  169.1 38.5 %copy-start = (bf16[1,256,1024]{2,1,0:T(8,128)(2,1)S(1)}, bf16[1,256,1024]{2,1,0:T(8,128)(2,1)}, u32[]{:S(2)}) copy-start(bf16[1,256,1024]{2,1,0:T(8,128)(2,1)} %param.10) | copy-start | bytes 1572868
  171.4 33.3 %all-to-all-start.1 = ((bf16[8,256,128]{1,2,0:T(8,128)(2,1)}), bf16[8,256,128]{1,2,0:T(8,128)(2,1)S(1)}, u32[]{:S(2)}, u32[]{:S(2)}) async-start(bf16[8,256,128]{1,2,0:T(8,128)(2,1)} %copy.43), calls=%async_computation.1 | async-start | bytes 1048576 | tf_op jit(solution)/shard_map/all_to_all | solution.py:478
  181.8 406.2 %reduce-scatter.16.cloned.1.call-start = ((), (), s32[]{:S(2)}) async-start(), calls=%async_computation.17 | async-start | bytes 540672
  204.7 3.5 copy-start.5
  317.7 6.8 copy-start.3
  324.2 2.3 copy-start.16
  326.2 11.2 copy-start.10
  337.4 6.7 copy-start.12
  344.2 2.6 copy-start.13
  344.6 1.2 copy-start.1
  345.8 1.0 copy-start.9
  445.5 5.4 copy-start.4
  445.5 8.1 copy-start.6
  450.9 1.0 copy-start.7
  453.5 272.2 %reduce-scatter.10.cloned.1.call-start = ((), (), s32[]{:S(2)}) async-start(), calls=%async_computation.14 | async-start | bytes 2162688 | tf_op jit(solution)/shard_map/reduce_scatter | solution.py:484
  457.0 385.8 %reduce-scatter.8.cloned.1.call-start = ((), (), s32[]{:S(2)}) async-start(), calls=%async_computation.13 | async-start | bytes 6488064 | tf_op jit(solution)/shard_map/reduce_scatter | solution.py:484
  463.4 564.9 %reduce-scatter.12.cloned.1.call-start = ((), (), s32[]{:S(2)}) async-start(), calls=%async_computation.15 | async-start | bytes 8650752 | tf_op jit(solution)/shard_map/reduce_scatter | solution.py:484
  470.8 1.2 copy-start.11
  470.8 744.5 %reduce-scatter.14.cloned.1.call-start = ((), (), s32[]{:S(2)}) async-start(), calls=%async_computation.16 | async-start | bytes 8650752 | tf_op jit(solution)/shard_map/reduce_scatter | solution.py:484
  479.3 1.2 copy-start.2
  479.3 1.5 copy-start.8
Sparse Core Ops, SparseCore 0:
  11.5 72.1 all-gather.5
  86.7 69.2 all-gather.7
  159.0 80.0 all-gather.9
  242.0 75.7 all-gather.11
  453.7 134.3 reduce-scatter.15
  590.2 135.4 reduce-scatter.9
  731.3 111.4 reduce-scatter.7
  845.1 183.2 reduce-scatter.11
  1030.7 184.5 reduce-scatter.13

commit v2 on v1

--- a/solution.py
+++ b/solution.py
@@ -1,3 +1,4 @@
+import functools
 import math
 
 import jax
@@ -270,6 +271,188 @@
         summed[5],
         summed[6],
     )
+
+
+MESH = pl.DeviceIdType.MESH
+SLAB = 32
+LANES = 1024
+
+
+def places():
+    fsdp, ctx = lax.axis_index("fsdp"), lax.axis_index("ctx")
+    return lax.div(fsdp, 2), lax.rem(fsdp, 2), lax.div(ctx, 2), lax.rem(ctx, 2)
+
+
+def at_place(y, core, z, x):
+    return (y * 2 + core, z * 2 + x)
+
+
+def meet(devices):
+    barrier = pltpu.get_barrier_semaphore()
+    for device in devices:
+        pl.semaphore_signal(barrier, inc=1, device_id=device, device_id_type=MESH)
+    pl.semaphore_wait(barrier, len(devices))
+
+
+def sum_kernel(views, lines, *refs):
+    grads, gain_ref = refs[:lines], refs[lines]
+    out_ref, gain_out, own, zero, first_x, first_y, second, third = refs[lines + 1 : lines + 9]
+    g_own, g_zero, g_first, g_second, g_third, load, send, arrive = refs[lines + 9 :]
+    y, core, z, x = places()
+    partner = at_place(y, 1 - core, z, x)
+    beside = at_place(y, core, z, 1 - x)
+    across = at_place(1 - y, core, z, x)
+    rank = [lax.rem(z + d, 4) for d in (1, 2, 3)]
+    others = [at_place(y, core, r, x) for r in rank]
+    meet([partner, beside, across] + others)
+    count = len(views) + 1
+    last = len(views)
+
+    def pick(k, side):
+        if k == last:
+            return gain_ref.at[:, side]
+        ref, part = views[k]
+        return grads[ref].at[(slice(None), side, slice(None), slice(None)) + part]
+
+    def remote(src, dst, k, phase, device):
+        return pltpu.make_async_remote_copy(
+            src_ref=src,
+            dst_ref=dst,
+            send_sem=send.at[k, phase],
+            recv_sem=arrive.at[k, phase],
+            device_id=device,
+            device_id_type=MESH,
+        )
+
+    def add(total, landed, pairs, rows):
+        def one(i, unused):
+            into, out_of = pairs(i)
+            total[into] = total[into] + landed[out_of]
+            return unused
+
+        lax.fori_loop(0, rows, one, 0)
+
+    def steps(k):
+        if k == last:
+            return g_own, g_zero, g_first, g_second, g_third
+        return own.at[k], zero.at[k], (first_y if k % 2 else first_x).at[k // 2], second.at[k], third.at[k]
+
+    def phase_zero(k):
+        return remote(pick(k, 1 - core), steps(k)[1], k, 0, partner)
+
+    def loading(k):
+        return pltpu.make_async_copy(pick(k, core), steps(k)[0], load.at[k])
+
+    def phase_one(k):
+        total = steps(k)[0]
+        if k % 2:
+            return remote(total.at[1 - y], steps(k)[2], k, 1, across)
+        return remote(total.at[:, :, 1 - x], steps(k)[2], k, 1, beside)
+
+    def phase_two(k):
+        total = steps(k)[0]
+        if k % 2:
+            return remote(total.at[y, :, 1 - x], steps(k)[3], k, 2, beside)
+        return remote(total.at[1 - y, :, x], steps(k)[3], k, 2, across)
+
+    def phase_three(k):
+        total = steps(k)[0]
+        return [
+            remote(total.at[y, r, x], steps(k)[4].at[2 - d], k, 3 + d, others[d])
+            for d, r in enumerate(rank)
+        ]
+
+    def after_zero(k):
+        loading(k).wait()
+        phase_zero(k).wait()
+        total, landed = steps(k)[:2]
+        split = lambda i: (lax.div(i, 8), lax.rem(lax.div(i, 2), 4), lax.rem(i, 2))
+        add(total, landed, lambda i: (split(i), split(i)), 16)
+        phase_one(k).start()
+
+    def after_one(k):
+        phase_one(k).wait()
+        total, landed = steps(k)[0], steps(k)[2]
+        if k % 2:
+            add(total, landed, lambda i: ((y, lax.div(i, 2), lax.rem(i, 2)), (lax.div(i, 2), lax.rem(i, 2))), 8)
+        else:
+            add(total, landed, lambda i: ((lax.div(i, 4), lax.rem(i, 4), x), (lax.div(i, 4), lax.rem(i, 4))), 8)
+        phase_two(k).start()
+
+    def after_two(k):
+        phase_two(k).wait()
+        total, landed = steps(k)[0], steps(k)[3]
+        add(total, landed, lambda i: ((y, i, x), (i,)), 4)
+        for copy in phase_three(k):
+            copy.start()
+
+    def after_three(k):
+        for copy in phase_three(k):
+            copy.wait()
+        total, landed = steps(k)[0], steps(k)[4]
+        value = total[y, z, x].astype(jnp.float32)
+        for d in range(3):
+            value = value + landed[d].astype(jnp.float32)
+        if k == last:
+            gain_out[...] = value
+        else:
+            out_ref[k] = value
+
+    for k in range(count):
+        loading(k).start()
+        phase_zero(k).start()
+    for step in range(count + 3):
+        for lag, run in enumerate((after_zero, after_one, after_two, after_three)):
+            if 0 <= step - lag < count:
+                run(step - lag)
+
+
+def sum_over_devices(grads, gain, collective_id):
+    shaped, views = [], []
+    for ref, grad in enumerate(grads):
+        rows, columns = grad.shape
+        if columns == LANES:
+            parts = rows // (32 * SLAB)
+            shaped.append(grad.reshape(2, 2, 4, 2, parts, SLAB, LANES))
+            views += [(ref, (part,)) for part in range(parts)]
+        else:
+            parts = columns // LANES
+            shaped.append(grad.reshape(2, 2, 4, 2, SLAB, columns))
+            views += [(ref, (slice(None), pl.ds(part * LANES, LANES))) for part in range(parts)]
+    count = len(views)
+    low = jnp.bfloat16
+    slab = (SLAB, LANES)
+    any_spec = pl.BlockSpec(memory_space=pl.ANY)
+    out, gain_out = pl.pallas_call(
+        functools.partial(sum_kernel, views, len(grads)),
+        out_shape=(
+            jax.ShapeDtypeStruct((count,) + slab, jnp.float32),
+            jax.ShapeDtypeStruct((8, 128), jnp.float32),
+        ),
+        in_specs=[any_spec] * (len(grads) + 1),
+        out_specs=(pl.BlockSpec(memory_space=pltpu.VMEM), pl.BlockSpec(memory_space=pltpu.VMEM)),
+        scratch_shapes=[
+            pltpu.VMEM((count, 2, 4, 2) + slab, low),
+            pltpu.VMEM((count, 2, 4, 2) + slab, low),
+            pltpu.VMEM(((count + 1) // 2, 2, 4) + slab, low),
+            pltpu.VMEM(((count + 1) // 2, 4, 2) + slab, low),
+            pltpu.VMEM((count, 4) + slab, low),
+            pltpu.VMEM((count, 3) + slab, low),
+            pltpu.VMEM((2, 4, 2, 8, 128), jnp.float32),
+            pltpu.VMEM((2, 4, 2, 8, 128), jnp.float32),
+            pltpu.VMEM(((4, 2) if count % 2 else (2, 4)) + (8, 128), jnp.float32),
+            pltpu.VMEM((4, 8, 128), jnp.float32),
+            pltpu.VMEM((3, 8, 128), jnp.float32),
+            pltpu.SemaphoreType.DMA((count + 1,)),
+            pltpu.SemaphoreType.DMA((count + 1, 6)),
+            pltpu.SemaphoreType.DMA((count + 1, 6)),
+        ],
+        compiler_params=pltpu.CompilerParams(
+            collective_id=collective_id, has_side_effects=True, vmem_limit_bytes=60 * 2**20
+        ),
+        name="sum_over_devices",
+    )(*shaped, gain)
+    return out, gain_out
 
 
 TILE = 256
@@ -480,12 +663,6 @@
     return split.reshape(tokens, count * groups * wide)
 
 
-def scatter_sum(grad):
-    return lax.psum_scatter(
-        grad.astype(jnp.bfloat16), ("fsdp", "ctx"), scatter_dimension=0, tiled=True
-    ).astype(jnp.float32)
-
-
 def fast_body(
     tokens_in, block_ids, w_query, w_key, w_value, w_out, w_up, w_down, norm_gain, cotangent
 ):
@@ -517,11 +694,11 @@
     unused_four, pull_four = jax.vjp(layer_norm, lowered, gains[3])
     grad_lowered, gain_four = pull_four(upstream)
     grad_lowered = grad_lowered.astype(jnp.bfloat16)
-    grad_down = scatter_sum(outer_sum(active, grad_lowered))
+    grad_down = outer_sum(active, grad_lowered).astype(jnp.bfloat16)
     grad_active = back_project(grad_lowered, full_down)
     unused_gelu, pull_gelu = jax.vjp(gelu_exact, lifted)
     grad_lifted = pull_gelu(grad_active)[0].astype(jnp.bfloat16)
-    grad_up = scatter_sum(outer_sum(inner, grad_lifted))
+    grad_up = outer_sum(inner, grad_lifted).astype(jnp.bfloat16)
     grad_inner = back_project(grad_lifted, full_up)
     unused_three, pull_three = jax.vjp(layer_norm, hidden, gains[2])
     grad_hidden_branch, gain_three = pull_three(grad_inner)
@@ -529,30 +706,38 @@
     unused_two, pull_two = jax.vjp(layer_norm, branch, gains[1])
     grad_branch, gain_two = pull_two(grad_hidden)
     grad_branch = grad_branch.astype(jnp.bfloat16)
-    grad_out = scatter_sum(outer_sum(mixed_low, grad_branch))
+    grad_out = outer_sum(mixed_low, grad_branch).astype(jnp.bfloat16)
     grad_mixed = back_project(grad_branch, full_out).astype(jnp.bfloat16)
     grad_joined = attention_backward(
         joined, to_heads(grad_mixed, groups, 1), mixed, log_total, blocks
     )
     grad_qkv = to_tokens(grad_joined, groups, 3)
-    grad_three = scatter_sum(outer_sum(normed, grad_qkv))
+    grad_three = outer_sum(normed, grad_qkv).astype(jnp.bfloat16)
     grad_normed = back_project(grad_qkv, full_qkv)
     unused_one, pull_one = jax.vjp(layer_norm, tokens, gains[0])
     grad_norm_in, gain_one = pull_one(grad_normed)
     grad_tokens = (grad_hidden + grad_norm_in).astype(jnp.bfloat16)[None]
     gain_grads = jnp.stack([gain_one, gain_two, gain_three, gain_four])
-    gain_sum = lax.psum_scatter(gain_grads, axes, scatter_dimension=1, tiled=True)
+    sums, gain_sum = sum_over_devices(
+        [grad_three, grad_out, grad_up, grad_down], by_owner(gain_grads), 3
+    )
     return (
         layer_out,
         grad_tokens,
-        grad_three[:, :width],
-        grad_three[:, width : 2 * width],
-        grad_three[:, 2 * width :],
-        grad_out,
-        grad_up,
-        grad_down,
-        gain_sum,
-    )
+        sums[0],
+        sums[1],
+        sums[2],
+        sums[3],
+        sums[4:8].transpose(1, 0, 2).reshape(w_up.shape),
+        sums[8:].reshape(w_down.shape),
+        gain_sum[0].reshape(norm_gain.shape),
+    )
+
+
+def by_owner(gain_grads):
+    kinds, width = gain_grads.shape
+    rows = gain_grads.reshape(kinds, 32, width // 32).transpose(1, 0, 2).reshape(32, 1, -1)
+    return jnp.pad(rows, ((0, 0), (0, 7), (0, 0))).reshape(2, 2, 4, 2, 8, rows.shape[-1])
 
 
 def pick(mesh):

time: 1230 us -> 607 us (0.49)
  waiting for transfers between devices: 845 us -> 140 us
  Pallas kernels: 64.1 us -> 194 us
  blocking collectives: 173 us -> 132 us
    reduce_scatter x4 -> x0, waiting for transfers between devices: 621 us -> none  [scatter_sum(): lax.psum_scatter(grad.astype(jnp.bfloat16), ('fsdp', 'ctx'), scatter_dime...]
    pallas_call x0 -> x1, Pallas kernels: none -> 130 us  [sum_over_devices(): pl.pallas_call(functools.partial(sum_kernel, views, len(grads)), out_shap...]
    unnamed x10 -> x4, waiting for transfers between devices: 108 us -> 1.91 us
    all_to_all x1 -> x0, blocking collectives: 40.6 us -> none  [to_tokens(): lax.all_to_all(rows.reshape(groups, tokens, count * wide), 'ctx', 0, 0, t...]
    all_to_all x1 -> x2, waiting for transfers between devices: 22.9 us -> 44.1 us  [to_tokens(): lax.all_to_all(rows.reshape(groups, tokens, count * wide), 'ctx', 0, 0, t...]
  transfers between devices with their start and end apart: 11 -> 7, of which waited for: 8 -> 4; matrix products, arithmetic and copies ran while one was open for 5% -> 8% of each run, Pallas kernels for 2% -> 5%
where the time goes in v2:
time: 607 us; the launch traced here: 602 us
  Pallas kernels  194 us (32%)
  waiting for transfers between devices  140 us (23%)
  blocking collectives  132 us (22%)
  matrix products  72.4 us (12%)
  local copies, waits for them, and re-layouts  19.1 us (3%)
  starting transfers between devices  18.9 us (3%)
  between operations  14.6 us (2%)
  other arithmetic  11.8 us (2%)
    pallas_call x1, Pallas kernels, sum_over_devices(): pl.pallas_call(functools.partial(sum_kernel, views, len(grads)), out_shap...  130 us
    all_gather x1, blocking collectives, fast_body(): full_gain = lax.all_gather(norm_gain, axes, axis=1, tiled=True)  70.7 us
    all_gather x1, waiting for transfers between devices, fast_body(): full_down = lax.all_gather(w_down, axes, axis=0, tiled=True)  63 us
    all_to_all x2, waiting for transfers between devices, to_tokens(): lax.all_to_all(rows.reshape(groups, tokens, count * wide), 'ctx', 0, 0, t...  44.1 us
    all_gather x1, blocking collectives, fast_body(): blocks = lax.all_gather(block_ids, 'ctx', axis=1, tiled=True)[0]  42.5 us
    pallas_call x1, Pallas kernels, attention_backward(): pl.pallas_call(grads_kernel, grid=(tiles,), out_shape=jax.ShapeDtypeStruc...  35.5 us
    all_gather x1, waiting for transfers between devices, fast_body(): full_up = lax.all_gather(w_up, axes, axis=0, tiled=True)  30.9 us
    dot_general x4, matrix products, project(): return jnp.dot(left, right, preferred_element_type=jnp.float32)  29.6 us
  transfers between devices with their start and end apart: 7, of which 4 were waited for; matrix products, arithmetic and copies ran while one was open for 8% of the time, Pallas kernels for 5%

profile of v2, /device:TPU:0, one launch (start us, length us, event | category | flops | bytes accessed | tf_op | source)
XLA Modules:
  0.0 602.3 jit_solution(17954998743601996191)
XLA Ops:
  7.2 1.6 pad_maximum_fusion
  10.9 70.7 %all-gather = bf16[32,32,4]{1,2,0:T(4,128)(2,1)S(1)} all-gather(bf16[1,32,4]{1,2,0:T(4,128)(2,1)} %bitcast.174), channel_id=1, replica_groups=mesh['fsdp'=4,'ctx'=8] {'fsdp','ctx'}, dimensions={0}, use_global_device_ids=true | all-gather | bytes 8448 | tf_op jit(solution)/shard_map/all_gather | solution.py:672
  84.3 4.9 fusion.6
  89.5 1.9 copy.42
  91.4 3.6 all-to-all-start
  95.0 42.5 %all_gather.20.col_ref = s32[1,2048]{1,0:T(1,128)S(1)} all-gather(s32[1,256]{1,0:T(1,128)S(1)} %copy-done.14), channel_id=1, replica_groups=mesh['fsdp'=4,'ctx'=8] {'ctx'}, dimensions={1}, use_global_device_ids=true | all-gather | bytes 9216 | tf_op jit(solution)/shard_map/all_gather | solution.py:676
  137.5 1.4 copy.44.row_ref
  138.9 1.6 copy.43
  140.5 28.6 %attention_forward.1 = (f32[2048,128]{1,0:T(8,128)}, f32[8,8,512]{2,1,0:T(8,128)}) custom-call(bf16[2048,384]{1,0:T(8,128)(2,1)} %bitcast.134, bf16[2048,384]{1,0:T(8,128)(2,1)} %bitcast.135, bf16[2048,384]{1,0:T(8,128)(2,1)} %bitcast.136, s32[2048,1]{1,0:T(8,128)} %copy.44.row_ref, s32[1,2048]{1,0:T(1,128)} %copy-done.13), custom_call_target="tpu_custom_call" | custom-call | tf_op jit(solution)/shard_map/attention_forward/pallas_call | solution.py:537
  171.4 10.6 %all-to-all-start.1 = ((bf16[8,256,128]{1,2,0:T(8,128)(2,1)}), bf16[8,256,128]{1,2,0:T(8,128)(2,1)S(1)}, u32[]{:S(2)}, u32[]{:S(2)}) async-start(bf16[8,256,128]{1,2,0:T(8,128)(2,1)} %copy.45), calls=%async_computation.1 | async-start | bytes 1048576 | tf_op jit(solution)/shard_map/all_to_all | solution.py:661
  182.0 22.9 %all-to-all-done.1 = bf16[8,256,128]{1,2,0:T(8,128)(2,1)S(1)} async-done(((bf16[8,256,128]{1,2,0:T(8,128)(2,1)}), bf16[8,256,128]{1,2,0:T(8,128)(2,1)S(1)}, u32[]{:S(2)}, u32[]{:S(2)}) %all-to-all-start.1) | async-done | bytes 524320 | tf_op jit(solution)/shard_map/all_to_all | solution.py:661
  204.9 2.6 fusion.53
  208.4 30.9 %all-gather.10.cloned.1.call-done = bf16[1024,4096]{1,0:T(8,128)(2,1)} async-done(((bf16[32,4096]{1,0:T(8,128)(2,1)}), bf16[1024,4096]{1,0:T(8,128)(2,1)}) %all-gather.10.cloned.1.call-update) | async-done | bytes 8388624 | tf_op jit(solution)/shard_map/all_gather | solution.py:678
  239.3 15.6 %multiply_convert_fusion = (bf16[256,4096]{1,0:T(8,128)(2,1)}, f32[256,4096]{1,0:T(8,128)}, f32[256,4096]{1,0:T(8,128)}) fusion(bf16[1024,4096]{1,0:T(8,128)(2,1)} %all-gather.10.cloned.1.call-done, f32[256,1024]{1,0:T(8,128)S(1)} %get-tuple-element.34, f32[1024]{0:T(1024)S(1)} %bitcast.163, f32[256]{0:T(256)S(1)} %fusion.40, ...), kind=kOutput, calls=%fused_computation.6 | convolution fusion | flops 2216689664 | bytes 19929088 | tf_op jit(solution)/shard_map/dot_general | solution.py:36
  254.9 63.0 %all-gather.12.cloned.1.call-done = bf16[4096,1024]{1,0:T(8,128)(2,1)} async-done(((bf16[128,1024]{1,0:T(8,128)(2,1)}), bf16[4096,1024]{1,0:T(8,128)(2,1)}) %all-gather.12.cloned.1.call-update) | async-done | bytes 8388624 | tf_op jit(solution)/shard_map/all_gather | solution.py:679
  317.9 6.5 %fusion.54 = (f32[256]{0:T(256)S(1)}, f32[256,1024]{1,0:T(8,128)S(1)}) fusion(bf16[256,4096]{1,0:T(8,128)(2,1)} %get-tuple-element.31, bf16[4096,1024]{1,0:T(8,128)(2,1)} %all-gather.12.cloned.1.call-done), kind=kOutput, calls=%fused_computation.115 | convolution fusion | flops 2147745536 | bytes 11535360 | tf_op jit(solution)/shard_map/dot_general | solution.py:36
  326.6 10.8 %add_convert_fusion = bf16[256,4096]{1,0:T(8,128)(2,1)S(1)} fusion(f32[256,4096]{1,0:T(8,128)S(1)} %copy-done.15, f32[256,4096]{1,0:T(8,128)} %get-tuple-element.48, bf16[4096,1024]{1,0:T(8,128)(2,1)} %all-gather.12.cloned.1.call-done, f32[256,1024]{1,0:T(8,128)S(1)} %get-tuple-element.30, f32[256]{0:T(256)S(1)} %negate_multiply_fusion.4), kind=kOutput, calls=%fused_computation.5 | convolution fusion | flops 2162688000 | bytes 19923968 | tf_op jit(solution)/shard_map/dot_general | solution.py:46
  337.5 6.7 %multiply_reduce_fusion = (f32[1024]{0:T(1024)S(1)}, f32[256]{0:T(256)S(1)}, f32[256,1024]{1,0:T(8,128)S(1)}) fusion(f32[256,1024]{1,0:T(8,128)S(1)} %get-tuple-element.34, f32[256]{0:T(256)S(1)} %fusion.40, f32[256]{0:T(256)S(1)} %broadcast_multiply_fusion.1, f32[1024]{0:T(1024)S(1)} %bitcast.164, bf16[256,4096]{1,0:T(8,128)(2,1)S(1)} %add_convert_fusion, ...), kind=kOutput, calls=%fused_computation.54 | convolution fusion | flops 2149317376 | bytes 12594176 | tf_op jit(solution)/shard_map/dot_general | solution.py:46
  347.7 18.9 %all_to_all.20 = bf16[8,256,128]{2,1,0:T(8,128)(2,1)} all-to-all(bf16[8,256,128]{2,1,0:T(8,128)(2,1)S(1)} %bitcast.154), channel_id=1, replica_groups=mesh['fsdp'=4,'ctx'=8] {'ctx'}, dimensions={0} | all-to-all | bytes 1048576 | tf_op jit(solution)/shard_map/all_to_all | solution.py:654
  366.6 35.5 %attention_backward.1 = bf16[2048,384]{1,0:T(8,128)(2,1)} custom-call(bf16[2048,384]{1,0:T(8,128)(2,1)} %bitcast.137, bf16[2048,384]{1,0:T(8,128)(2,1)} %bitcast.138, bf16[2048,384]{1,0:T(8,128)(2,1)} %bitcast.139, bf16[2048,128]{1,0:T(8,128)(2,1)} %bitcast.151, f32[2048,128]{1,0:T(8,128)} %get-tuple-element.13.mixed_ref, ...), custom_call_target="tpu_custom_call" | custom-call | tf_op jit(solution)/shard_map/attention_backward/pallas_call | solution.py:617
  402.2 2.6 copy.48
  404.8 4.5 all-to-all-start.3
  409.6 3.5 convolution_convert_fusion.4
  413.2 5.7 convolution_convert_fusion
  418.8 5.7 convolution_convert_fusion.1
  424.5 21.2 %all-to-all-done.3 = bf16[8,256,384]{1,2,0:T(8,128)(2,1)} async-done(((bf16[8,256,384]{1,2,0:T(8,128)(2,1)}), bf16[8,256,384]{1,2,0:T(8,128)(2,1)}, u32[]{:S(2)}, u32[]{:S(2)}) %all-to-all-start.3) | async-done | bytes 1572896 | tf_op jit(solution)/shard_map/all_to_all | solution.py:661
  445.8 1.5 copy.49
  447.3 4.7 convolution_convert_fusion.2
  452.0 4.8 fusion.22
  458.3 129.6 %sum_over_devices.1 = (f32[12,32,1024]{2,1,0:T(8,128)}, f32[8,128]{1,0:T(8,128)}) custom-call(bf16[2,2,4,2,32,3072]{5,4,3,2,1,0:T(8,128)(2,1)} %bitcast.142, bf16[2,2,4,2,1,32,1024]{6,5,4,3,2,1,0:T(8,128)(2,1)} %bitcast.143, bf16[2,2,4,2,32,4096]{5,4,3,2,1,0:T(8,128)(2,1)} %bitcast.141, bf16[2,2,4,2,4,32,1024]{6,5,4,3,2,1,0:T(8,128)(2,1)} %bitcast.140, ...), custom_call_target="tpu_custom_call" | custom-call | tf_op jit(solution)/shard_map/sum_over_devices/pallas_call | solution.py:426
  587.9 1.9 slice_bitcast_fusion.1
  589.8 2.1 fusion.51
  (91 shorter events, 19.2 us)
Async XLA Ops:
  7.2 77.1 %all-gather.6.cloned.1.call-start = ((), (), s32[]{:S(2)}) async-start(), calls=%async_computation.4 | async-start | bytes 6488064 | tf_op jit(solution)/shard_map/all_gather | solution.py:673
  8.8 173.2 %all-gather.8.cloned.1.call-start = ((), (), s32[]{:S(2)}) async-start(), calls=%async_computation.5 | async-start | bytes 2162688 | tf_op jit(solution)/shard_map/all_gather | solution.py:677
  9.6 229.7 %all-gather.10.cloned.1.call-start = ((), (), s32[]{:S(2)}) async-start(), calls=%async_computation.6 | async-start | bytes 8650752 | tf_op jit(solution)/shard_map/all_gather | solution.py:678
  10.3 307.6 %all-gather.12.cloned.1.call-start = ((), (), s32[]{:S(2)}) async-start(), calls=%async_computation.7 | async-start | bytes 8650752 | tf_op jit(solution)/shard_map/all_gather | solution.py:679
  89.2 5.8 copy-start.14
  91.4 47.5 %all-to-all-start = ((bf16[8,256,384]{1,2,0:T(8,128)(2,1)}), bf16[8,256,384]{1,2,0:T(8,128)(2,1)S(1)}, u32[]{:S(2)}, u32[]{:S(2)}) async-start(bf16[8,256,384]{1,2,0:T(8,128)(2,1)} %bitcast.144), calls=%async_computation | async-start | bytes 3145728 | tf_op jit(solution)/shard_map/all_to_all | solution.py:654
  137.5 2.9 copy-start.13
  169.1 38.7 %copy-start = (bf16[1,256,1024]{2,1,0:T(8,128)(2,1)S(1)}, bf16[1,256,1024]{2,1,0:T(8,128)(2,1)}, u32[]{:S(2)}) copy-start(bf16[1,256,1024]{2,1,0:T(8,128)(2,1)} %param.10) | copy-start | bytes 1572868
  171.4 33.5 %all-to-all-start.1 = ((bf16[8,256,128]{1,2,0:T(8,128)(2,1)}), bf16[8,256,128]{1,2,0:T(8,128)(2,1)S(1)}, u32[]{:S(2)}, u32[]{:S(2)}) async-start(bf16[8,256,128]{1,2,0:T(8,128)(2,1)} %copy.45), calls=%async_computation.1 | async-start | bytes 1048576 | tf_op jit(solution)/shard_map/all_to_all | solution.py:661
  204.9 3.5 copy-start.4
  317.9 6.8 %copy-start.3 = (bf16[1,256,1024]{2,1,0:T(8,128)(2,1)S(1)}, bf16[1,256,1024]{2,1,0:T(8,128)(2,1)}, u32[]{:S(2)}) copy-start(bf16[1,256,1024]{2,1,0:T(8,128)(2,1)} %param.19) | copy-start | bytes 1572868
  324.4 2.3 copy-start.15
  326.4 11.1 %copy-start.7 = (f32[256,1024]{1,0:T(8,128)}, f32[256,1024]{1,0:T(8,128)S(1)}, u32[]{:S(2)}) copy-start(f32[256,1024]{1,0:T(8,128)S(1)} %get-tuple-element.30) | copy-start | bytes 3145732
  337.5 6.7 %copy-start.10 = (bf16[256,4096]{1,0:T(8,128)(2,1)}, bf16[256,4096]{1,0:T(8,128)(2,1)S(1)}, u32[]{:S(2)}) copy-start(bf16[256,4096]{1,0:T(8,128)(2,1)S(1)} %add_convert_fusion) | copy-start | bytes 6291460
  344.2 2.5 copy-start.12
  344.6 1.2 copy-start.1
  345.8 1.0 copy-start.6
  402.2 7.4 %copy-start.5 = (bf16[8,256,128]{1,2,0:T(8,128)(2,1)S(1)}, bf16[8,256,128]{1,2,0:T(8,128)(2,1)}, u32[]{:S(2)}) copy-start(bf16[8,256,128]{1,2,0:T(8,128)(2,1)} %copy-done.4) | copy-start | bytes 1572868
  404.8 41.0 %all-to-all-start.3 = ((bf16[8,256,384]{1,2,0:T(8,128)(2,1)}), bf16[8,256,384]{1,2,0:T(8,128)(2,1)}, u32[]{:S(2)}, u32[]{:S(2)}) async-start(bf16[8,256,384]{1,2,0:T(8,128)(2,1)} %copy.48), calls=%async_computation.3 | async-start | bytes 3145728 | tf_op jit(solution)/shard_map/all_to_all | solution.py:661
  409.6 3.5 copy-start.8
  409.6 3.5 copy-start.9
  413.2 5.7 copy-start.11
  458.3 133.6 %copy-start.2 = (f32[256,1024]{1,0:T(8,128)S(1)}, f32[256,1024]{1,0:T(8,128)}, u32[]{:S(2)}) copy-start(f32[256,1024]{1,0:T(8,128)} %copy-done.1) | copy-start | bytes 3145732
Sparse Core Ops, SparseCore 0:
  11.5 72.1 all-gather.5
  86.7 69.2 all-gather.7
  159.0 80.2 all-gather.9
  242.1 75.7 all-gather.11

commit v3 on v2

--- a/solution.py
+++ b/solution.py
@@ -455,6 +455,343 @@
     return out, gain_out
 
 
+def gather_schedule(chunks, send, arrive, keep):
+    y, core, z, x = places()
+    partner = at_place(y, 1 - core, z, x)
+    beside = at_place(y, core, z, 1 - x)
+    across = at_place(1 - y, core, z, x)
+    rank = [lax.rem(z + d, 4) for d in (1, 2, 3)]
+    others = [at_place(y, core, r, x) for r in rank]
+    count = len(chunks)
+    every = slice(None)
+
+    def remote(src, dst, k, phase, device):
+        return pltpu.make_async_remote_copy(
+            src_ref=src,
+            dst_ref=dst,
+            send_sem=send.at[k, phase],
+            recv_sem=arrive.at[k, phase],
+            device_id=device,
+            device_id_type=MESH,
+        )
+
+    def keeping(k):
+        own, whole = chunks[k]
+        return pltpu.make_async_copy(own, whole(y, core, z, x), keep.at[k])
+
+    def along_z(k):
+        own, whole = chunks[k]
+        return [remote(own, whole(y, core, z, x), k, 3 + d, others[d]) for d in range(3)]
+
+    def hop(k, phase):
+        whole = chunks[k][1]
+        if phase == 0:
+            part, device = whole(y, core, every, x), (across if k % 2 else beside)
+        elif k % 2:
+            part, device = whole(every, core, every, x), beside
+        else:
+            part, device = whole(y, core, every, every), across
+        return remote(part, part, k, phase, device)
+
+    def over(k):
+        part = chunks[k][1](every, core, every, every)
+        return remote(part, part, k, 2, partner)
+
+    def begin():
+        for k in range(count):
+            keeping(k).start()
+            for copy in along_z(k):
+                copy.start()
+
+    def after_z(k):
+        keeping(k).wait()
+        for copy in along_z(k):
+            copy.wait()
+        hop(k, 0).start()
+
+    def after_first(k):
+        hop(k, 0).wait()
+        hop(k, 1).start()
+
+    def after_second(k):
+        hop(k, 1).wait()
+        over(k).start()
+
+    def after_over(k):
+        over(k).wait()
+
+    steps = [begin]
+    for step in range(count + 3):
+        for lag, run in enumerate((after_z, after_first, after_second, after_over)):
+            if 0 <= step - lag < count:
+                steps.append(functools.partial(run, step - lag))
+    return steps
+
+
+def weight_chunks(shards, wholes):
+    chunks = []
+    for own, whole in zip(shards, wholes):
+        columns = own.shape[1]
+        if len(whole.shape) == 7:
+            for part in range(whole.shape[4]):
+                chunks.append(
+                    (own.at[pl.ds(part * SLAB, SLAB)], lambda *p, w=whole, n=part: w.at[p + (n,)])
+                )
+        elif columns > LANES:
+            for part in range(columns // LANES):
+                at = pl.ds(part * LANES, LANES)
+                chunks.append(
+                    (own.at[:, at], lambda *p, w=whole, n=at: w.at[p + (slice(None), n)])
+                )
+        else:
+            chunks.append((own, lambda *p, w=whole: w.at[p]))
+    return chunks
+
+
+def whole_shape(shard):
+    rows, columns = shard.shape
+    if rows > SLAB and columns == LANES:
+        return jax.ShapeDtypeStruct((2, 2, 4, 2, rows // SLAB, SLAB, columns), shard.dtype)
+    return jax.ShapeDtypeStruct((2, 2, 4, 2, rows, columns), shard.dtype)
+
+
+def gather_kernel(count, *refs):
+    shards, wholes = refs[:count], refs[count : 2 * count]
+    send, arrive, keep = refs[2 * count :]
+    y, core, z, x = places()
+    meet(
+        [at_place(y, 1 - core, z, x), at_place(y, core, z, 1 - x), at_place(1 - y, core, z, x)]
+        + [at_place(y, core, lax.rem(z + d, 4), x) for d in (1, 2, 3)]
+    )
+    for step in gather_schedule(weight_chunks(shards, wholes), send, arrive, keep):
+        step()
+
+
+def gather_over_devices(shards, collective_id):
+    shapes = [whole_shape(shard) for shard in shards]
+    count = sum(max(1, shard.size // (SLAB * LANES)) for shard in shards)
+    any_spec = pl.BlockSpec(memory_space=pl.ANY)
+    wholes = pl.pallas_call(
+        functools.partial(gather_kernel, len(shards)),
+        out_shape=shapes,
+        in_specs=[pl.BlockSpec(memory_space=pltpu.VMEM)] * len(shards),
+        out_specs=[any_spec] * len(shards),
+        scratch_shapes=[
+            pltpu.SemaphoreType.DMA((count, 6)),
+            pltpu.SemaphoreType.DMA((count, 6)),
+            pltpu.SemaphoreType.DMA((count,)),
+        ],
+        compiler_params=pltpu.CompilerParams(
+            collective_id=collective_id, has_side_effects=True, vmem_limit_bytes=60 * 2**20
+        ),
+        name="gather_over_devices",
+    )(*shards)
+    return [whole.reshape(-1, whole.shape[-1]) for whole in wholes]
+
+
+def same_column(offset):
+    return lax.rem(lax.axis_index("ctx") + offset, lax.axis_size("ctx"))
+
+
+def greet(devices):
+    meet(devices + [(lax.axis_index("fsdp"), same_column(o)) for o in range(1, 8)])
+
+
+def to_column(src, dst, send, arrive, place):
+    return pltpu.make_async_remote_copy(
+        src_ref=src,
+        dst_ref=dst,
+        send_sem=send,
+        recv_sem=arrive,
+        device_id=(lax.axis_index("fsdp"), place),
+        device_id_type=MESH,
+    )
+
+
+def rows_of(index):
+    return pl.ds(pl.multiple_of(index * TILE, TILE), TILE)
+
+
+def lanes_of(index, start=0):
+    return pl.ds(pl.multiple_of(start + index * 2 * HD, 2 * HD), 2 * HD)
+
+
+def spread_steps(steps, tiles, first, per_tile):
+    before, rest = steps[:first], steps[first:]
+    beside = [rest[t * per_tile : (t + 1) * per_tile] for t in range(tiles)]
+    return before, beside, rest[tiles * per_tile :]
+
+
+def forward_kernel(count, *refs):
+    joined_in, row_ref, col_ref = refs[:3]
+    shards, refs = refs[3 : 3 + count], refs[3 + count :]
+    joined, mixed_ref, log_ref, mixed_in = refs[:4]
+    wholes, refs = refs[4 : 4 + count], refs[4 + count :]
+    score_ref, low_ref, q_send, q_arrive, m_send, m_arrive, send, arrive, keep = refs
+    y, core, z, x = places()
+    me = lax.axis_index("ctx")
+    tiles = 8
+    wide = 2 * HD
+    width = HEADS * HD
+    greet([at_place(y, 1 - core, z, x), at_place(1 - y, core, z, x)])
+
+    def outward(offset, part):
+        place = same_column(offset)
+        src = joined_in.at[:, lanes_of(place, part * width)]
+        dst = joined.at[part, rows_of(me)]
+        if offset == 0:
+            return pltpu.make_async_copy(src, dst, q_arrive.at[0, part])
+        return to_column(src, dst, q_send.at[offset, part], q_arrive.at[offset, part], place)
+
+    for offset in (4, 3, 5, 2, 6, 1, 7, 0):
+        for part in range(3):
+            outward(offset, part).start()
+    steps = gather_schedule(weight_chunks(shards, wholes), send, arrive, keep)
+    before, beside, after = spread_steps(steps, tiles, 3, 2)
+    for step in before:
+        step()
+
+    def receive(source):
+        offset = lax.rem(me + 8 - source, 8)
+        for part in range(3):
+            dst = joined.at[part, rows_of(source)]
+
+            @pl.when(offset == 0)
+            def _():
+                outward(0, part).wait()
+
+            @pl.when(offset != 0)
+            def _():
+                to_column(
+                    dst, dst, q_send.at[offset, part], q_arrive.at[offset, part], source
+                ).wait_recv()
+
+    def back(tile):
+        return to_column(
+            low_ref.at[tile], mixed_in.at[:, lanes_of(me)], m_send.at[tile], m_arrive.at[me], tile
+        )
+
+    def back_here():
+        return pltpu.make_async_copy(
+            low_ref.at[me], mixed_in.at[:, lanes_of(me)], m_arrive.at[me]
+        )
+
+    receive(jnp.int32(0))
+
+    def one_tile(tile, unused):
+        @pl.when(tile < tiles - 1)
+        def _():
+            receive(tile + 1)
+
+        scaled = both_heads(
+            (joined[0, rows_of(tile)].astype(jnp.float32) * HD**-0.5).astype(jnp.bfloat16)
+        )
+        own = row_ref[rows_of(tile), :]
+        own = jnp.concatenate([own, own], axis=0)
+
+        def score(index, best, masked):
+            here = rows_of(index)
+            part = nt(scaled, joined[1, here])
+            if masked:
+                part = jnp.where(col_ref[:, here] <= own, part, MASKED)
+            score_ref[:, here] = part
+            for lane in range(0, TILE, wide):
+                best = jnp.maximum(best, part[:, lane : lane + wide])
+            return best
+
+        best = jnp.full((2 * TILE, wide), MASKED, jnp.float32)
+        best = lax.fori_loop(0, tile, lambda i, b: score(i, b, False), best)
+        stop = jnp.minimum(tile + 2, tiles)
+        best = lax.fori_loop(tile, stop, lambda i, b: score(i, b, True), best)
+        best = jnp.max(best, axis=1, keepdims=True)
+
+        def weigh(index, carry):
+            total, accum = carry
+            here = rows_of(index)
+            weights = jnp.exp(score_ref[:, here] - best)
+            for lane in range(0, TILE, wide):
+                total = total + weights[:, lane : lane + wide]
+            return (total, accum + nn(weights.astype(jnp.bfloat16), joined[2, here]))
+
+        zero = jnp.zeros((2 * TILE, wide), jnp.float32)
+        total, accum = lax.fori_loop(0, stop, weigh, (zero, zero))
+        total = jnp.sum(total, axis=1, keepdims=True)
+        mixed = own_lanes(accum / total)
+        mixed_ref[rows_of(tile), :] = mixed
+        low_ref[tile] = mixed.astype(jnp.bfloat16)
+        log_total = jnp.broadcast_to(best + jnp.log(total), (2 * TILE, wide))
+        log_ref[tile] = jnp.transpose(log_total)[:8]
+
+        @pl.when(tile != me)
+        def _():
+            back(tile).start()
+
+        @pl.when(tile == me)
+        def _():
+            back_here().start()
+
+        for turn in range(tiles):
+            if beside[turn]:
+
+                @pl.when(tile == turn)
+                def _():
+                    for step in beside[turn]:
+                        step()
+
+        return unused
+
+    lax.fori_loop(0, tiles, one_tile, 0)
+    for step in after:
+        step()
+    for offset in range(1, 8):
+        for part in range(3):
+            outward(offset, part).wait_send()
+        place = same_column(offset)
+        back(place).wait_send()
+        lane = mixed_in.at[:, lanes_of(place)]
+        to_column(lane, lane, m_send.at[place], m_arrive.at[place], place).wait_recv()
+    back_here().wait()
+
+
+def attention_forward(joined, blocks, shards, collective_id):
+    tokens = joined.shape[0]
+    rows = tokens * 8
+    wide = 2 * HD
+    low = jnp.bfloat16
+    chunks = sum(shard.size // (SLAB * LANES) for shard in shards)
+    vmem = pl.BlockSpec(memory_space=pltpu.VMEM)
+    any_spec = pl.BlockSpec(memory_space=pl.ANY)
+    results = pl.pallas_call(
+        functools.partial(forward_kernel, len(shards)),
+        out_shape=[
+            jax.ShapeDtypeStruct((3, rows, wide), low),
+            jax.ShapeDtypeStruct((rows, wide), jnp.float32),
+            jax.ShapeDtypeStruct((8, 8, 2 * TILE), jnp.float32),
+            jax.ShapeDtypeStruct((tokens, HEADS * HD), low),
+        ]
+        + [whole_shape(shard) for shard in shards],
+        in_specs=[vmem] * (3 + len(shards)),
+        out_specs=[vmem] * 4 + [any_spec] * len(shards),
+        scratch_shapes=[
+            pltpu.VMEM((2 * TILE, rows), jnp.float32),
+            pltpu.VMEM((8, TILE, wide), low),
+            pltpu.SemaphoreType.DMA((8, 3)),
+            pltpu.SemaphoreType.DMA((8, 3)),
+            pltpu.SemaphoreType.DMA((8,)),
+            pltpu.SemaphoreType.DMA((8,)),
+            pltpu.SemaphoreType.DMA((chunks, 6)),
+            pltpu.SemaphoreType.DMA((chunks, 6)),
+            pltpu.SemaphoreType.DMA((chunks,)),
+        ],
+        compiler_params=pltpu.CompilerParams(
+            collective_id=collective_id, has_side_effects=True, vmem_limit_bytes=60 * 2**20
+        ),
+        name="attention_forward",
+    )(joined, blocks.reshape(rows, 1), blocks.reshape(1, rows), *shards)
+    wholes = [whole.reshape(-1, whole.shape[-1]) for whole in results[4:]]
+    return results[0], results[1], results[2], results[3], wholes
+
+
 TILE = 256
 
 
@@ -488,73 +825,6 @@
     half = pair.shape[0] // 2
     lane = lax.broadcasted_iota(jnp.int32, (half, pair.shape[1]), 1)
     return jnp.where(lane < HD, pair[:half], pair[half:])
-
-
-def attend_kernel(query_ref, key_ref, value_ref, row_ref, col_ref, mixed_ref, log_ref, score_ref):
-    tile = pl.program_id(0)
-    tiles = pl.num_programs(0)
-    wide = 2 * HD
-    scaled = both_heads((query_ref[...].astype(jnp.float32) * HD**-0.5).astype(jnp.bfloat16))
-    own = row_ref[...]
-    own = jnp.concatenate([own, own], axis=0)
-
-    def score(index, best, masked):
-        at = pl.multiple_of(index * TILE, TILE)
-        part = nt(scaled, key_ref[pl.ds(at, TILE), :])
-        if masked:
-            part = jnp.where(col_ref[:, pl.ds(at, TILE)] <= own, part, MASKED)
-        score_ref[:, pl.ds(at, TILE)] = part
-        for lane in range(0, TILE, wide):
-            best = jnp.maximum(best, part[:, lane : lane + wide])
-        return best
-
-    best = jnp.full((2 * TILE, wide), MASKED, jnp.float32)
-    best = lax.fori_loop(0, tile, lambda i, b: score(i, b, False), best)
-    stop = jnp.minimum(tile + 2, tiles)
-    best = lax.fori_loop(tile, stop, lambda i, b: score(i, b, True), best)
-    best = jnp.max(best, axis=1, keepdims=True)
-
-    def weigh(index, carry):
-        total, accum = carry
-        at = pl.multiple_of(index * TILE, TILE)
-        weights = jnp.exp(score_ref[:, pl.ds(at, TILE)] - best)
-        for lane in range(0, TILE, wide):
-            total = total + weights[:, lane : lane + wide]
-        return (total, accum + nn(weights.astype(jnp.bfloat16), value_ref[pl.ds(at, TILE), :]))
-
-    zero = jnp.zeros((2 * TILE, wide), jnp.float32)
-    total, accum = lax.fori_loop(0, stop, weigh, (zero, zero))
-    total = jnp.sum(total, axis=1, keepdims=True)
-    mixed_ref[...] = own_lanes(accum / total)
-    log_total = jnp.broadcast_to(best + jnp.log(total), (2 * TILE, wide))
-    log_ref[0] = jnp.transpose(log_total)[:8]
-
-
-def attention_forward(joined, blocks):
-    rows = joined.shape[0]
-    wide = 2 * HD
-    tiles = rows // TILE
-    return pl.pallas_call(
-        attend_kernel,
-        grid=(tiles,),
-        out_shape=(
-            jax.ShapeDtypeStruct((rows, wide), jnp.float32),
-            jax.ShapeDtypeStruct((tiles, 8, 2 * TILE), jnp.float32),
-        ),
-        in_specs=[
-            pl.BlockSpec((TILE, wide), lambda t: (t, 0)),
-            pl.BlockSpec((rows, wide), lambda t: (0, 1)),
-            pl.BlockSpec((rows, wide), lambda t: (0, 2)),
-            pl.BlockSpec((TILE, 1), lambda t: (t, 0)),
-            pl.BlockSpec((1, rows), lambda t: (0, 0)),
-        ],
-        out_specs=(
-            pl.BlockSpec((TILE, wide), lambda t: (t, 0)),
-            pl.BlockSpec((1, 8, 2 * TILE), lambda t: (t, 0, 0)),
-        ),
-        scratch_shapes=[pltpu.VMEM((2 * TILE, rows), jnp.float32)],
-        name="attention_forward",
-    )(joined, joined, joined, blocks.reshape(rows, 1), blocks.reshape(1, rows))
 
 
 def grads_kernel(
@@ -611,7 +881,7 @@
 
 
 def attention_backward(joined, grad_mixed, mixed, log_total, blocks):
-    rows = joined.shape[0]
+    rows = joined.shape[1]
     wide = 2 * HD
     tiles = rows // TILE
     return pl.pallas_call(
@@ -619,9 +889,9 @@
         grid=(tiles,),
         out_shape=jax.ShapeDtypeStruct((rows, 3 * wide), jnp.bfloat16),
         in_specs=[
-            pl.BlockSpec((TILE, wide), lambda t: (t, 0)),
-            pl.BlockSpec((rows, wide), lambda t: (0, 1)),
-            pl.BlockSpec((rows, wide), lambda t: (0, 2)),
+            pl.BlockSpec((None, TILE, wide), lambda t: (0, t, 0)),
+            pl.BlockSpec((None, rows, wide), lambda t: (1, 0, 0)),
+            pl.BlockSpec((None, rows, wide), lambda t: (2, 0, 0)),
             pl.BlockSpec((TILE, wide), lambda t: (t, 0)),
             pl.BlockSpec((TILE, wide), lambda t: (t, 0)),
             pl.BlockSpec((1, 8, 2 * TILE), lambda t: (t, 0, 0)),
@@ -666,23 +936,29 @@
 def fast_body(
     tokens_in, block_ids, w_query, w_key, w_value, w_out, w_up, w_down, norm_gain, cotangent
 ):
-    axes = ("fsdp", "ctx")
     width = tokens_in.shape[2]
     groups = lax.axis_size("ctx")
-    full_gain = lax.all_gather(norm_gain, axes, axis=1, tiled=True)
-    full_qkv = lax.all_gather(
-        jnp.concatenate([w_query, w_key, w_value], axis=1), axes, axis=0, tiled=True
-    )
-    blocks = lax.all_gather(block_ids, "ctx", axis=1, tiled=True)[0]
-    full_out = lax.all_gather(w_out, axes, axis=0, tiled=True)
-    full_up = lax.all_gather(w_up, axes, axis=0, tiled=True)
-    full_down = lax.all_gather(w_down, axes, axis=0, tiled=True)
-    gains = full_gain.astype(jnp.float32)
+    kinds = norm_gain.shape[0]
+    small = jnp.concatenate(
+        [norm_gain.astype(jnp.float32).reshape(1, -1), block_ids.astype(jnp.float32).reshape(-1, 128)]
+    )
+    small = jnp.pad(small, ((0, 8 - small.shape[0]), (0, 0)))
+    smalls, full_query, full_key, full_value = gather_over_devices(
+        [small, w_query, w_key, w_value], 1
+    )
+    smalls = smalls.reshape(32, 8, 128)
+    gains = smalls[:, 0].reshape(32, kinds, -1).transpose(1, 0, 2).reshape(kinds, width)
+    blocks = lax.dynamic_slice_in_dim(smalls, lax.axis_index("fsdp") * groups, groups, 0)
+    blocks = blocks[:, 1:3].reshape(-1).astype(jnp.int32)
     tokens = tokens_in[0].astype(jnp.float32)
     normed = layer_norm(tokens, gains[0]).astype(jnp.bfloat16)
-    joined = to_heads(project(normed, full_qkv).astype(jnp.bfloat16), groups, 3)
-    mixed, log_total = attention_forward(joined, blocks)
-    mixed_low = to_tokens(mixed.astype(jnp.bfloat16), groups, 1)
+    queries = jnp.concatenate(
+        [project(normed, w).astype(jnp.bfloat16) for w in (full_query, full_key, full_value)], axis=1
+    )
+    joined, mixed, log_total, mixed_low, wholes = attention_forward(
+        queries, blocks, [w_out, w_up, w_down], 2
+    )
+    full_out, full_up, full_down = wholes
     branch = project(mixed_low, full_out)
     hidden = tokens + layer_norm(branch, gains[1])
     inner = layer_norm(hidden, gains[2]).astype(jnp.bfloat16)
@@ -713,7 +989,11 @@
     )
     grad_qkv = to_tokens(grad_joined, groups, 3)
     grad_three = outer_sum(normed, grad_qkv).astype(jnp.bfloat16)
-    grad_normed = back_project(grad_qkv, full_qkv)
+    grad_normed = (
+        back_project(grad_qkv[:, :width], full_query)
+        + back_project(grad_qkv[:, width : 2 * width], full_key)
+        + back_project(grad_qkv[:, 2 * width :], full_value)
+    )
     unused_one, pull_one = jax.vjp(layer_norm, tokens, gains[0])
     grad_norm_in, gain_one = pull_one(grad_normed)
     grad_tokens = (grad_hidden + grad_norm_in).astype(jnp.bfloat16)[None]

time: 607 us -> 539 us (0.89)
  Pallas kernels: 194 us -> 380 us
  waiting for transfers between devices: 140 us -> 21.7 us
  blocking collectives: 132 us -> 27.2 us
  starting transfers between devices: 18.9 us -> 4.55 us
  between operations: 14.6 us -> 1.52 us
    pallas_call x1 -> x2, Pallas kernels: 28.6 us -> 214 us  [the longest x1 163 us: attention_forward(): pl.pallas_call(functools.partial(forward_kernel, len(shards)), out_shape=...]
    all_gather x2 -> x0, blocking collectives: 113 us -> none  [the longest x1 70.7 us: fast_body(): full_gain = lax.all_gather(norm_gain, axes, axis=1, tiled=True)]
    all_gather x4 -> x0, waiting for transfers between devices: 93.9 us -> none  [the longest x1 63 us: fast_body(): full_down = lax.all_gather(w_down, axes, axis=0, tiled=True)]
    all_to_all x2 -> x1, waiting for transfers between devices: 44.1 us -> 21.7 us  [to_tokens(): lax.all_to_all(rows.reshape(groups, tokens, count * wide), 'ctx', 0, 0, t...]
    all_to_all x2 -> x1, starting transfers between devices: 15.1 us -> 4.55 us  [to_tokens(): lax.all_to_all(rows.reshape(groups, tokens, count * wide), 'ctx', 0, 0, t...]
    all_to_all x1, blocking collectives: 18.9 us -> 27.2 us  [to_heads(): whole = lax.all_to_all(split, 'ctx', 0, 0, tiled=True)]
    dot_general x4 -> x6, matrix products: 29.6 us -> 25.2 us  [project(): return jnp.dot(left, right, preferred_element_type=jnp.float32)]
    dot_general x4 -> x6, matrix products: 23.1 us -> 22.5 us  [back_project(): lax.dot_general(grad, weight, (((1,), (1,)), ((), ())), preferred_element...]
  transfers between devices with their start and end apart: 7 -> 1, of which waited for: 4 -> 1; matrix products, arithmetic and copies ran while one was open for 8% -> 3% of each run, Pallas kernels for 5% -> 0%
where the time goes in v3:
time: 539 us; the launch traced here: 535 us
  Pallas kernels  380 us (71%)
  matrix products  67.2 us (12%)
  blocking collectives  27.2 us (5%)
  waiting for transfers between devices  21.7 us (4%)
  local copies, waits for them, and re-layouts  18.3 us (3%)
  other arithmetic  15 us (3%)
    pallas_call x1, Pallas kernels, attention_forward(): pl.pallas_call(functools.partial(forward_kernel, len(shards)), out_shape=...  163 us
    pallas_call x1, Pallas kernels, sum_over_devices(): pl.pallas_call(functools.partial(sum_kernel, views, len(grads)), out_shap...  130 us
    pallas_call x1, Pallas kernels, gather_over_devices(): pl.pallas_call(functools.partial(gather_kernel, len(shards)), out_shape=s...  50.5 us
    pallas_call x1, Pallas kernels, attention_backward(): pl.pallas_call(grads_kernel, grid=(tiles,), out_shape=jax.ShapeDtypeStruc...  35.5 us
    all_to_all x1, blocking collectives, to_heads(): whole = lax.all_to_all(split, 'ctx', 0, 0, tiled=True)  27.2 us
    dot_general x6, matrix products, project(): return jnp.dot(left, right, preferred_element_type=jnp.float32)  25.2 us
    dot_general x6, matrix products, back_project(): lax.dot_general(grad, weight, (((1,), (1,)), ((), ())), preferred_element...  22.5 us
    all_to_all x1, waiting for transfers between devices, to_tokens(): lax.all_to_all(rows.reshape(groups, tokens, count * wide), 'ctx', 0, 0, t...  21.7 us
  transfers between devices with their start and end apart: 1, of which 1 were waited for; matrix products, arithmetic and copies ran while one was open for 3% of the time, Pallas kernels for 0%

profile of v3, /device:TPU:0, one launch (start us, length us, event | category | flops | bytes accessed | tf_op | source)
XLA Modules:
  0.0 534.9 jit_solution(5499408561806169391)
XLA Ops:
  2.8 50.5 %gather_over_devices.1 = (f32[2,2,4,2,8,128]{5,4,3,2,1,0:T(8,128)}, bf16[2,2,4,2,32,1024]{5,4,3,2,1,0:T(8,128)(2,1)}, bf16[2,2,4,2,32,1024]{5,4,3,2,1,0:T(8,128)(2,1)}, bf16[2,2,4,2,32,1024]{5,4,3,2,1,0:T(8,128)(2,1)}) custom-call(f32[8,128]{1,0:T(8,128)} %select_maximum_fusion.refs_0_, bf16[32,1024]{1,0:T(8,128)(2,1)} %refs_1_.1, bf16[32,1024]{1,0:T(8,128)(2,1)} %refs_2_.1, ...), custom_call_target="tpu_custom_call" | custom-call | tf_op jit(solution)/shard_map/gather_over_devices/pallas_call | solution.py:574
  53.3 1.1 slice_reduce_fusion.4
  54.7 1.2 convert_reduce_fusion
  55.9 1.5 fusion.16
  57.4 2.5 convolution_convert_fusion.5
  60.0 1.6 convolution_convert_fusion.6
  63.1 1.4 copy.20.refs_1_.row_ref
  64.5 1.3 pad_maximum_fusion.refs_0_
  65.8 163.5 %attention_forward.1 = (bf16[3,2048,128]{2,1,0:T(8,128)(2,1)}, f32[2048,128]{1,0:T(8,128)}, f32[8,8,512]{2,1,0:T(8,128)}, bf16[256,1024]{1,0:T(8,128)(2,1)}, bf1...) custom-call(bf16[256,3072]{1,0:T(8,128)(2,1)} %pad_maximum_fusion.re, ...), custom_call_target="tpu_custom_call" | custom-call | tf_op jit(solution)/shard_map/attention_forward/pallas_call | solution.py:764
  229.3 2.6 fusion.49
  232.8 15.4 %multiply_convert_fusion = (bf16[256,4096]{1,0:T(8,128)(2,1)S(1)}, f32[256,4096]{1,0:T(8,128)}, f32[256,4096]{1,0:T(8,128)}) fusion(bf16[1024,4096]{1,0:T(8,128)(2,1)} %bitcast.151, f32[256,1024]{1,0:T(8,128)S(1)} %get-tuple-element.56, f32[1024]{0:T(1024)S(1)} %mul.305, f32[256]{0:T(256)S(1)} %fusion.33, f32[256]{0:T(256)S(1)} %broadcast_multiply_fusion.1), kind=kOutput, calls=%fused_computation.6 | convolution fusion | flops 2216689664 | bytes 19929088 | tf_op jit(solution)/shard_map/dot_general | solution.py:36
  248.3 2.4 fusion.50
  250.7 1.0 copy-done.4
  252.0 1.8 fusion.23
  253.9 2.5 fusion.44
  256.4 11.0 %add_convert_fusion = bf16[256,4096]{1,0:T(8,128)(2,1)S(1)} fusion(f32[256,4096]{1,0:T(8,128)S(1)} %copy-done.20, f32[256,4096]{1,0:T(8,128)} %get-tuple-element.66, bf16[4096,1024]{1,0:T(8,128)(2,1)} %bitcast.153, f32[256,1024]{1,0:T(8,128)S(1)} %get-tuple-element.52, f32[256]{0:T(256)S(1)} %negate_multiply_fusion.4), kind=kOutput, calls=%fused_computation.5 | convolution fusion | flops 2162688000 | bytes 19923968 | tf_op jit(solution)/shard_map/dot_general | solution.py:46
  267.4 6.7 %multiply_reduce_fusion = (f32[1024]{0:T(1024)S(1)}, f32[256]{0:T(256)S(1)}, f32[256,1024]{1,0:T(8,128)S(1)}) fusion(f32[256,1024]{1,0:T(8,128)S(1)} %get-tuple-element.56, f32[256]{0:T(256)S(1)} %fusion.33, f32[256]{0:T(256)S(1)} %broadcast_multiply_fusion.1, f32[1024]{0:T(1024)S(1)} %mul.305, bf16[256,4096]{1,0:T(8,128)(2,1)S(1)} %add_convert_fusion, ...), kind=kOutput, calls=%fused_computation.56 | convolution fusion | flops 2149317376 | bytes 12594176 | tf_op jit(solution)/shard_map/dot_general | solution.py:46
  277.6 27.2 %all_to_all.10 = bf16[8,256,128]{2,1,0:T(8,128)(2,1)} all-to-all(bf16[8,256,128]{2,1,0:T(8,128)(2,1)S(1)} %bitcast.140), channel_id=1, replica_groups=mesh['fsdp'=4,'ctx'=8] {'ctx'}, dimensions={0} | all-to-all | bytes 1048576 | tf_op jit(solution)/shard_map/all_to_all | solution.py:924
  304.8 35.5 %attention_backward.1 = bf16[2048,384]{1,0:T(8,128)(2,1)} custom-call(bf16[3,2048,128]{2,1,0:T(8,128)(2,1)} %get-tuple-element.30.query_ref.key_ref.value_ref, bf16[3,2048,128]{2,1,0:T(8,128)(2,1)} %get-tuple-element.30.query_ref.key_ref.value_ref, bf16[3,2048,128]{2,1,0:T(8,128)(2,1)} %get-tuple-element.30.query_ref.key_ref.value_ref, ...), custom_call_target="tpu_custom_call" | custom-call | tf_op jit(solution)/shard_map/attention_backward/pallas_call | solution.py:887
  340.3 2.7 copy.23
  343.0 4.5 all-to-all-start.1
  347.9 3.3 convolution_convert_fusion.3
  351.2 5.7 %convolution_convert_fusion = bf16[4096,1024]{1,0:T(8,128)(2,1)} fusion(bf16[256,4096]{1,0:T(8,128)(2,1)S(1)} %copy-done.10, f32[256,1024]{1,0:T(8,128)S(1)} %copy-done.8, f32[256]{0:T(256)S(1)} %negate_multiply_fusion.4), kind=kOutput, calls=%fused_computation | convolution fusion | flops 2152202240 | bytes 11535360 | tf_op jit(solution)/shard_map/dot_general | solution.py:40
  356.9 5.7 %convolution_convert_fusion.1 = bf16[1024,4096]{1,0:T(8,128)(2,1)} fusion(bf16[256,4096]{1,0:T(8,128)(2,1)S(1)} %copy-done.12, f32[256,1024]{1,0:T(8,128)S(1)} %get-tuple-element.56, f32[1024]{0:T(1024)S(1)} %mul.305, f32[256]{0:T(256)S(1)} %fusion.33, f32[256]{0:T(256)S(1)} %broadcast_multiply_fusion.1), kind=kOutput, calls=%fused_computation.1 | convolution fusion | flops 2152726528 | bytes 11540480 | tf_op jit(solution)/shard_map/dot_general | solution.py:40
  362.6 21.7 %all-to-all-done.1 = bf16[8,256,384]{1,2,0:T(8,128)(2,1)} async-done(((bf16[8,256,384]{1,2,0:T(8,128)(2,1)}), bf16[8,256,384]{1,2,0:T(8,128)(2,1)}, u32[]{:S(2)}, u32[]{:S(2)}) %all-to-all-start.1) | async-done | bytes 1572896 | tf_op jit(solution)/shard_map/all_to_all | solution.py:931
  384.2 1.5 copy.24
  385.8 2.4 fusion.29
  388.1 4.7 convolution_convert_fusion.2
  396.9 130.2 %sum_over_devices.1 = (f32[12,32,1024]{2,1,0:T(8,128)}, f32[8,128]{1,0:T(8,128)}) custom-call(bf16[2,2,4,2,32,3072]{5,4,3,2,1,0:T(8,128)(2,1)} %bitcast.123, bf16[2,2,4,2,1,32,1024]{6,5,4,3,2,1,0:T(8,128)(2,1)} %bitcast.128, bf16[2,2,4,2,32,4096]{5,4,3,2,1,0:T(8,128)(2,1)} %bitcast.122, bf16[2,2,4,2,4,32,1024]{6,5,4,3,2,1,0:T(8,128)(2,1)} %bitcast.121, ...), custom_call_target="tpu_custom_call" | custom-call | tf_op jit(solution)/shard_map/sum_over_devices/pallas_call | solution.py:426
  527.1 1.9 slice_bitcast_fusion.1
  528.9 2.1 fusion.48
  531.0 1.3 fusion.25
  (96 shorter events, 15.3 us)
Async XLA Ops:
  0.6 59.3 %copy-start = (bf16[1,256,1024]{2,1,0:T(8,128)(2,1)S(1)}, bf16[1,256,1024]{2,1,0:T(8,128)(2,1)}, u32[]{:S(2)}) copy-start(bf16[1,256,1024]{2,1,0:T(8,128)(2,1)} %param.10) | copy-start | bytes 1572868
  53.2 6.7 %copy-start.15 = (bf16[2,2,4,2,32,1024]{5,4,3,2,1,0:T(8,128)(2,1)S(1)}, bf16[2,2,4,2,32,1024]{5,4,3,2,1,0:T(8,128)(2,1)}, u32[]{:S(2)}) copy-start(bf16[2,2,4,2,32,1024]{5,4,3,2,1,0:T(8,128)(2,1)} %get-tuple-element.24) | copy-start | bytes 6291460
  55.9 5.6 %copy-start.13 = (bf16[2,2,4,2,32,1024]{5,4,3,2,1,0:T(8,128)(2,1)S(1)}, bf16[2,2,4,2,32,1024]{5,4,3,2,1,0:T(8,128)(2,1)}, u32[]{:S(2)}) copy-start(bf16[2,2,4,2,32,1024]{5,4,3,2,1,0:T(8,128)(2,1)} %get-tuple-element.23) | copy-start | bytes 6291460
  61.5 3.0 copy-start.18
  63.1 2.7 copy-start.19
  232.2 16.1 %slice-start = ((s8[8388608]{0:T(1024)(128)(4,1)}), s8[4194304]{0:T(1024)(128)(4,1)S(1)}, s32[]{:S(2)}) async-start(s8[8388608]{0:T(1024)(128)(4,1)} %bitcast.154), calls=%async_computation.2 | async-start | bytes 8388608
  232.8 15.4 %slice-start.1 = ((s8[8388608]{0:T(1024)(128)(4,1)}), s8[4194304]{0:T(1024)(128)(4,1)S(1)}, s32[]{:S(2)}) async-start(s8[8388608]{0:T(1024)(128)(4,1)} %bitcast.154), calls=%async_computation.3 | async-start | bytes 8388608
  248.2 2.5 copy-start.9
  248.2 3.8 copy-start.3
  250.7 1.0 copy-start.4
  252.0 4.3 copy-start.20
  256.3 11.0 %copy-start.7 = (f32[256,1024]{1,0:T(8,128)}, f32[256,1024]{1,0:T(8,128)S(1)}, u32[]{:S(2)}) copy-start(f32[256,1024]{1,0:T(8,128)S(1)} %get-tuple-element.52) | copy-start | bytes 3145732
  267.3 6.7 %copy-start.11 = (bf16[256,4096]{1,0:T(8,128)(2,1)}, bf16[256,4096]{1,0:T(8,128)(2,1)S(1)}, u32[]{:S(2)}) copy-start(bf16[256,4096]{1,0:T(8,128)(2,1)S(1)} %add_convert_fusion) | copy-start | bytes 6291460
  274.1 2.6 copy-start.17
  274.5 1.2 copy-start.1
  275.7 1.0 copy-start.5
  340.3 7.5 %copy-start.6 = (f32[256,1024]{1,0:T(8,128)S(1)}, f32[256,1024]{1,0:T(8,128)}, u32[]{:S(2)}) copy-start(f32[256,1024]{1,0:T(8,128)} %copy-done.5) | copy-start | bytes 3145732
  343.0 41.2 %all-to-all-start.1 = ((bf16[8,256,384]{1,2,0:T(8,128)(2,1)}), bf16[8,256,384]{1,2,0:T(8,128)(2,1)}, u32[]{:S(2)}, u32[]{:S(2)}) async-start(bf16[8,256,384]{1,2,0:T(8,128)(2,1)} %copy.23), calls=%async_computation.1 | async-start | bytes 3145728 | tf_op jit(solution)/shard_map/all_to_all | solution.py:931
  347.8 3.3 copy-start.8
  347.9 3.3 copy-start.10
  351.2 5.7 %copy-start.12 = (bf16[256,4096]{1,0:T(8,128)(2,1)S(1)}, bf16[256,4096]{1,0:T(8,128)(2,1)}, u32[]{:S(2)}) copy-start(bf16[256,4096]{1,0:T(8,128)(2,1)} %copy-done.11) | copy-start | bytes 6291460
  388.1 4.7 copy-start.16
  392.9 1.6 copy-start.14
  396.9 134.1 %copy-start.2 = (f32[256,1024]{1,0:T(8,128)S(1)}, f32[256,1024]{1,0:T(8,128)}, u32[]{:S(2)}) copy-start(f32[256,1024]{1,0:T(8,128)} %copy-done.1) | copy-start | bytes 3145732

commit v4 on v3

--- a/solution.py
+++ b/solution.py
@@ -455,76 +455,65 @@
     return out, gain_out
 
 
+WINDOW = 4
+ORDERS = ("zxy", "zyx")
+
+
 def gather_schedule(chunks, send, arrive, keep):
-    y, core, z, x = places()
-    partner = at_place(y, 1 - core, z, x)
-    beside = at_place(y, core, z, 1 - x)
-    across = at_place(1 - y, core, z, x)
-    rank = [lax.rem(z + d, 4) for d in (1, 2, 3)]
-    others = [at_place(y, core, r, x) for r in rank]
+    here = dict(zip(("y", "core", "z", "x"), places()))
     count = len(chunks)
-    every = slice(None)
-
-    def remote(src, dst, k, phase, device):
-        return pltpu.make_async_remote_copy(
-            src_ref=src,
-            dst_ref=dst,
-            send_sem=send.at[k, phase],
-            recv_sem=arrive.at[k, phase],
-            device_id=device,
-            device_id_type=MESH,
-        )
+    slots = {"x": 0, "y": 1, "core": 2, "z": 3}
+
+    def copies(k, stage):
+        own, whole = chunks[k]
+        order = tuple(ORDERS[k % len(ORDERS)]) + ("core",)
+        axis, done = order[stage], order[:stage]
+        part = whole(*(slice(None) if a in done else here[a] for a in here))
+        made = []
+        for distance in range(1, 4 if axis == "z" else 2):
+            there = dict(here)
+            there[axis] = lax.rem(here[axis] + distance, 4 if axis == "z" else 2)
+            made.append(
+                pltpu.make_async_remote_copy(
+                    src_ref=part if stage else own,
+                    dst_ref=part,
+                    send_sem=send.at[k, slots[axis] + distance - 1],
+                    recv_sem=arrive.at[k, slots[axis] + distance - 1],
+                    device_id=at_place(*there.values()),
+                    device_id_type=MESH,
+                )
+            )
+        return made
 
     def keeping(k):
         own, whole = chunks[k]
-        return pltpu.make_async_copy(own, whole(y, core, z, x), keep.at[k])
-
-    def along_z(k):
-        own, whole = chunks[k]
-        return [remote(own, whole(y, core, z, x), k, 3 + d, others[d]) for d in range(3)]
-
-    def hop(k, phase):
-        whole = chunks[k][1]
-        if phase == 0:
-            part, device = whole(y, core, every, x), (across if k % 2 else beside)
-        elif k % 2:
-            part, device = whole(every, core, every, x), beside
-        else:
-            part, device = whole(y, core, every, every), across
-        return remote(part, part, k, phase, device)
-
-    def over(k):
-        part = chunks[k][1](every, core, every, every)
-        return remote(part, part, k, 2, partner)
+        return pltpu.make_async_copy(own, whole(*here.values()), keep.at[k])
+
+    def enter(k):
+        keeping(k).start()
+        for copy in copies(k, 0):
+            copy.start()
 
     def begin():
-        for k in range(count):
-            keeping(k).start()
-            for copy in along_z(k):
+        for k in range(min(WINDOW, count)):
+            enter(k)
+
+    def after(k, stage):
+        if stage == 0:
+            if k + WINDOW < count:
+                enter(k + WINDOW)
+            keeping(k).wait()
+        for copy in copies(k, stage):
+            copy.wait()
+        if stage < 3:
+            for copy in copies(k, stage + 1):
                 copy.start()
-
-    def after_z(k):
-        keeping(k).wait()
-        for copy in along_z(k):
-            copy.wait()
-        hop(k, 0).start()
-
-    def after_first(k):
-        hop(k, 0).wait()
-        hop(k, 1).start()
-
-    def after_second(k):
-        hop(k, 1).wait()
-        over(k).start()
-
-    def after_over(k):
-        over(k).wait()
 
     steps = [begin]
     for step in range(count + 3):
-        for lag, run in enumerate((after_z, after_first, after_second, after_over)):
-            if 0 <= step - lag < count:
-                steps.append(functools.partial(run, step - lag))
+        for stage in range(4):
+            if 0 <= step - stage < count:
+                steps.append(functools.partial(after, step - stage, stage))
     return steps
 
 
@@ -589,6 +578,9 @@
     return [whole.reshape(-1, whole.shape[-1]) for whole in wholes]
 
 
+FIRST = 3
+
+
 def same_column(offset):
     return lax.rem(lax.axis_index("ctx") + offset, lax.axis_size("ctx"))
 
@@ -647,7 +639,7 @@
         for part in range(3):
             outward(offset, part).start()
     steps = gather_schedule(weight_chunks(shards, wholes), send, arrive, keep)
-    before, beside, after = spread_steps(steps, tiles, 3, 2)
+    before, beside, after = spread_steps(steps, tiles, FIRST, 2)
     for step in before:
         step()
 
@@ -779,9 +771,9 @@
             pltpu.SemaphoreType.DMA((8, 3)),
             pltpu.SemaphoreType.DMA((8,)),
             pltpu.SemaphoreType.DMA((8,)),
-            pltpu.SemaphoreType.DMA((chunks, 6)),
-            pltpu.SemaphoreType.DMA((chunks, 6)),
-            pltpu.SemaphoreType.DMA((chunks,)),
+            pltpu.SemaphoreType.DMA((max(chunks, 1), 6)),
+            pltpu.SemaphoreType.DMA((max(chunks, 1), 6)),
+            pltpu.SemaphoreType.DMA((max(chunks, 1),)),
         ],
         compiler_params=pltpu.CompilerParams(
             collective_id=collective_id, has_side_effects=True, vmem_limit_bytes=60 * 2**20
@@ -792,6 +784,257 @@
     return results[0], results[1], results[2], results[3], wholes
 
 
+def backward_kernel(
+    grad_in, joined, mixed_ref, log_ref, row_ref, col_ref, out_ref,
+    grad_ref, key_sum, value_sum, low_ref, g_send, g_arrive, o_send, o_arrive,
+):
+    me = lax.axis_index("ctx")
+    tiles = 8
+    wide = 2 * HD
+    width = HEADS * HD
+    greet([])
+
+    def outward(offset):
+        place = same_column(offset)
+        src, dst = grad_in.at[:, lanes_of(place)], grad_ref.at[rows_of(me)]
+        if offset == 0:
+            return pltpu.make_async_copy(src, dst, g_arrive.at[0])
+        return to_column(src, dst, g_send.at[offset], g_arrive.at[offset], place)
+
+    for offset in range(8):
+        outward(offset).start()
+    key_sum[...] = jnp.zeros_like(key_sum)
+    value_sum[...] = jnp.zeros_like(value_sum)
+
+    def receive(source):
+        offset = lax.rem(me + 8 - source, 8)
+
+        @pl.when(offset == 0)
+        def _():
+            outward(0).wait()
+
+        @pl.when(offset != 0)
+        def _():
+            dst = grad_ref.at[rows_of(source)]
+            to_column(dst, dst, g_send.at[offset], g_arrive.at[offset], source).wait_recv()
+
+    def back(tile, part):
+        return to_column(
+            low_ref.at[part, tile],
+            out_ref.at[:, lanes_of(me, part * width)],
+            o_send.at[part, tile],
+            o_arrive.at[part, me],
+            tile,
+        )
+
+    def back_here(part):
+        return pltpu.make_async_copy(
+            low_ref.at[part, me], out_ref.at[:, lanes_of(me, part * width)], o_arrive.at[part, me]
+        )
+
+    def deliver(tile, parts):
+        @pl.when(tile != me)
+        def _():
+            for part in parts:
+                back(tile, part).start()
+
+        @pl.when(tile == me)
+        def _():
+            for part in parts:
+                back_here(part).start()
+
+    def finish_keys(tile):
+        low_ref[1, tile] = key_sum[rows_of(tile), :].astype(jnp.bfloat16)
+        low_ref[2, tile] = value_sum[rows_of(tile), :].astype(jnp.bfloat16)
+        deliver(tile, (1, 2))
+
+    def one_tile(turn, unused):
+        tile = tiles - 1 - turn
+        receive(tile)
+        scaled = both_heads(
+            (joined[0, rows_of(tile)].astype(jnp.float32) * HD**-0.5).astype(jnp.bfloat16)
+        )
+        grads = both_heads(grad_ref[rows_of(tile), :])
+        products = grad_ref[rows_of(tile), :].astype(jnp.float32) * mixed_ref[rows_of(tile), :]
+        products = jnp.transpose(products)
+        delta = jnp.concatenate(
+            [
+                jnp.sum(products[:HD], axis=0, keepdims=True),
+                jnp.sum(products[HD:], axis=0, keepdims=True),
+            ],
+            axis=1,
+        )
+        log_total = log_ref[tile, :1]
+        own = col_ref[:, rows_of(tile)]
+        own = jnp.concatenate([own, own], axis=1)
+
+        def step(index, accum, masked):
+            here = rows_of(index)
+            keys = joined[1, here]
+            scores = nt(keys, scaled)
+            if masked:
+                scores = jnp.where(row_ref[here, :] <= own, scores, MASKED)
+            probs = jnp.exp(scores - log_total)
+            value_sum[here, :] += nn(probs.astype(jnp.bfloat16), grads)
+            grad_scores = (probs * (nt(joined[2, here], grads) - delta)).astype(jnp.bfloat16)
+            key_sum[here, :] += nn(grad_scores, scaled)
+            return accum + tn(grad_scores, keys)
+
+        accum = jnp.zeros((2 * TILE, wide), jnp.float32)
+        accum = lax.fori_loop(0, tile, lambda i, a: step(i, a, False), accum)
+        stop = jnp.minimum(tile + 2, tiles)
+        accum = lax.fori_loop(tile, stop, lambda i, a: step(i, a, True), accum)
+        low_ref[0, tile] = (own_lanes(accum) * HD**-0.5).astype(jnp.bfloat16)
+        deliver(tile, (0,))
+
+        @pl.when(tile < tiles - 1)
+        def _():
+            finish_keys(tile + 1)
+
+        return unused
+
+    lax.fori_loop(0, tiles, one_tile, 0)
+    finish_keys(jnp.int32(0))
+    for offset in range(1, 8):
+        outward(offset).wait_send()
+        place = same_column(offset)
+        for part in range(3):
+            back(place, part).wait_send()
+            lane = out_ref.at[:, lanes_of(place, part * width)]
+            to_column(
+                lane, lane, o_send.at[part, place], o_arrive.at[part, place], place
+            ).wait_recv()
+    for part in range(3):
+        back_here(part).wait()
+
+
+def attention_backward(grad_mixed, joined, mixed, log_total, blocks, collective_id):
+    tokens, width = grad_mixed.shape
+    rows = joined.shape[1]
+    wide = 2 * HD
+    low = jnp.bfloat16
+    vmem = pl.BlockSpec(memory_space=pltpu.VMEM)
+    return pl.pallas_call(
+        backward_kernel,
+        out_shape=jax.ShapeDtypeStruct((tokens, 3 * width), low),
+        in_specs=[vmem] * 6,
+        out_specs=vmem,
+        scratch_shapes=[
+            pltpu.VMEM((rows, wide), low),
+            pltpu.VMEM((rows, wide), jnp.float32),
+            pltpu.VMEM((rows, wide), jnp.float32),
+            pltpu.VMEM((3, 8, TILE, wide), low),
+            pltpu.SemaphoreType.DMA((8,)),
+            pltpu.SemaphoreType.DMA((8,)),
+            pltpu.SemaphoreType.DMA((3, 8)),
+            pltpu.SemaphoreType.DMA((3, 8)),
+        ],
+        compiler_params=pltpu.CompilerParams(
+            collective_id=collective_id, has_side_effects=True, vmem_limit_bytes=60 * 2**20
+        ),
+        name="attention_backward",
+    )(grad_mixed, joined, mixed, log_total, blocks.reshape(rows, 1), blocks.reshape(1, rows))
+
+
+FF_BLOCK = 512
+
+
+def feed_kernel(
+    inner_ref, hidden_ref, upstream_ref, gain_ref, up_ref, down_ref,
+    out_ref, grad_inner_ref, gain_grad_ref, grad_up_ref, grad_down_ref,
+    turned_ref, slope_ref, active_ref, lowered_ref, grad_ref,
+):
+    step = pl.program_id(0)
+    blocks = slope_ref.shape[0]
+
+    @pl.when(step == 0)
+    def _():
+        lowered_ref[...] = jnp.zeros_like(lowered_ref)
+        grad_inner_ref[...] = jnp.zeros_like(grad_inner_ref)
+        turned_ref[...] = jnp.transpose(inner_ref[...])
+
+    @pl.when(step < blocks)
+    def _():
+        lifted = nn(inner_ref[...], up_ref[...])
+        share = 0.5 + 0.5 * lax.erf(lifted * 0.5**0.5)
+        slope_ref[step] = share + lifted * jnp.exp(lifted * lifted * -0.5) * (2 * math.pi) ** -0.5
+        active = (lifted * share).astype(jnp.bfloat16)
+        active_ref[step] = active
+        lowered_ref[...] += nn(active, down_ref[...])
+
+    @pl.when(step == blocks - 1)
+    def _():
+        lowered = lowered_ref[...]
+        centre = lowered - jnp.mean(lowered, axis=-1, keepdims=True)
+        inverse = lax.rsqrt(jnp.mean(centre * centre, axis=-1, keepdims=True) + EPS)
+        unit = centre * inverse
+        gain = gain_ref[...]
+        out_ref[...] = (hidden_ref[...] + unit * gain).astype(jnp.bfloat16)
+        upstream = upstream_ref[...].astype(jnp.float32)
+        gain_grad_ref[...] = jnp.sum(upstream * unit, axis=0, keepdims=True)
+        scaled = upstream * gain
+        mean = jnp.mean(scaled, axis=-1, keepdims=True)
+        along = jnp.mean(scaled * unit, axis=-1, keepdims=True)
+        grad_ref[...] = ((scaled - mean - unit * along) * inverse).astype(jnp.bfloat16)
+
+    @pl.when(step >= blocks)
+    def _():
+        block = step - blocks
+        grad = grad_ref[...]
+        grad_lifted = (nt(grad, down_ref[...]) * slope_ref[block]).astype(jnp.bfloat16)
+        grad_up_ref[...] = nn(turned_ref[...], grad_lifted).astype(jnp.bfloat16)
+        grad_down_ref[...] = tn(active_ref[block], grad).astype(jnp.bfloat16)
+        grad_inner_ref[...] += nt(grad_lifted, up_ref[...])
+
+
+def feed_forward(inner, hidden, upstream, gain, full_up, full_down):
+    tokens, width = inner.shape
+    blocks = full_up.shape[1] // FF_BLOCK
+    low = jnp.bfloat16
+    whole = pl.BlockSpec((tokens, width), lambda i: (0, 0))
+    row = pl.BlockSpec((1, width), lambda i: (0, 0))
+    at = lambda i: lax.rem(i, blocks)
+    late = lambda i: jnp.maximum(i - blocks, 0)
+    return pl.pallas_call(
+        feed_kernel,
+        grid=(2 * blocks,),
+        out_shape=(
+            jax.ShapeDtypeStruct((tokens, width), low),
+            jax.ShapeDtypeStruct((tokens, width), jnp.float32),
+            jax.ShapeDtypeStruct((1, width), jnp.float32),
+            jax.ShapeDtypeStruct(full_up.shape, low),
+            jax.ShapeDtypeStruct(full_down.shape, low),
+        ),
+        in_specs=[
+            whole,
+            whole,
+            whole,
+            row,
+            pl.BlockSpec((width, FF_BLOCK), lambda i: (0, at(i))),
+            pl.BlockSpec((FF_BLOCK, width), lambda i: (at(i), 0)),
+        ],
+        out_specs=(
+            whole,
+            whole,
+            row,
+            pl.BlockSpec((width, FF_BLOCK), lambda i: (0, late(i))),
+            pl.BlockSpec((FF_BLOCK, width), lambda i: (late(i), 0)),
+        ),
+        scratch_shapes=[
+            pltpu.VMEM((width, tokens), low),
+            pltpu.VMEM((blocks, tokens, FF_BLOCK), jnp.float32),
+            pltpu.VMEM((blocks, tokens, FF_BLOCK), low),
+            pltpu.VMEM((tokens, width), jnp.float32),
+            pltpu.VMEM((tokens, width), low),
+        ],
+        compiler_params=pltpu.CompilerParams(vmem_limit_bytes=60 * 2**20),
+        name="feed_forward",
+    )(inner, hidden, upstream, gain, full_up, full_down)
+
+
+EARLY = 3
+
+
 TILE = 256
 
 
@@ -825,112 +1068,6 @@
     half = pair.shape[0] // 2
     lane = lax.broadcasted_iota(jnp.int32, (half, pair.shape[1]), 1)
     return jnp.where(lane < HD, pair[:half], pair[half:])
-
-
-def grads_kernel(
-    query_ref, key_ref, value_ref, grad_ref, mixed_ref, log_ref, row_ref, col_ref, out_ref, key_sum, value_sum
-):
-    tile = pl.program_id(0)
-    tiles = pl.num_programs(0)
-    wide = 2 * HD
-
-    @pl.when(tile == 0)
-    def _():
-        key_sum[...] = jnp.zeros_like(key_sum)
-        value_sum[...] = jnp.zeros_like(value_sum)
-
-    scaled = both_heads((query_ref[...].astype(jnp.float32) * HD**-0.5).astype(jnp.bfloat16))
-    grads = both_heads(grad_ref[...])
-    products = grad_ref[...].astype(jnp.float32) * mixed_ref[...]
-    products = jnp.transpose(products)
-    delta = jnp.concatenate(
-        [
-            jnp.sum(products[:HD], axis=0, keepdims=True),
-            jnp.sum(products[HD:], axis=0, keepdims=True),
-        ],
-        axis=1,
-    )
-    log_total = log_ref[0, :1]
-    own = col_ref[...]
-    own = jnp.concatenate([own, own], axis=1)
-
-    def step(index, accum, masked):
-        at = pl.multiple_of(index * TILE, TILE)
-        here = pl.ds(at, TILE)
-        keys = key_ref[here, :]
-        scores = nt(keys, scaled)
-        if masked:
-            scores = jnp.where(row_ref[here, :] <= own, scores, MASKED)
-        probs = jnp.exp(scores - log_total)
-        value_sum[here, :] += nn(probs.astype(jnp.bfloat16), grads)
-        grad_scores = (probs * (nt(value_ref[here, :], grads) - delta)).astype(jnp.bfloat16)
-        key_sum[here, :] += nn(grad_scores, scaled)
-        return accum + tn(grad_scores, keys)
-
-    accum = jnp.zeros((2 * TILE, wide), jnp.float32)
-    accum = lax.fori_loop(0, tile, lambda i, a: step(i, a, False), accum)
-    stop = jnp.minimum(tile + 2, tiles)
-    accum = lax.fori_loop(tile, stop, lambda i, a: step(i, a, True), accum)
-    at = pl.multiple_of(tile * TILE, TILE)
-    out_ref[pl.ds(at, TILE), :wide] = (own_lanes(accum) * HD**-0.5).astype(jnp.bfloat16)
-
-    @pl.when(tile == tiles - 1)
-    def _():
-        out_ref[:, wide : 2 * wide] = key_sum[...].astype(jnp.bfloat16)
-        out_ref[:, 2 * wide :] = value_sum[...].astype(jnp.bfloat16)
-
-
-def attention_backward(joined, grad_mixed, mixed, log_total, blocks):
-    rows = joined.shape[1]
-    wide = 2 * HD
-    tiles = rows // TILE
-    return pl.pallas_call(
-        grads_kernel,
-        grid=(tiles,),
-        out_shape=jax.ShapeDtypeStruct((rows, 3 * wide), jnp.bfloat16),
-        in_specs=[
-            pl.BlockSpec((None, TILE, wide), lambda t: (0, t, 0)),
-            pl.BlockSpec((None, rows, wide), lambda t: (1, 0, 0)),
-            pl.BlockSpec((None, rows, wide), lambda t: (2, 0, 0)),
-            pl.BlockSpec((TILE, wide), lambda t: (t, 0)),
-            pl.BlockSpec((TILE, wide), lambda t: (t, 0)),
-            pl.BlockSpec((1, 8, 2 * TILE), lambda t: (t, 0, 0)),
-            pl.BlockSpec((rows, 1), lambda t: (0, 0)),
-            pl.BlockSpec((1, TILE), lambda t: (0, t)),
-        ],
-        out_specs=pl.BlockSpec((rows, 3 * wide), lambda t: (0, 0)),
-        scratch_shapes=[
-            pltpu.VMEM((rows, wide), jnp.float32),
-            pltpu.VMEM((rows, wide), jnp.float32),
-        ],
-        name="attention_backward",
-    )(
-        joined,
-        joined,
-        joined,
-        grad_mixed,
-        mixed,
-        log_total,
-        blocks.reshape(rows, 1),
-        blocks.reshape(1, rows),
-    )
-
-
-def to_heads(rows, groups, count):
-    tokens = rows.shape[0]
-    wide = rows.shape[1] // (groups * count)
-    split = rows.reshape(tokens, count, groups, wide).transpose(2, 0, 1, 3)
-    split = split.reshape(groups, tokens, count * wide)
-    whole = lax.all_to_all(split, "ctx", 0, 0, tiled=True)
-    return whole.reshape(groups * tokens, count * wide)
-
-
-def to_tokens(rows, groups, count):
-    tokens = rows.shape[0] // groups
-    wide = rows.shape[1] // count
-    split = lax.all_to_all(rows.reshape(groups, tokens, count * wide), "ctx", 0, 0, tiled=True)
-    split = split.reshape(groups, tokens, count, wide).transpose(1, 2, 0, 3)
-    return split.reshape(tokens, count * groups * wide)
 
 
 def fast_body(
@@ -943,8 +1080,9 @@
         [norm_gain.astype(jnp.float32).reshape(1, -1), block_ids.astype(jnp.float32).reshape(-1, 128)]
     )
     small = jnp.pad(small, ((0, 8 - small.shape[0]), (0, 0)))
-    smalls, full_query, full_key, full_value = gather_over_devices(
-        [small, w_query, w_key, w_value], 1
+    early, late = [w_out, w_up, w_down][:EARLY], [w_out, w_up, w_down][EARLY:]
+    smalls, full_query, full_key, full_value, *first = gather_over_devices(
+        [small, w_query, w_key, w_value] + early, 1
     )
     smalls = smalls.reshape(32, 8, 128)
     gains = smalls[:, 0].reshape(32, kinds, -1).transpose(1, 0, 2).reshape(kinds, width)
@@ -956,26 +1094,17 @@
         [project(normed, w).astype(jnp.bfloat16) for w in (full_query, full_key, full_value)], axis=1
     )
     joined, mixed, log_total, mixed_low, wholes = attention_forward(
-        queries, blocks, [w_out, w_up, w_down], 2
-    )
-    full_out, full_up, full_down = wholes
+        queries, blocks, late, 2
+    )
+    full_out, full_up, full_down = first + wholes
     branch = project(mixed_low, full_out)
     hidden = tokens + layer_norm(branch, gains[1])
     inner = layer_norm(hidden, gains[2]).astype(jnp.bfloat16)
-    lifted = project(inner, full_up)
-    active = gelu_exact(lifted).astype(jnp.bfloat16)
-    lowered = project(active, full_down)
-    layer_out = (hidden + layer_norm(lowered, gains[3])).astype(jnp.bfloat16)[None]
     upstream = cotangent[0].astype(jnp.float32)
-    unused_four, pull_four = jax.vjp(layer_norm, lowered, gains[3])
-    grad_lowered, gain_four = pull_four(upstream)
-    grad_lowered = grad_lowered.astype(jnp.bfloat16)
-    grad_down = outer_sum(active, grad_lowered).astype(jnp.bfloat16)
-    grad_active = back_project(grad_lowered, full_down)
-    unused_gelu, pull_gelu = jax.vjp(gelu_exact, lifted)
-    grad_lifted = pull_gelu(grad_active)[0].astype(jnp.bfloat16)
-    grad_up = outer_sum(inner, grad_lifted).astype(jnp.bfloat16)
-    grad_inner = back_project(grad_lifted, full_up)
+    layer_out, grad_inner, gain_four, grad_up, grad_down = feed_forward(
+        inner, hidden, cotangent[0], gains[3:], full_up, full_down
+    )
+    layer_out, gain_four = layer_out[None], gain_four[0]
     unused_three, pull_three = jax.vjp(layer_norm, hidden, gains[2])
     grad_hidden_branch, gain_three = pull_three(grad_inner)
     grad_hidden = upstream + grad_hidden_branch
@@ -984,10 +1113,7 @@
     grad_branch = grad_branch.astype(jnp.bfloat16)
     grad_out = outer_sum(mixed_low, grad_branch).astype(jnp.bfloat16)
     grad_mixed = back_project(grad_branch, full_out).astype(jnp.bfloat16)
-    grad_joined = attention_backward(
-        joined, to_heads(grad_mixed, groups, 1), mixed, log_total, blocks
-    )
-    grad_qkv = to_tokens(grad_joined, groups, 3)
+    grad_qkv = attention_backward(grad_mixed, joined, mixed, log_total, blocks, 4)
     grad_three = outer_sum(normed, grad_qkv).astype(jnp.bfloat16)
     grad_normed = (
         back_project(grad_qkv[:, :width], full_query)

time: 539 us -> 489 us (0.907)
  Pallas kernels: 380 us -> 436 us
  matrix products: 67.2 us -> 20.6 us
  blocking collectives: 27.2 us -> 0 us
  waiting for transfers between devices: 21.7 us -> 0 us
    pallas_call x1, Pallas kernels: 163 us -> 56 us  [attention_forward(): pl.pallas_call(functools.partial(forward_kernel, len(shards)), out_shape=...]
    pallas_call x1 -> x2, Pallas kernels: 35.5 us -> 120 us  [the longest x1 89.9 us: attention_backward(): pl.pallas_call(backward_kernel, out_shape=jax.ShapeDtypeStruct((tokens, 3...]
    pallas_call x1, Pallas kernels: 50.5 us -> 131 us  [gather_over_devices(): pl.pallas_call(functools.partial(gather_kernel, len(shards)), out_shape=s...]
    all_to_all x1 -> x0, blocking collectives: 27.2 us -> none  [to_heads(): whole = lax.all_to_all(split, 'ctx', 0, 0, tiled=True)]
    all_to_all x1 -> x0, waiting for transfers between devices: 21.7 us -> none  [to_tokens(): lax.all_to_all(rows.reshape(groups, tokens, count * wide), 'ctx', 0, 0, t...]
    dot_general x6 -> x4, matrix products: 25.2 us -> 6.57 us  [project(): return jnp.dot(left, right, preferred_element_type=jnp.float32)]
    dot_general x6 -> x4, matrix products: 22.5 us -> 5.89 us  [back_project(): lax.dot_general(grad, weight, (((1,), (1,)), ((), ())), preferred_element...]
    dot_general x4 -> x2, matrix products: 19.4 us -> 8.16 us  [outer_sum(): lax.dot_general(left, right, (((0,), (0,)), ((), ())), preferred_element_...]
  transfers between devices with their start and end apart: 1 -> 0, of which waited for: 1 -> 0; matrix products, arithmetic and copies ran while one was open for 3% -> 0% of each run, Pallas kernels for 0% -> 0%
where the time goes in v4:
time: 489 us; the launch traced here: 488 us
  Pallas kernels  436 us (89%)
  matrix products  20.6 us (4%)
  local copies, waits for them, and re-layouts  16.5 us (3%)
  other arithmetic  13.9 us (3%)
    pallas_call x1, Pallas kernels, gather_over_devices(): pl.pallas_call(functools.partial(gather_kernel, len(shards)), out_shape=s...  131 us
    pallas_call x1, Pallas kernels, sum_over_devices(): pl.pallas_call(functools.partial(sum_kernel, views, len(grads)), out_shap...  129 us
    pallas_call x1, Pallas kernels, attention_backward(): pl.pallas_call(backward_kernel, out_shape=jax.ShapeDtypeStruct((tokens, 3...  89.9 us
    pallas_call x1, Pallas kernels, attention_forward(): pl.pallas_call(functools.partial(forward_kernel, len(shards)), out_shape=...  56 us
    pallas_call x1, Pallas kernels, feed_forward(): pl.pallas_call(feed_kernel, grid=(2 * blocks,), out_shape=(jax.ShapeDtype...  29.8 us

profile of v4, /device:TPU:0, one launch (start us, length us, event | category | flops | bytes accessed | tf_op | source)
XLA Modules:
  0.0 487.7 jit_solution(9335145600124704236)
XLA Ops:
  1.4 0.8 reshape.275
  2.8 130.8 %gather_over_devices.1 = (f32[2,2,4,2,8,128]{5,4,3,2,1,0:T(8,128)}, bf16[2,2,4,2,32,1024]{5,4,3,2,1,0:T(8,128)(2,1)}, bf16[2,2,4,2,32,1024]{5,4,3,2,1,0:T(8,128)...) custom-call(f32[8,128]{1,0:T(8,128)} %select_maximum_fusion.refs_0_,, ...), custom_call_target="tpu_custom_call" | custom-call | tf_op jit(solution)/shard_map/gather_over_devices/pallas_call | solution.py:563
  133.6 0.9 slice_reduce_fusion
  134.7 1.2 convert_reduce_fusion
  135.9 1.3 fusion.10
  137.3 2.5 convolution_convert_fusion.5
  139.8 0.8 convolution_convert_fusion.4
  140.6 0.8 copy-done.10
  141.4 0.8 convolution_convert_fusion.3
  142.1 1.3 pad_maximum_fusion.refs_0_
  143.4 0.8 dynamic-slice_convert_fusion
  144.2 1.4 copy.22.refs_1_.row_ref
  145.5 56.0 %attention_forward.1 = (bf16[3,2048,128]{2,1,0:T(8,128)(2,1)}, f32[2048,128]{1,0:T(8,128)}, f32[8,8,512]{2,1,0:T(8,128)}, bf16[256,1024]{1,0:T(8,128)(2,1)}) custom-call(bf16[256,3072]{1,0:T(8,128)(2,1)} %pad_maximum_fusion.refs_0_, s32[2048,1]{1,0:T(8,128)} %copy.22.refs_1_.row_ref, s32[1,2048]{1,0:T(1,128)} %bitcast.117), custom_call_target="tpu_custom_call" | custom-call | tf_op jit(solution)/shard_map/attention_forward/pallas_call | solution.py:756
  201.6 2.6 fusion.38
  205.2 1.0 multiply_convert_fusion.inner_ref
  206.9 29.8 %feed_forward.1 = (bf16[256,1024]{1,0:T(8,128)(2,1)}, f32[256,1024]{1,0:T(8,128)}, f32[1,1024]{1,0:T(1,128)}, bf16[1024,4096]{1,0:T(8,128)(2,1)}, bf16[4096,1024]{1,0:T(8,128)(2,1)}) custom-call(bf16[256,1024]{1,0:T(8,128)(2,1)} %multiply_convert_fusion.inner_ref, f32[256,1024]{1,0:T(8,128)} %copy-done, bf16[256,1024]{1,0:T(8,128)(2,1)} %bitcast.103, ...), custom_call_target="tpu_custom_call" | custom-call | tf_op jit(solution)/shard_map/feed_forward/pallas_call | solution.py:998
  236.7 2.0 multiply_reduce_fusion
  241.0 1.0 copy-done.9
  242.0 1.6 convolution_convert_fusion.2.grad_in
  243.6 89.9 %attention_backward.1 = bf16[256,3072]{1,0:T(8,128)(2,1)} custom-call(bf16[256,1024]{1,0:T(8,128)(2,1)} %convolution_convert_fusion.2.grad_in, bf16[3,2048,128]{2,1,0:T(8,128)(2,1)} %get-tuple-element.37.joined, f32[2048,128]{1,0:T(8,128)} %get-tuple-element.38.mixed_ref, f32[8,8,512]{2,1,0:T(8,128)} %get-tuple-element.39.log_ref, ...), custom_call_target="tpu_custom_call" | custom-call | tf_op jit(solution)/shard_map/attention_backward/pallas_call | solution.py:917
  333.6 2.6 fusion.22
  336.4 0.8 convolution_add_fusion.1
  337.2 0.8 copy-done.11
  338.0 0.9 fusion.11
  339.0 1.0 copy-done.4
  342.8 3.5 convolution_convert_fusion.1
  346.3 4.6 convolution_convert_fusion
  351.0 129.1 %sum_over_devices.1 = (f32[12,32,1024]{2,1,0:T(8,128)}, f32[8,128]{1,0:T(8,128)}) custom-call(bf16[2,2,4,2,32,3072]{5,4,3,2,1,0:T(8,128)(2,1)} %bitcast.97, bf16[2,2,4,2,1,32,1024]{6,5,4,3,2,1,0:T(8,128)(2,1)} %bitcast.102, bf16[2,2,4,2,32,4096]{5,4,3,2,1,0:T(8,128)(2,1)} %bitcast.98, bf16[2,2,4,2,4,32,1024]{6,5,4,3,2,1,0:T(8,128)(2,1)} %bitcast.99, ...), custom_call_target="tpu_custom_call" | custom-call | tf_op jit(solution)/shard_map/sum_over_devices/pallas_call | solution.py:426
  480.1 2.2 fusion.36
  482.4 0.8 copy.26
  483.2 1.9 slice_bitcast_fusion.1
  486.5 1.3 fusion.15
  (70 shorter events, 9.9 us)
Async XLA Ops:
  0.6 136.6 %copy-start.2 = (bf16[1,256,1024]{2,1,0:T(8,128)(2,1)S(1)}, bf16[1,256,1024]{2,1,0:T(8,128)(2,1)}, u32[]{:S(2)}) copy-start(bf16[1,256,1024]{2,1,0:T(8,128)(2,1)} %param.10) | copy-start | bytes 1572868
  137.2 2.5 copy-start.12
  139.8 1.6 copy-start.10
  144.2 1.4 copy-start.15
  204.8 2.0 copy-start
  236.7 2.1 copy-start.1
  236.7 2.2 copy-start.8
  238.7 1.1 copy-start.6
  240.4 1.7 copy-start.14
  241.0 1.0 copy-start.9
  333.5 2.7 copy-start.3
  333.5 2.9 copy-start.13
  336.4 1.6 copy-start.11
  338.0 3.2 copy-start.16
  338.9 1.0 copy-start.4
  480.1 6.3 %copy-start.5 = (f32[256,1024]{1,0:T(8,128)S(1)}, f32[256,1024]{1,0:T(8,128)}, u32[]{:S(2)}) copy-start(f32[256,1024]{1,0:T(8,128)} %copy-done.4) | copy-start | bytes 3145732
  480.1 6.3 %copy-start.7 = (bf16[1,256,1024]{2,1,0:T(8,128)(2,1)S(1)}, bf16[1,256,1024]{2,1,0:T(8,128)(2,1)}, u32[]{:S(2)}) copy-start(bf16[1,256,1024]{2,1,0:T(8,128)(2,1)} %param.19) | copy-start | bytes 1572868

commit v5 on v4

--- a/solution.py
+++ b/solution.py
@@ -274,8 +274,9 @@
 
 
 MESH = pl.DeviceIdType.MESH
-SLAB = 32
+SLAB = 16
 LANES = 1024
+SUM_LAG = 2
 
 
 def places():
@@ -401,24 +402,23 @@
     for k in range(count):
         loading(k).start()
         phase_zero(k).start()
-    for step in range(count + 3):
-        for lag, run in enumerate((after_zero, after_one, after_two, after_three)):
-            if 0 <= step - lag < count:
-                run(step - lag)
+    for step in range(count + 3 * SUM_LAG):
+        for stage, run in enumerate((after_zero, after_one, after_two, after_three)):
+            if 0 <= step - SUM_LAG * stage < count:
+                run(step - SUM_LAG * stage)
 
 
 def sum_over_devices(grads, gain, collective_id):
     shaped, views = [], []
     for ref, grad in enumerate(grads):
         rows, columns = grad.shape
-        if columns == LANES:
-            parts = rows // (32 * SLAB)
-            shaped.append(grad.reshape(2, 2, 4, 2, parts, SLAB, LANES))
-            views += [(ref, (part,)) for part in range(parts)]
-        else:
-            parts = columns // LANES
-            shaped.append(grad.reshape(2, 2, 4, 2, SLAB, columns))
-            views += [(ref, (slice(None), pl.ds(part * LANES, LANES))) for part in range(parts)]
+        parts = rows // (32 * SLAB)
+        shaped.append(grad.reshape(2, 2, 4, 2, parts, SLAB, columns))
+        views += [
+            (ref, (part, slice(None), pl.ds(left, LANES)))
+            for left in range(0, columns, LANES)
+            for part in range(parts)
+        ]
     count = len(views)
     low = jnp.bfloat16
     slab = (SLAB, LANES)
@@ -455,7 +455,8 @@
     return out, gain_out
 
 
-WINDOW = 4
+WINDOW = 8
+LAG = 2
 ORDERS = ("zxy", "zyx")
 
 
@@ -510,36 +511,35 @@
                 copy.start()
 
     steps = [begin]
-    for step in range(count + 3):
+    for step in range(count + 3 * LAG):
         for stage in range(4):
-            if 0 <= step - stage < count:
-                steps.append(functools.partial(after, step - stage, stage))
+            if 0 <= step - LAG * stage < count:
+                steps.append(functools.partial(after, step - LAG * stage, stage))
     return steps
 
 
 def weight_chunks(shards, wholes):
     chunks = []
     for own, whole in zip(shards, wholes):
-        columns = own.shape[1]
-        if len(whole.shape) == 7:
-            for part in range(whole.shape[4]):
+        rows, columns = own.shape
+        if len(whole.shape) < 7:
+            chunks.append((own, lambda *p, w=whole: w.at[p]))
+            continue
+        for left in range(0, columns, LANES):
+            for part in range(rows // SLAB):
+                lanes = pl.ds(left, LANES)
                 chunks.append(
-                    (own.at[pl.ds(part * SLAB, SLAB)], lambda *p, w=whole, n=part: w.at[p + (n,)])
+                    (
+                        own.at[pl.ds(part * SLAB, SLAB), lanes],
+                        lambda *p, w=whole, n=(part, slice(None), lanes): w.at[p + n],
+                    )
                 )
-        elif columns > LANES:
-            for part in range(columns // LANES):
-                at = pl.ds(part * LANES, LANES)
-                chunks.append(
-                    (own.at[:, at], lambda *p, w=whole, n=at: w.at[p + (slice(None), n)])
-                )
-        else:
-            chunks.append((own, lambda *p, w=whole: w.at[p]))
     return chunks
 
 
 def whole_shape(shard):
     rows, columns = shard.shape
-    if rows > SLAB and columns == LANES:
+    if rows % SLAB == 0:
         return jax.ShapeDtypeStruct((2, 2, 4, 2, rows // SLAB, SLAB, columns), shard.dtype)
     return jax.ShapeDtypeStruct((2, 2, 4, 2, rows, columns), shard.dtype)
 
@@ -578,15 +578,13 @@
     return [whole.reshape(-1, whole.shape[-1]) for whole in wholes]
 
 
-FIRST = 3
-
-
+SEND_ORDER = (1, 2, 3, 4, 5, 6, 7, 0)
 def same_column(offset):
     return lax.rem(lax.axis_index("ctx") + offset, lax.axis_size("ctx"))
 
 
-def greet(devices):
-    meet(devices + [(lax.axis_index("fsdp"), same_column(o)) for o in range(1, 8)])
+def greet():
+    meet([(lax.axis_index("fsdp"), same_column(o)) for o in range(1, 8)])
 
 
 def to_column(src, dst, send, arrive, place):
@@ -608,24 +606,15 @@
     return pl.ds(pl.multiple_of(start + index * 2 * HD, 2 * HD), 2 * HD)
 
 
-def spread_steps(steps, tiles, first, per_tile):
-    before, rest = steps[:first], steps[first:]
-    beside = [rest[t * per_tile : (t + 1) * per_tile] for t in range(tiles)]
-    return before, beside, rest[tiles * per_tile :]
-
-
-def forward_kernel(count, *refs):
-    joined_in, row_ref, col_ref = refs[:3]
-    shards, refs = refs[3 : 3 + count], refs[3 + count :]
-    joined, mixed_ref, log_ref, mixed_in = refs[:4]
-    wholes, refs = refs[4 : 4 + count], refs[4 + count :]
-    score_ref, low_ref, q_send, q_arrive, m_send, m_arrive, send, arrive, keep = refs
-    y, core, z, x = places()
+def forward_kernel(
+    joined_in, row_ref, col_ref, joined, mixed_ref, log_ref, mixed_in,
+    score_ref, low_ref, q_send, q_arrive, m_send, m_arrive,
+):
     me = lax.axis_index("ctx")
     tiles = 8
     wide = 2 * HD
     width = HEADS * HD
-    greet([at_place(y, 1 - core, z, x), at_place(1 - y, core, z, x)])
+    greet()
 
     def outward(offset, part):
         place = same_column(offset)
@@ -635,17 +624,12 @@
             return pltpu.make_async_copy(src, dst, q_arrive.at[0, part])
         return to_column(src, dst, q_send.at[offset, part], q_arrive.at[offset, part], place)
 
-    for offset in (4, 3, 5, 2, 6, 1, 7, 0):
+    for offset in SEND_ORDER:
         for part in range(3):
             outward(offset, part).start()
-    steps = gather_schedule(weight_chunks(shards, wholes), send, arrive, keep)
-    before, beside, after = spread_steps(steps, tiles, FIRST, 2)
-    for step in before:
-        step()
-
-    def receive(source):
+    def receive(source, parts):
         offset = lax.rem(me + 8 - source, 8)
-        for part in range(3):
+        for part in parts:
             dst = joined.at[part, rows_of(source)]
 
             @pl.when(offset == 0)
@@ -668,12 +652,12 @@
             low_ref.at[me], mixed_in.at[:, lanes_of(me)], m_arrive.at[me]
         )
 
-    receive(jnp.int32(0))
+    receive(jnp.int32(0), (0, 1, 2))
 
     def one_tile(tile, unused):
         @pl.when(tile < tiles - 1)
         def _():
-            receive(tile + 1)
+            receive(tile + 1, (0, 1, 2))
 
         scaled = both_heads(
             (joined[0, rows_of(tile)].astype(jnp.float32) * HD**-0.5).astype(jnp.bfloat16)
@@ -722,19 +706,9 @@
         def _():
             back_here().start()
 
-        for turn in range(tiles):
-            if beside[turn]:
-
-                @pl.when(tile == turn)
-                def _():
-                    for step in beside[turn]:
-                        step()
-
         return unused
 
     lax.fori_loop(0, tiles, one_tile, 0)
-    for step in after:
-        step()
     for offset in range(1, 8):
         for part in range(3):
             outward(offset, part).wait_send()
@@ -745,25 +719,22 @@
     back_here().wait()
 
 
-def attention_forward(joined, blocks, shards, collective_id):
+def attention_forward(joined, blocks, collective_id):
     tokens = joined.shape[0]
     rows = tokens * 8
     wide = 2 * HD
     low = jnp.bfloat16
-    chunks = sum(shard.size // (SLAB * LANES) for shard in shards)
     vmem = pl.BlockSpec(memory_space=pltpu.VMEM)
-    any_spec = pl.BlockSpec(memory_space=pl.ANY)
-    results = pl.pallas_call(
-        functools.partial(forward_kernel, len(shards)),
+    return pl.pallas_call(
+        forward_kernel,
         out_shape=[
             jax.ShapeDtypeStruct((3, rows, wide), low),
             jax.ShapeDtypeStruct((rows, wide), jnp.float32),
             jax.ShapeDtypeStruct((8, 8, 2 * TILE), jnp.float32),
             jax.ShapeDtypeStruct((tokens, HEADS * HD), low),
-        ]
-        + [whole_shape(shard) for shard in shards],
-        in_specs=[vmem] * (3 + len(shards)),
-        out_specs=[vmem] * 4 + [any_spec] * len(shards),
+        ],
+        in_specs=[vmem] * 3,
+        out_specs=[vmem] * 4,
         scratch_shapes=[
             pltpu.VMEM((2 * TILE, rows), jnp.float32),
             pltpu.VMEM((8, TILE, wide), low),
@@ -771,28 +742,23 @@
             pltpu.SemaphoreType.DMA((8, 3)),
             pltpu.SemaphoreType.DMA((8,)),
             pltpu.SemaphoreType.DMA((8,)),
-            pltpu.SemaphoreType.DMA((max(chunks, 1), 6)),
-            pltpu.SemaphoreType.DMA((max(chunks, 1), 6)),
-            pltpu.SemaphoreType.DMA((max(chunks, 1),)),
         ],
         compiler_params=pltpu.CompilerParams(
             collective_id=collective_id, has_side_effects=True, vmem_limit_bytes=60 * 2**20
         ),
         name="attention_forward",
-    )(joined, blocks.reshape(rows, 1), blocks.reshape(1, rows), *shards)
-    wholes = [whole.reshape(-1, whole.shape[-1]) for whole in results[4:]]
-    return results[0], results[1], results[2], results[3], wholes
+    )(joined, blocks.reshape(rows, 1), blocks.reshape(1, rows))
 
 
 def backward_kernel(
     grad_in, joined, mixed_ref, log_ref, row_ref, col_ref, out_ref,
-    grad_ref, key_sum, value_sum, low_ref, g_send, g_arrive, o_send, o_arrive,
+    grad_ref, scaled_ref, pair_ref, delta_ref, query_sum, low_ref, g_send, g_arrive, o_send, o_arrive,
 ):
     me = lax.axis_index("ctx")
     tiles = 8
     wide = 2 * HD
     width = HEADS * HD
-    greet([])
+    greet()
 
     def outward(offset):
         place = same_column(offset)
@@ -803,8 +769,7 @@
 
     for offset in range(8):
         outward(offset).start()
-    key_sum[...] = jnp.zeros_like(key_sum)
-    value_sum[...] = jnp.zeros_like(value_sum)
+    query_sum[...] = jnp.zeros_like(query_sum)
 
     def receive(source):
         offset = lax.rem(me + 8 - source, 8)
@@ -843,58 +808,63 @@
             for part in parts:
                 back_here(part).start()
 
-    def finish_keys(tile):
-        low_ref[1, tile] = key_sum[rows_of(tile), :].astype(jnp.bfloat16)
-        low_ref[2, tile] = value_sum[rows_of(tile), :].astype(jnp.bfloat16)
-        deliver(tile, (1, 2))
-
-    def one_tile(turn, unused):
-        tile = tiles - 1 - turn
+    def prepare(turn, unused):
+        tile = lax.rem(me + turn, tiles)
         receive(tile)
-        scaled = both_heads(
+        scaled_ref[tile] = both_heads(
             (joined[0, rows_of(tile)].astype(jnp.float32) * HD**-0.5).astype(jnp.bfloat16)
         )
-        grads = both_heads(grad_ref[rows_of(tile), :])
+        pair_ref[tile] = both_heads(grad_ref[rows_of(tile), :])
         products = grad_ref[rows_of(tile), :].astype(jnp.float32) * mixed_ref[rows_of(tile), :]
         products = jnp.transpose(products)
-        delta = jnp.concatenate(
+        delta_ref[tile] = jnp.concatenate(
             [
                 jnp.sum(products[:HD], axis=0, keepdims=True),
                 jnp.sum(products[HD:], axis=0, keepdims=True),
             ],
             axis=1,
         )
-        log_total = log_ref[tile, :1]
-        own = col_ref[:, rows_of(tile)]
-        own = jnp.concatenate([own, own], axis=1)
-
-        def step(index, accum, masked):
-            here = rows_of(index)
-            keys = joined[1, here]
+        return unused
+
+    lax.fori_loop(0, tiles, prepare, 0)
+
+    def one_tile(turn, unused):
+        tile = lax.rem(me + turn, tiles)
+        keys, values = joined[1, rows_of(tile)], joined[2, rows_of(tile)]
+        ids = row_ref[rows_of(tile), :]
+
+        def step(index, sums, masked):
+            key_sum, value_sum = sums
+            scaled, pair = scaled_ref[index], pair_ref[index]
             scores = nt(keys, scaled)
             if masked:
-                scores = jnp.where(row_ref[here, :] <= own, scores, MASKED)
-            probs = jnp.exp(scores - log_total)
-            value_sum[here, :] += nn(probs.astype(jnp.bfloat16), grads)
-            grad_scores = (probs * (nt(joined[2, here], grads) - delta)).astype(jnp.bfloat16)
-            key_sum[here, :] += nn(grad_scores, scaled)
-            return accum + tn(grad_scores, keys)
-
-        accum = jnp.zeros((2 * TILE, wide), jnp.float32)
-        accum = lax.fori_loop(0, tile, lambda i, a: step(i, a, False), accum)
-        stop = jnp.minimum(tile + 2, tiles)
-        accum = lax.fori_loop(tile, stop, lambda i, a: step(i, a, True), accum)
-        low_ref[0, tile] = (own_lanes(accum) * HD**-0.5).astype(jnp.bfloat16)
+                own = col_ref[:, rows_of(index)]
+                own = jnp.concatenate([own, own], axis=1)
+                scores = jnp.where(ids <= own, scores, MASKED)
+            probs = jnp.exp(scores - log_ref[index, :1])
+            value_sum = value_sum + nn(probs.astype(jnp.bfloat16), pair)
+            grad_scores = (probs * (nt(values, pair) - delta_ref[index])).astype(jnp.bfloat16)
+            query_sum[index] += tn(grad_scores, keys)
+            return (key_sum + nn(grad_scores, scaled), value_sum)
+
+        zero = jnp.zeros((TILE, wide), jnp.float32)
+        first = jnp.maximum(tile - 1, 0)
+        sums = lax.fori_loop(first, tile + 1, lambda i, s: step(i, s, True), (zero, zero))
+        sums = lax.fori_loop(tile + 1, tiles, lambda i, s: step(i, s, False), sums)
+        low_ref[1, tile] = sums[0].astype(jnp.bfloat16)
+        low_ref[2, tile] = sums[1].astype(jnp.bfloat16)
+        deliver(tile, (1, 2))
+        return unused
+
+    lax.fori_loop(0, tiles, one_tile, 0)
+
+    def finish(turn, unused):
+        tile = lax.rem(me + turn, tiles)
+        low_ref[0, tile] = (own_lanes(query_sum[tile]) * HD**-0.5).astype(jnp.bfloat16)
         deliver(tile, (0,))
-
-        @pl.when(tile < tiles - 1)
-        def _():
-            finish_keys(tile + 1)
-
         return unused
 
-    lax.fori_loop(0, tiles, one_tile, 0)
-    finish_keys(jnp.int32(0))
+    lax.fori_loop(0, tiles, finish, 0)
     for offset in range(1, 8):
         outward(offset).wait_send()
         place = same_column(offset)
@@ -921,8 +891,10 @@
         out_specs=vmem,
         scratch_shapes=[
             pltpu.VMEM((rows, wide), low),
-            pltpu.VMEM((rows, wide), jnp.float32),
-            pltpu.VMEM((rows, wide), jnp.float32),
+            pltpu.VMEM((8, 2 * TILE, wide), low),
+            pltpu.VMEM((8, 2 * TILE, wide), low),
+            pltpu.VMEM((8, 1, 2 * TILE), jnp.float32),
+            pltpu.VMEM((8, 2 * TILE, wide), jnp.float32),
             pltpu.VMEM((3, 8, TILE, wide), low),
             pltpu.SemaphoreType.DMA((8,)),
             pltpu.SemaphoreType.DMA((8,)),
@@ -1032,9 +1004,6 @@
     )(inner, hidden, upstream, gain, full_up, full_down)
 
 
-EARLY = 3
-
-
 TILE = 256
 
 
@@ -1080,9 +1049,8 @@
         [norm_gain.astype(jnp.float32).reshape(1, -1), block_ids.astype(jnp.float32).reshape(-1, 128)]
     )
     small = jnp.pad(small, ((0, 8 - small.shape[0]), (0, 0)))
-    early, late = [w_out, w_up, w_down][:EARLY], [w_out, w_up, w_down][EARLY:]
-    smalls, full_query, full_key, full_value, *first = gather_over_devices(
-        [small, w_query, w_key, w_value] + early, 1
+    smalls, full_query, full_key, full_value, full_out, full_up, full_down = gather_over_devices(
+        [small, w_query, w_key, w_value, w_out, w_up, w_down], 1
     )
     smalls = smalls.reshape(32, 8, 128)
     gains = smalls[:, 0].reshape(32, kinds, -1).transpose(1, 0, 2).reshape(kinds, width)
@@ -1093,10 +1061,7 @@
     queries = jnp.concatenate(
         [project(normed, w).astype(jnp.bfloat16) for w in (full_query, full_key, full_value)], axis=1
     )
-    joined, mixed, log_total, mixed_low, wholes = attention_forward(
-        queries, blocks, late, 2
-    )
-    full_out, full_up, full_down = first + wholes
+    joined, mixed, log_total, mixed_low = attention_forward(queries, blocks, 2)
     branch = project(mixed_low, full_out)
     hidden = tokens + layer_norm(branch, gains[1])
     inner = layer_norm(hidden, gains[2]).astype(jnp.bfloat16)
@@ -1130,12 +1095,9 @@
     return (
         layer_out,
         grad_tokens,
-        sums[0],
-        sums[1],
-        sums[2],
-        sums[3],
-        sums[4:8].transpose(1, 0, 2).reshape(w_up.shape),
-        sums[8:].reshape(w_down.shape),
+        *(sums[2 * k : 2 * k + 2].reshape(w_out.shape) for k in range(4)),
+        sums[8:16].reshape(-1, w_up.shape[0], LANES).transpose(1, 0, 2).reshape(w_up.shape),
+        sums[16:].reshape(w_down.shape),
         gain_sum[0].reshape(norm_gain.shape),
     )
 

time: 489 us -> 466 us (0.953)
  Pallas kernels: 436 us -> 413 us
    pallas_call x1, Pallas kernels: 89.9 us -> 77.1 us  [attention_backward(): pl.pallas_call(backward_kernel, out_shape=jax.ShapeDtypeStruct((tokens, 3...]
    pallas_call x1, Pallas kernels: 131 us -> 126 us  [gather_over_devices(): pl.pallas_call(functools.partial(gather_kernel, len(shards)), out_shape=s...]
where the time goes in v5:
time: 466 us; the launch traced here: 465 us
  Pallas kernels  413 us (89%)
  matrix products  20.6 us (4%)
  local copies, waits for them, and re-layouts  16.5 us (4%)
  other arithmetic  13.9 us (3%)
    pallas_call x1, Pallas kernels, sum_over_devices(): pl.pallas_call(functools.partial(sum_kernel, views, len(grads)), out_shap...  128 us
    pallas_call x1, Pallas kernels, gather_over_devices(): pl.pallas_call(functools.partial(gather_kernel, len(shards)), out_shape=s...  126 us
    pallas_call x1, Pallas kernels, attention_backward(): pl.pallas_call(backward_kernel, out_shape=jax.ShapeDtypeStruct((tokens, 3...  77.1 us
    pallas_call x1, Pallas kernels, attention_forward(): pl.pallas_call(forward_kernel, out_shape=[jax.ShapeDtypeStruct((3, rows,...  53 us
    pallas_call x1, Pallas kernels, feed_forward(): pl.pallas_call(feed_kernel, grid=(2 * blocks,), out_shape=(jax.ShapeDtype...  29.8 us

profile of v5, /device:TPU:0, one launch (start us, length us, event | category | flops | bytes accessed | tf_op | source)
XLA Modules:
  0.0 465.3 jit_solution(4829933029643621130)
XLA Ops:
  1.4 0.8 reshape.295
  2.8 125.7 %gather_over_devices.1 = (f32[2,2,4,2,8,128]{5,4,3,2,1,0:T(8,128)}, bf16[2,2,4,2,2,16,1024]{6,5,4,3,2,1,0:T(8,128)(2,1)}, bf16[2,2,4,2,2,16,1024]{6,5,4,3,2,1,0:...) custom-call(f32[8,128]{1,0:T(8,128)} %select_maximum_fusion.refs_0_,, ...), custom_call_target="tpu_custom_call" | custom-call | tf_op jit(solution)/shard_map/gather_over_devices/pallas_call | solution.py:563
  128.5 0.9 slice_reduce_fusion
  129.6 1.2 convert_reduce_fusion
  130.8 1.3 fusion.10
  132.2 2.5 convolution_convert_fusion.5
  134.7 0.8 convolution_convert_fusion.4
  135.5 0.8 copy-done.10
  136.3 0.8 convolution_convert_fusion.3
  137.0 1.3 pad_maximum_fusion.joined_in
  138.3 0.8 dynamic-slice_convert_fusion
  139.1 1.4 copy.23.row_ref
  140.4 53.0 %attention_forward.1 = (bf16[3,2048,128]{2,1,0:T(8,128)(2,1)}, f32[2048,128]{1,0:T(8,128)}, f32[8,8,512]{2,1,0:T(8,128)}, bf16[256,1024]{1,0:T(8,128)(2,1)}) custom-call(bf16[256,3072]{1,0:T(8,128)(2,1)} %pad_maximum_fusion.joined_in, s32[2048,1]{1,0:T(8,128)} %copy.23.row_ref, s32[1,2048]{1,0:T(1,128)} %bitcast.115), custom_call_target="tpu_custom_call" | custom-call | tf_op jit(solution)/shard_map/attention_forward/pallas_call | solution.py:728
  193.5 2.6 fusion.39
  197.1 1.0 multiply_convert_fusion.inner_ref
  198.8 29.8 %feed_forward.1 = (bf16[256,1024]{1,0:T(8,128)(2,1)}, f32[256,1024]{1,0:T(8,128)}, f32[1,1024]{1,0:T(1,128)}, bf16[1024,4096]{1,0:T(8,128)(2,1)}, bf16[4096,1024]{1,0:T(8,128)(2,1)}) custom-call(bf16[256,1024]{1,0:T(8,128)(2,1)} %multiply_convert_fusion.inner_ref, f32[256,1024]{1,0:T(8,128)} %copy-done, bf16[256,1024]{1,0:T(8,128)(2,1)} %bitcast.100, ...), custom_call_target="tpu_custom_call" | custom-call | tf_op jit(solution)/shard_map/feed_forward/pallas_call | solution.py:970
  228.6 2.0 multiply_reduce_fusion
  232.9 1.0 copy-done.9
  233.9 1.6 convolution_convert_fusion.2.grad_in
  235.5 77.1 %attention_backward.1 = bf16[256,3072]{1,0:T(8,128)(2,1)} custom-call(bf16[256,1024]{1,0:T(8,128)(2,1)} %convolution_convert_fusion.2.grad_in, bf16[3,2048,128]{2,1,0:T(8,128)(2,1)} %get-tuple-element.37.joined, f32[2048,128]{1,0:T(8,128)} %get-tuple-element.38.mixed_ref, f32[8,8,512]{2,1,0:T(8,128)} %get-tuple-element.39.log_ref, s32[2048,1]{1,0:T(8,128)} %copy.23.row_ref, ...), custom_call_target="tpu_custom_call" | custom-call | tf_op jit(solution)/shard_map/attention_backward/pallas_call | solution.py:887
  312.6 2.6 fusion.22
  315.4 0.8 convolution_add_fusion.1
  316.2 0.8 copy-done.11
  317.0 0.9 fusion.11
  318.0 1.0 copy-done.4
  321.8 3.5 convolution_convert_fusion.1
  325.4 4.6 convolution_convert_fusion
  330.0 127.7 %sum_over_devices.1 = (f32[24,16,1024]{2,1,0:T(8,128)}, f32[8,128]{1,0:T(8,128)}) custom-call(bf16[2,2,4,2,2,16,3072]{6,5,4,3,2,1,0:T(8,128)(2,1)} %bitcast.94, bf16[2,2,4,2,2,16,1024]{6,5,4,3,2,1,0:T(8,128)(2,1)} %bitcast.99, bf16[2,2,4,2,2,16,4096]{6,5,4,3,2,1,0:T(8,128)(2,1)} %bitcast.95, bf16[2,2,4,2,8,16,1024]{6,5,4,3,2,1,0:T(8,128)(2,1)} %bitcast.96, ...), custom_call_target="tpu_custom_call" | custom-call | tf_op jit(solution)/shard_map/sum_over_devices/pallas_call | solution.py:426
  457.7 2.2 fusion.36
  459.9 0.8 copy.27
  460.8 1.9 fusion.37
  464.0 1.3 fusion.15
  (70 shorter events, 9.9 us)
Async XLA Ops:
  0.6 131.5 %copy-start.2 = (bf16[1,256,1024]{2,1,0:T(8,128)(2,1)S(1)}, bf16[1,256,1024]{2,1,0:T(8,128)(2,1)}, u32[]{:S(2)}) copy-start(bf16[1,256,1024]{2,1,0:T(8,128)(2,1)} %param.10) | copy-start | bytes 1572868
  132.1 2.5 copy-start.12
  134.7 1.6 copy-start.10
  139.1 1.4 copy-start.15
  196.7 2.0 copy-start
  228.6 2.1 copy-start.1
  228.6 2.2 copy-start.8
  230.6 1.1 copy-start.6
  232.3 1.7 copy-start.14
  232.8 1.0 copy-start.9
  312.5 2.7 copy-start.3
  312.6 2.9 copy-start.13
  315.4 1.6 copy-start.11
  317.0 3.2 copy-start.16
  317.9 1.0 copy-start.4
  457.7 6.3 %copy-start.5 = (f32[256,1024]{1,0:T(8,128)S(1)}, f32[256,1024]{1,0:T(8,128)}, u32[]{:S(2)}) copy-start(f32[256,1024]{1,0:T(8,128)} %copy-done.4) | copy-start | bytes 3145732
  457.7 6.3 %copy-start.7 = (bf16[1,256,1024]{2,1,0:T(8,128)(2,1)S(1)}, bf16[1,256,1024]{2,1,0:T(8,128)(2,1)}, u32[]{:S(2)}) copy-start(bf16[1,256,1024]{2,1,0:T(8,128)(2,1)} %param.19) | copy-start | bytes 1572868
